TPU v7x, 256 devices: a whole 4x4x8 slice. The times are simulated.
256 devices in a mesh: grp: 16 (over x, y), seq: 16 (over z, core).
Axes of the slice: x: 4, y: 4, z: 8, core: 2. Of those that a mesh axis runs over, the one named last changes fastest.
Arguments:
- events: bfloat16 [65536, 1024], P(('grp', 'seq')), may hold values from -6 to 6
- lengths: int32 [256, 16], P(('grp', 'seq')), may hold values from 1 to 24, as said below
- destinations: int32 [256, 16], P(('grp', 'seq')), may hold values from 0 to 15, as said below
- history: int32 [65536], P(('grp', 'seq')), may hold values from 0 to 8191, as said below
- negatives: int32 [65536, 3], P(('grp', 'seq')), may hold values from 0 to 8191, as said below
- in_weight: bfloat16 [1024, 2048], replicated, may hold values from -0.1875 to 0.1875
- out_weight: bfloat16 [1024, 512], replicated, may hold values from -0.25 to 0.25
- item_table: bfloat16 [8192, 1024], P('seq'), may hold values from -0.1875 to 0.1875
Outputs:
- layer_out: bfloat16 [65536, 1024], P(('grp', 'seq'))
- in_grad: float32 [1024, 2048], P('seq')
- out_grad: float32 [1024, 512], P('seq')
- table_grad: float32 [8192, 1024], P('seq')
Inputs may be any that keep to these rules, and one draw needn't show every extreme that they name: Each loader device holds 16 users whose lengths sum to 256; the longest history is 24. `destinations`: the 16 users of a loader device go to the 16 different devices of its group, one to each, and every device of a group receives users with 256 rows in all. `history`: item i lies in row i % 512 of owner i // 512. The 4 candidates of an event lie on 4 different owners, and after the relayout every device holds exactly 64 candidates of each owner. `negatives`: numbered as history; see there.
All inputs are finite; a program needn't handle non-finite values.
Results may differ from a plain program's by a relative error of at most 0.02.
Values may be sent and summed in bfloat16 or wider, within the bound.
A program may use at most 128 MiB of HBM per device.

v0:
```python
import jax
import jax.numpy as jnp
from jax import lax
from jax.sharding import PartitionSpec as P

D = 1024
HEADS = 4
HEAD_DIM = 128
NCAND = 4
VOCAB_DEV = 512


epsilon = 1e-05
softmax_warmth = 0.05


def center_scale(values):
    average = jnp.mean(values, -1, keepdims=True)
    centered = values - average
    inverse = lax.rsqrt(jnp.mean(centered * centered, -1, keepdims=True) + epsilon)
    return (centered * inverse, inverse)


def silu_slope(values):
    sigmoid = jax.nn.sigmoid(values)
    return sigmoid * (1.0 + values * (1.0 - sigmoid))


def batch_stacked(pattern, first_operand, second_operand):
    return jnp.einsum(pattern, first_operand, second_operand, preferred_element_type=jnp.float32)


def layer_forward(tokens, attend_mask, in_weight, out_weight, batch_count):
    hidden_width = out_weight.shape[1]
    scoring_scale = HEAD_DIM ** (-0.5)
    features = tokens.astype(jnp.float32)
    normed_in = center_scale(features)[0].astype(jnp.bfloat16)
    preact = jnp.dot(normed_in, in_weight, preferred_element_type=jnp.float32)
    projected = jax.nn.silu(preact).astype(jnp.bfloat16)
    gate_part = projected[:, :hidden_width]
    value_portion = projected[:, hidden_width : 2 * hidden_width].reshape(
        batch_count, -1, hidden_width
    )
    query_portion = projected[:, 2 * hidden_width : 3 * hidden_width].reshape(
        batch_count, -1, hidden_width
    )
    key_portion = projected[:, 3 * hidden_width :].reshape(batch_count, -1, hidden_width)
    score_list, weight_pieces, output_pieces = ([], [], [])
    for current_head in range(HEADS):
        column_begin = current_head * HEAD_DIM
        column_end = column_begin + HEAD_DIM
        attention_scores = (
            batch_stacked(
                "ptx,pux->ptu",
                query_portion[..., column_begin:column_end],
                key_portion[..., column_begin:column_end],
            )
            * scoring_scale
        )
        attention_weight = (jax.nn.silu(attention_scores) * attend_mask).astype(jnp.bfloat16)
        output_pieces.append(
            batch_stacked(
                "fjz,fzy->fjy", attention_weight, value_portion[..., column_begin:column_end]
            )
        )
        score_list.append(attention_scores)
        weight_pieces.append(attention_weight)
    attended = jnp.concatenate(output_pieces, -1).reshape(-1, hidden_width)
    normed, inverse = center_scale(attended)
    gated_rows = (normed * gate_part.astype(jnp.float32)).astype(jnp.bfloat16)
    result = features + lax.dot_general(
        gated_rows, out_weight, (((1,), (1,)), ((), ())), preferred_element_type=jnp.float32
    )
    saved_state = (
        normed_in,
        preact,
        gate_part,
        value_portion,
        query_portion,
        key_portion,
        score_list,
        weight_pieces,
        normed,
        inverse,
        gated_rows,
    )
    return (result, saved_state)


def layer_backward(upstream, saved_state, attend_mask, out_weight, batch_count):
    (
        normed_in,
        preact,
        gate_part,
        value_portion,
        query_portion,
        key_portion,
        score_list,
        weight_pieces,
        normed,
        inverse,
        gated_rows,
    ) = saved_state
    hidden_width = out_weight.shape[1]
    scoring_scale = HEAD_DIM ** (-0.5)
    upstream_b = upstream.astype(jnp.bfloat16)
    grad_gated = jnp.dot(upstream_b, out_weight, preferred_element_type=jnp.float32)
    grad_gate = grad_gated * normed
    grad_normed = grad_gated * gate_part.astype(jnp.float32)
    grad_attended = inverse * (
        grad_normed
        - jnp.mean(grad_normed, -1, keepdims=True)
        - normed * jnp.mean(grad_normed * normed, -1, keepdims=True)
    )
    grad_attended = grad_attended.astype(jnp.bfloat16).reshape(batch_count, -1, hidden_width)
    value_gradient, query_gradient, key_gradient = ([], [], [])
    for current_head in range(HEADS):
        column_begin = current_head * HEAD_DIM
        column_end = column_begin + HEAD_DIM
        gradient_portion = grad_attended[..., column_begin:column_end]
        weight_gradient = batch_stacked(
            "ptx,pux->ptu", gradient_portion, value_portion[..., column_begin:column_end]
        )
        value_gradient.append(
            batch_stacked("hyo,hyx->hox", weight_pieces[current_head], gradient_portion)
        )
        score_gradient = (
            weight_gradient * attend_mask * silu_slope(score_list[current_head]) * scoring_scale
        ).astype(jnp.bfloat16)
        query_gradient.append(
            batch_stacked("fjz,fzy->fjy", score_gradient, key_portion[..., column_begin:column_end])
        )
        key_gradient.append(
            batch_stacked(
                "hyo,hyx->hox", score_gradient, query_portion[..., column_begin:column_end]
            )
        )
    grad_project = jnp.concatenate(
        [
            grad_gate,
            jnp.concatenate(value_gradient, -1).reshape(-1, hidden_width),
            jnp.concatenate(query_gradient, -1).reshape(-1, hidden_width),
            jnp.concatenate(key_gradient, -1).reshape(-1, hidden_width),
        ],
        -1,
    )
    grad_preact = (grad_project * silu_slope(preact)).astype(jnp.bfloat16)
    return (normed_in, grad_preact, upstream_b, gated_rows)


def item_scores(result, cand_rows):
    length_out = jnp.sqrt(jnp.sum(result * result, -1, keepdims=True) + epsilon)
    single_output = result / length_out
    row_float = cand_rows.astype(jnp.float32)
    row_length = jnp.sqrt(jnp.sum(row_float * row_float, -1, keepdims=True) + epsilon)
    single_row = row_float / row_length
    logit_values = jnp.sum(single_output[:, None, :] * single_row, -1) / softmax_warmth
    exponent = jnp.exp(logit_values)
    softmax_weights = exponent / jnp.sum(exponent, -1, keepdims=True)
    logit_gradient = softmax_weights - (jnp.arange(NCAND) == 0).astype(jnp.float32)[None, :]
    gathered_rows = jnp.sum(logit_gradient[..., None] * single_row, 1) / softmax_warmth
    upstream = (
        gathered_rows - single_output * jnp.sum(single_output * gathered_rows, -1, keepdims=True)
    ) / length_out
    scattered_rows = logit_gradient[..., None] * single_output[:, None, :] / softmax_warmth
    grad_rows = (
        (scattered_rows - single_row * jnp.sum(single_row * scattered_rows, -1, keepdims=True))
        / row_length
    ).astype(jnp.bfloat16)
    return (upstream, grad_rows)


def body(events, lengths, destinations, history, negatives, in_weight, out_weight, item_table):
    owners = lax.axis_size("seq")
    hidden_width = out_weight.shape[1]
    tok_rows = events.shape[0]
    slot_rows = 3 * tok_rows // (2 * owners)
    user_lengths = lengths[0]
    user_dests = destinations[0]
    starts = jnp.cumsum(user_lengths) - user_lengths
    candidates = jnp.concatenate([history[:, None], negatives], 1)
    chosen_user = (user_dests[None, :] == jnp.arange(owners)[:, None]).astype(jnp.int32)
    send_length = jnp.sum(chosen_user * user_lengths[None, :], 1)
    send_start = jnp.sum(chosen_user * starts[None, :], 1)
    slot_index = jnp.arange(slot_rows)
    filled = slot_index[None, :] < send_length[:, None]
    sources = jnp.clip(send_start[:, None] + slot_index[None, :], 0, tok_rows - 1)
    send_tokens = jnp.where(filled[..., None], events[sources], jnp.zeros((), jnp.bfloat16))
    send_items = jnp.where(filled[..., None], candidates[sources], 0)
    got_tokens, got_items, got_length = (
        lax.all_to_all(send_tokens, "seq", split_axis=0, concat_axis=0, tiled=True),
        lax.all_to_all(send_items, "seq", split_axis=0, concat_axis=0, tiled=True),
        lax.all_to_all(send_length[:, None], "seq", split_axis=0, concat_axis=0, tiled=True),
    )
    counts = got_length[:, 0]
    block_ends = jnp.cumsum(counts)
    offsets = block_ends - counts
    positions = jnp.arange(tok_rows)
    anchor = jnp.minimum(
        jnp.sum((block_ends[None, :] <= positions[:, None]).astype(jnp.int32), 1), owners - 1
    )
    placed = anchor * slot_rows + positions - offsets[anchor]
    slot_tokens = got_tokens.reshape(owners * slot_rows, D)
    relayed_items = got_items.reshape(owners * slot_rows, NCAND)[placed]
    attend_mask = (
        (anchor[:, None] == anchor[None, :]) & (positions[None, :] <= positions[:, None])
    ).astype(jnp.float32)[None]
    batch_count = 1
    result_rows, saved_state = layer_forward(
        slot_tokens[placed], attend_mask, in_weight, out_weight, batch_count
    )
    per_owner = tok_rows * NCAND // owners
    flat_items = relayed_items.reshape(-1)
    owner_order = jnp.argsort(flat_items // VOCAB_DEV, stable=True)
    asked_rows = (flat_items % VOCAB_DEV)[owner_order].reshape(owners, per_owner)
    requested = lax.all_to_all(asked_rows, "seq", split_axis=0, concat_axis=0, tiled=True)
    found_rows = item_table[requested]
    fetched, requested = (
        lax.all_to_all(found_rows, "seq", split_axis=0, concat_axis=0, tiled=True),
        requested,
    )
    cand_rows = (
        jnp.zeros((tok_rows * NCAND, D), jnp.bfloat16)
        .at[owner_order]
        .set(fetched.reshape(-1, D))
        .reshape(tok_rows, NCAND, D)
    )
    upstream, grad_rows = item_scores(result_rows, cand_rows)
    outgoing = grad_rows.reshape(-1, D)[owner_order].reshape(owners, per_owner, D)
    returned = lax.all_to_all(outgoing, "seq", split_axis=0, concat_axis=0, tiled=True)
    table_part = jax.ops.segment_sum(
        returned.reshape(-1, D).astype(jnp.float32), requested.reshape(-1), num_segments=VOCAB_DEV
    )
    normed_in, grad_preact, upstream_b, gated_rows = layer_backward(
        upstream, saved_state, attend_mask, out_weight, batch_count
    )
    first_term = lax.dot_general(
        lax.slice_in_dim(normed_in, 0, lax.axis_size("seq") * (D // owners), axis=1),
        grad_preact,
        (((0,), (0,)), ((), ())),
        preferred_element_type=jnp.float32,
    )
    second_term = lax.dot_general(
        lax.slice_in_dim(upstream_b, 0, lax.axis_size("seq") * (D // owners), axis=1),
        gated_rows,
        (((0,), (0,)), ((), ())),
        preferred_element_type=jnp.float32,
    )
    weight_shard = lax.psum_scatter(
        jnp.concatenate([first_term, second_term], 1).astype(jnp.bfloat16),
        "seq",
        scatter_dimension=0,
        tiled=True,
    ).astype(jnp.float32)
    table_grad, weight_shard = (
        lax.psum(table_part.astype(jnp.bfloat16), "grp").astype(jnp.float32),
        lax.psum(weight_shard.astype(jnp.bfloat16), "grp").astype(jnp.float32),
    )
    layer_out = result_rows.astype(jnp.bfloat16)
    return (
        layer_out,
        weight_shard[:, : 4 * hidden_width],
        weight_shard[:, 4 * hidden_width :],
        table_grad,
    )


def solution(mesh):
    return jax.shard_map(
        body,
        mesh=mesh,
        in_specs=(
            P(("grp", "seq"), None),
            P(("grp", "seq"), None),
            P(("grp", "seq"), None),
            P(("grp", "seq")),
            P(("grp", "seq"), None),
            P(),
            P(),
            P("seq", None),
        ),
        out_specs=(P(("grp", "seq"), None), P("seq", None), P("seq", None), P("seq", None)),
        check_vma=False,
    )
```

profile of v0, /device:TPU:32, one launch (start us, length us, event | category | flops | bytes accessed | tf_op | source)
XLA Modules:
  0.0 399.3 jit_solution(15326774801198506185)
XLA Ops:
  10.3 8.6 %all-to-all-start.1 = ((s32[16,1,1]{2,1,0:T(1,128)}), s32[16,1,1]{2,1,0:T(1,128)S(1)}, u32[]{:S(2)}, u32[]{:S(2)}) async-start(s32[16,1,1]{2,1,0:T(1,128)} %copy.95), calls=%async_computation.1 | async-start | bytes 16384 | tf_op jit(solution)/shard_map/all_to_all | solution.py:193
  21.9 2.1 gather_fusion
  25.0 6.2 %all-to-all-start.2 = ((s32[16,24,4]{1,2,0:T(4,128)}), s32[16,24,4]{1,2,0:T(4,128)S(1)}, u32[]{:S(2)}, u32[]{:S(2)}) async-start(s32[16,24,4]{1,2,0:T(4,128)} %broadcast_select_fusion.1), calls=%async_computation.2 | async-start | bytes 65536 | tf_op jit(solution)/shard_map/all_to_all | solution.py:192
  32.6 4.3 %compare_select_fusion.5 = (s32[256,1]{0,1:T(1,128)S(1)}, s32[256,1]{0,1:T(1,128)S(1)}) fusion(s32[]{:T(128)} %bitcast.17, s32[]{:T(128)} %bitcast.18, s32[]{:T(128)} %bitcast.19, s32[]{:T(128)} %bitcast.20, s32[]{:T(128)} %bitcast.21, s32[]{:T(128)} %bitcast.23, s32[]{:T(128)} %bitcast.22, s32[256,1]{0,1:T(1,128)S(1)} %bitcast.229), kind=kLoop, calls=%fused_computation.155 | loop fusion | flops 3840 | bytes 3100 | tf_op jit(solution)/shard_map/gather | solution.py:202
  37.0 5.7 %select_select_fusion = s32[256]{0:T(256)S(1)} fusion(pred[256]{0:T(512)(128)(4,1)S(1)} %get-tuple-element.16, pred[256]{0:T(512)(128)(4,1)S(1)} %get-tuple-element.15, pred[256]{0:T(512)(128)(4,1)S(1)} %get-tuple-element.14, pred[256]{0:T(512)(128)(4,1)S(1)} %get-tuple-element.13, pred[256]{0:T(512)(128)(4,1)S(1)} %get-tuple-element.12, ...), kind=kLoop, calls=%fused_computation.165 | loop fusion | flops 2304 | bytes 4388 | tf_op jit(solution)/shard_map/gather | solution.py:202
  43.8 4.4 %sort.17 = (s32[1024]{0:T(1024)}, s32[1024]{0:T(1024)S(1)}) sort(s32[1024]{0:T(1024)S(1)} %get-tuple-element.33, s32[1024]{0:T(1024)S(1)} %iota.37), dimensions={0}, to_apply=%region_13.14 | sort | flops 10240 | bytes 16384 | tf_op jit(solution)/shard_map/jit(argsort)/sort | solution.py:214
  48.2 4.5 %gather_fusion.4 = s32[1024]{0:T(1024)S(1)} fusion(s32[1024]{0:T(1024)S(1)} %get-tuple-element.32, s32[1024]{0:T(1024)S(1)} %get-tuple-element.30), kind=kCustom, calls=%fused_computation.4 | custom fusion | bytes 12288 | tf_op jit(solution)/shard_map/gather | solution.py:215
  53.4 7.2 %all-to-all-start.3 = ((s32[16,1,64]{2,1,0:T(1,128)}), s32[16,1,64]{2,1,0:T(1,128)S(1)}, u32[]{:S(2)}, u32[]{:S(2)}) async-start(s32[16,1,64]{2,1,0:T(1,128)} %all_to_all.30), calls=%async_computation.3 | async-start | bytes 16384 | tf_op jit(solution)/shard_map/all_to_all | solution.py:216
  61.6 5.1 %all-to-all-done.3 = s32[16,1,64]{2,1,0:T(1,128)S(1)} async-done(((s32[16,1,64]{2,1,0:T(1,128)}), s32[16,1,64]{2,1,0:T(1,128)S(1)}, u32[]{:S(2)}, u32[]{:S(2)}) %all-to-all-start.3) | async-done | bytes 4128 | tf_op jit(solution)/shard_map/all_to_all | solution.py:216
  66.8 4.9 %all-to-all-start = ((bf16[16,24,1024]{2,1,0:T(8,128)(2,1)}), bf16[16,24,1024]{2,1,0:T(8,128)(2,1)S(1)}, u32[]{:S(2)}, u32[]{:S(2)}) async-start(bf16[16,24,1024]{2,1,0:T(8,128)(2,1)} %broadcast_select_fusion), calls=%async_computation | async-start | bytes 1572864 | tf_op jit(solution)/shard_map/all_to_all | solution.py:191
  72.2 5.4 %gather_fusion.5 = bf16[1024,1024]{1,0:T(8,128)(2,1)} fusion(bf16[512,1024]{1,0:T(8,128)(2,1)S(1)} %copy-done, s32[1024]{0:T(1024)S(1)} %broadcast_clamp_fusion), kind=kCustom, calls=%fused_computation.5 | custom fusion | bytes 4198400 | tf_op jit(solution)/shard_map/gather | solution.py:217
  77.6 13.0 %all-to-all-done = bf16[16,24,1024]{2,1,0:T(8,128)(2,1)S(1)} async-done(((bf16[16,24,1024]{2,1,0:T(8,128)(2,1)}), bf16[16,24,1024]{2,1,0:T(8,128)(2,1)S(1)}, u32[]{:S(2)}, u32[]{:S(2)}) %all-to-all-start) | async-done | bytes 786464 | tf_op jit(solution)/shard_map/all_to_all | solution.py:191
  90.6 6.9 %all-to-all-start.4 = ((bf16[16,64,1024]{2,1,0:T(8,128)(2,1)}), bf16[16,64,1024]{2,1,0:T(8,128)(2,1)}, u32[]{:S(2)}, u32[]{:S(2)}) async-start(bf16[16,64,1024]{2,1,0:T(8,128)(2,1)} %bitcast.201), calls=%async_computation.4 | async-start | bytes 4194304 | tf_op jit(solution)/shard_map/all_to_all | solution.py:219
  99.4 4.9 %multiply_convert_fusion = (bf16[256,2048]{1,0:T(8,128)(2,1)S(1)}, f32[256,2048]{1,0:T(8,128)}) fusion(bf16[1024,2048]{1,0:T(8,128)(2,1)} %param.13, bf16[256,1024]{1,0:T(8,128)(2,1)S(1)} %gather_fusion.1, f32[256]{0:T(256)S(1)} %add_rsqrt_fusion.1, f32[256]{0:T(256)S(1)} %broadcast_multiply_fusion.2), kind=kOutput, calls=%fused_computation.22 | convolution fusion | flops 1077411840 | bytes 7866368 | tf_op jit(solution)/shard_map/dot_general | solution.py:38
  110.4 3.1 mul.315
  113.6 5.4 %mul.316 = f32[1024,1024]{1,0:T(8,128)} reshape(f32[256,4,1024]{2,1,0:T(4,128)} %mul.315) | data formatting | bytes 8388608 | tf_op jit(solution)/shard_map/mul | solution.py:157
  118.9 25.8 %all-to-all-done.4 = bf16[16,64,1024]{2,1,0:T(8,128)(2,1)} async-done(((bf16[16,64,1024]{2,1,0:T(8,128)(2,1)}), bf16[16,64,1024]{2,1,0:T(8,128)(2,1)}, u32[]{:S(2)}, u32[]{:S(2)}) %all-to-all-start.4) | async-done | bytes 2097184 | tf_op jit(solution)/shard_map/all_to_all | solution.py:219
  144.7 6.8 %scatter_custom_fusion = bf16[1024,1024]{1,0:T(8,128)(2,1)S(1)} fusion(s32[1024]{0:T(1024)S(1)} %get-tuple-element.31, bf16[1024,1024]{1,0:T(8,128)(2,1)} %bitcast.52, bf16[]{:T(256)} %constant.83.clone.1), kind=kCustom, calls=%fused_computation.67 | custom fusion | bytes 2097664 | tf_op jit(solution)/shard_map/scatter | solution.py:225
  152.0 3.0 reshape.577
  155.8 2.9 multiply_reduce_fusion.2
  163.4 4.6 %multiply_reduce_fusion.1 = f32[256,1024]{1,0:T(8,128)S(1)} fusion(f32[256,4,1024]{2,1,0:T(4,128)} %reshape.577, f32[256,4]{1,0:T(8,128)} %sqrt.22, f32[256,4]{1,0:T(8,128)S(1)} %divide_subtract_fusion), kind=kLoop, calls=%fused_computation.15 | loop fusion | flops 2883584 | bytes 5251072 | tf_op jit(solution)/shard_map/reduce_sum | solution.py:161
  179.0 2.7 pad_maximum_fusion
  182.8 3.3 multiply_reduce_fusion
  186.2 2.6 divide_convert_fusion
  188.8 5.3 %gather_fusion.6 = bf16[1024,1024]{1,0:T(8,128)(2,1)} fusion(bf16[1024,1024]{1,0:T(8,128)(2,1)S(1)} %divide_convert_fusion, s32[1024]{0:T(1024)S(1)} %copy-done.34), kind=kCustom, calls=%fused_computation.6 | custom fusion | bytes 4198400 | tf_op jit(solution)/shard_map/gather | solution.py:229
  194.1 6.8 %all-to-all-start.5 = ((bf16[16,64,1024]{2,1,0:T(8,128)(2,1)}), bf16[16,64,1024]{2,1,0:T(8,128)(2,1)S(1)}, u32[]{:S(2)}, u32[]{:S(2)}) async-start(bf16[16,64,1024]{2,1,0:T(8,128)(2,1)} %bitcast.202), calls=%async_computation.6 | async-start | bytes 4194304 | tf_op jit(solution)/shard_map/all_to_all | solution.py:230
  202.5 55.5 %all-to-all-done.5 = bf16[16,64,1024]{2,1,0:T(8,128)(2,1)S(1)} async-done(((bf16[16,64,1024]{2,1,0:T(8,128)(2,1)}), bf16[16,64,1024]{2,1,0:T(8,128)(2,1)S(1)}, u32[]{:S(2)}, u32[]{:S(2)}) %all-to-all-start.5) | async-done | bytes 2097184 | tf_op jit(solution)/shard_map/all_to_all | solution.py:230
  257.9 10.4 %scatter_custom_fusion.1 = f32[512,1024]{1,0:T(8,128)} fusion(s32[1024]{0:T(1024)S(1)} %reshape.668, bf16[1024,1024]{1,0:T(8,128)(2,1)S(1)} %bitcast.203, f32[]{:T(128)} %constant.88.clone.1), kind=kCustom, calls=%fused_computation.10 | custom fusion | flops 2097152 | bytes 4194308 | tf_op jit(solution)/shard_map/scatter-add | solution.py:231
  268.4 2.8 convert_element_type.134
  271.1 11.9 %reduce-scatter.2.cloned.1.call-done = bf16[64,2560]{1,0:T(8,128)(2,1)} async-done(((bf16[1024,2560]{1,0:T(8,128)(2,1)}), bf16[64,2560]{1,0:T(8,128)(2,1)}) %reduce-scatter.2.cloned.1.call-update) | async-done | bytes 327696 | tf_op jit(solution)/shard_map/reduce_scatter | solution.py:249
  283.1 103.2 %all-reduce.3.cloned.1.call-done = (bf16[64,2560]{1,0:T(8,128)(2,1)}, bf16[512,1024]{1,0:T(8,128)(2,1)}) async-done(((bf16[64,2560]{1,0:T(8,128)(2,1)}, bf16[512,1024]{1,0:T(8,128)(2,1)}), (bf16[64,2560]{1,0:T(8,128)(2,1)}, bf16[512,1024]{1,0:T(8,128)(2,1)})) %all-reduce.3.cloned.1.call-update) | async-done | bytes 1376272 | tf_op jit(solution)/shard_map/psum | solution.py:257
  389.6 2.8 convert_element_type.135
  (212 shorter events, 42.2 us)
Async XLA Ops:
  7.2 65.1 %copy-start = (bf16[512,1024]{1,0:T(8,128)(2,1)S(1)}, bf16[512,1024]{1,0:T(8,128)(2,1)}, u32[]{:S(2)}) copy-start(bf16[512,1024]{1,0:T(8,128)(2,1)} %param.15) | copy-start | bytes 3145732
  7.2 14.7 %copy-start.3 = (bf16[256,1024]{1,0:T(8,128)(2,1)S(1)}, bf16[256,1024]{1,0:T(8,128)(2,1)}, u32[]{:S(2)}) copy-start(bf16[256,1024]{1,0:T(8,128)(2,1)} %param.8) | copy-start | bytes 1572868
  10.3 14.7 %all-to-all-start.1 = ((s32[16,1,1]{2,1,0:T(1,128)}), s32[16,1,1]{2,1,0:T(1,128)S(1)}, u32[]{:S(2)}, u32[]{:S(2)}) async-start(s32[16,1,1]{2,1,0:T(1,128)} %copy.95), calls=%async_computation.1 | async-start | bytes 16384 | tf_op jit(solution)/shard_map/all_to_all | solution.py:193
  25.0 17.7 %all-to-all-start.2 = ((s32[16,24,4]{1,2,0:T(4,128)}), s32[16,24,4]{1,2,0:T(4,128)S(1)}, u32[]{:S(2)}, u32[]{:S(2)}) async-start(s32[16,24,4]{1,2,0:T(4,128)} %broadcast_select_fusion.1), calls=%async_computation.2 | async-start | bytes 65536 | tf_op jit(solution)/shard_map/all_to_all | solution.py:192
  32.6 72.4 %copy-start.40 = (s32[256]{0:T(256)}, s32[256]{0:T(256)S(1)}, u32[]{:S(2)}) copy-start(s32[256]{0:T(256)S(1)} %broadcast_minimum_fusion) | copy-start | bytes 3076
  48.2 4.5 %copy-start.33 = (s32[1024]{0:T(1024)}, s32[1024]{0:T(1024)S(1)}, u32[]{:S(2)}) copy-start(s32[1024]{0:T(1024)S(1)} %get-tuple-element.30) | copy-start | bytes 12292
  53.4 13.4 %all-to-all-start.3 = ((s32[16,1,64]{2,1,0:T(1,128)}), s32[16,1,64]{2,1,0:T(1,128)S(1)}, u32[]{:S(2)}, u32[]{:S(2)}) async-start(s32[16,1,64]{2,1,0:T(1,128)} %all_to_all.30), calls=%async_computation.3 | async-start | bytes 16384 | tf_op jit(solution)/shard_map/all_to_all | solution.py:216
  66.8 23.8 %all-to-all-start = ((bf16[16,24,1024]{2,1,0:T(8,128)(2,1)}), bf16[16,24,1024]{2,1,0:T(8,128)(2,1)S(1)}, u32[]{:S(2)}, u32[]{:S(2)}) async-start(bf16[16,24,1024]{2,1,0:T(8,128)(2,1)} %broadcast_select_fusion), calls=%async_computation | async-start | bytes 1572864 | tf_op jit(solution)/shard_map/all_to_all | solution.py:191
  90.6 54.1 %all-to-all-start.4 = ((bf16[16,64,1024]{2,1,0:T(8,128)(2,1)}), bf16[16,64,1024]{2,1,0:T(8,128)(2,1)}, u32[]{:S(2)}, u32[]{:S(2)}) async-start(bf16[16,64,1024]{2,1,0:T(8,128)(2,1)} %bitcast.201), calls=%async_computation.4 | async-start | bytes 4194304 | tf_op jit(solution)/shard_map/all_to_all | solution.py:219
  97.5 185.5 %reduce-scatter.2.cloned.1.call-start = ((), (), s32[]{:S(2)}) async-start(), calls=%async_computation.7 | async-start | bytes 5570560 | tf_op jit(solution)/shard_map/reduce_scatter | solution.py:249
  98.9 8.7 %copy-start.5 = (bf16[256,1024]{1,0:T(8,128)(2,1)}, bf16[256,1024]{1,0:T(8,128)(2,1)S(1)}, u32[]{:S(2)}) copy-start(bf16[256,1024]{1,0:T(8,128)(2,1)S(1)} %gather_fusion.1) | copy-start | bytes 1572868
  99.1 5.2 %copy-start.42 = (f32[256]{0:T(256)}, f32[256]{0:T(256)S(1)}, u32[]{:S(2)}) copy-start(f32[256]{0:T(256)S(1)} %broadcast_multiply_fusion.2) | copy-start | bytes 3076
  99.4 4.9 %copy-start.47 = (f32[256]{0:T(256)}, f32[256]{0:T(256)S(1)}, u32[]{:S(2)}) copy-start(f32[256]{0:T(256)S(1)} %add_rsqrt_fusion.1) | copy-start | bytes 3076
  104.3 3.3 copy-start.17
  104.4 2.7 copy-start.15
  106.0 3.5 copy-start.19
  106.0 3.5 copy-start.21
  106.0 3.5 copy-start.23
  106.0 3.5 copy-start.25
  106.7 2.8 copy-start.9
  107.0 2.5 copy-start.11
  107.4 2.1 copy-start.13
  107.4 2.1 copy-start.36
  107.6 1.9 copy-start.44
  109.5 4.0 %copy-start.38 = (f32[256]{0:T(256)}, f32[256]{0:T(256)S(1)}, u32[]{:S(2)}) copy-start(f32[256]{0:T(256)S(1)} %add_sqrt_fusion.1) | copy-start | bytes 3076
  151.5 31.2 %copy-start.2 = (bf16[1024,1024]{1,0:T(8,128)(2,1)}, bf16[1024,1024]{1,0:T(8,128)(2,1)S(1)}, u32[]{:S(2)}) copy-start(bf16[1024,1024]{1,0:T(8,128)(2,1)S(1)} %scatter_custom_fusion) | copy-start | bytes 6291460
  175.7 1.8 copy-start.51
  182.8 3.5 copy-start.4
  186.2 2.6 copy-start.34
  194.1 63.8 %all-to-all-start.5 = ((bf16[16,64,1024]{2,1,0:T(8,128)(2,1)}), bf16[16,64,1024]{2,1,0:T(8,128)(2,1)S(1)}, u32[]{:S(2)}, u32[]{:S(2)}) async-start(bf16[16,64,1024]{2,1,0:T(8,128)(2,1)} %bitcast.202), calls=%async_computation.6 | async-start | bytes 4194304 | tf_op jit(solution)/shard_map/all_to_all | solution.py:230
  200.9 185.3 %all-reduce.3.cloned.1.call-start = ((), (), s32[]{:S(2)}) async-start(), calls=%async_computation.8 | async-start | bytes 2752512 | tf_op jit(solution)/shard_map/psum | solution.py:257
  386.2 6.2 %copy-start.1 = (bf16[512,1024]{1,0:T(8,128)(2,1)S(1)}, bf16[512,1024]{1,0:T(8,128)(2,1)}, u32[]{:S(2)}) copy-start(bf16[512,1024]{1,0:T(8,128)(2,1)} %param.15) | copy-start | bytes 3145732
  (28 other events, 33.1 us)
Sparse Core Ops, SparseCore 0:
  181.9 101.0 reduce-scatter.1
  286.4 99.8 all-reduce.2
where the time goes:
time: 401 us; the launch traced here: 399 us
  waiting for transfers between devices  216 us (54%)
  other arithmetic  59.3 us (15%)
  local copies, waits for them, and re-layouts  53.1 us (13%)
  starting transfers between devices  41.1 us (10%)
  matrix products  15.2 us (4%)
  between operations  15.1 us (4%)
    psum x1, waiting for transfers between devices, body(): lax.psum(weight_shard.astype(jnp.bfloat16), 'grp').astype(jnp.float32)  103 us
    all_to_all x1, waiting for transfers between devices, body(): lax.all_to_all(outgoing, 'seq', split_axis=0, concat_axis=0, tiled=True)  55.5 us
    all_to_all x1, waiting for transfers between devices, body(): lax.all_to_all(found_rows, 'seq', split_axis=0, concat_axis=0, tiled=True)  25.8 us
    all_to_all x1, waiting for transfers between devices, body(): lax.all_to_all(send_tokens, 'seq', split_axis=0, concat_axis=0, tiled=True)  13 us
    reduce_scatter x1, waiting for transfers between devices, body(): lax.psum_scatter(jnp.concatenate([first_term, second_term], 1).astype(jnp...  11.9 us
    scatter-add x1, other arithmetic, body(): jax.ops.segment_sum(returned.reshape(-1, D).astype(jnp.float32), requeste...  10.4 us
    gather x3, other arithmetic, body(): placed = anchor * slot_rows + positions - offsets[anchor]  10.1 us
    all_to_all x1, starting transfers between devices, body(): lax.all_to_all(send_length[:, None], 'seq', split_axis=0, concat_axis=0,...  8.59 us
  transfers between devices with their start and end apart: 8, of which 7 were waited for; matrix products, arithmetic and copies ran while one was open for 18% of the time, Pallas kernels for 0%

commit v1 on v0

v1 whole, which is shorter than its diff:
```python
import jax
import jax.numpy as jnp
from jax import lax
from jax.experimental import pallas as pl
from jax.experimental.pallas import tpu as pltpu
from jax.sharding import PartitionSpec as P

F32, BF, I32 = jnp.float32, jnp.bfloat16, jnp.int32
MESH = pl.DeviceIdType.MESH
T, D, HID = 256, 1024, 512
HEADS, HEAD_DIM, NCAND = 4, 128, 4
EPS = 1e-5
TEMP = 0.05
SCALE = HEAD_DIM ** -0.5
VMEM_BYTES = 64_000_000


def rep(n, body):
    def step(i, carry):
        body(i)
        return carry

    lax.fori_loop(0, n, step, 0)


def ds(i, size):
    return pl.ds(pl.multiple_of(i * size, size), size)


def iota(shape, dim):
    return lax.broadcasted_iota(I32, shape, dim)


def mm(a, b):
    return jnp.dot(a, b, preferred_element_type=F32)


def mm_t(a, b):
    return lax.dot_general(a, b, (((1,), (1,)), ((), ())), preferred_element_type=F32)


def sigmoid(v):
    return 1.0 / (1.0 + jnp.exp(-v))


class Where:
    def __init__(self):
        self.g, self.s = lax.axis_index("grp"), lax.axis_index("seq")
        self.px, self.py = self.g // 4, self.g % 4
        self.z, self.c = self.s // 2, self.s % 2

    def at(self, grp=None, seq=None):
        return {"grp": self.g if grp is None else grp, "seq": self.s if seq is None else seq}

    def zoff(self, k):
        return self.at(seq=((self.z + k) % 8) * 2 + self.c)

    def mate(self):
        return self.at(seq=self.z * 2 + 1 - self.c)

    def xoff(self, k):
        return self.at(grp=((self.px + k) % 4) * 4 + self.py)

    def yoff(self, k):
        return self.at(grp=self.px * 4 + (self.py + k) % 4)


class Links:
    def __init__(self, send, recv):
        self.send, self.recv, self.n, self.sent = send, recv, 0, []

    def go(self, src, dst, dev):
        copy = pltpu.make_async_remote_copy(
            src_ref=src, dst_ref=dst, send_sem=self.send.at[self.n], recv_sem=self.recv.at[self.n],
            device_id=dev, device_id_type=MESH)
        self.n += 1
        copy.start()
        self.sent.append(copy)
        return copy

    def drain(self):
        for copy in self.sent:
            copy.wait_send()


def greet(devices):
    barrier = pltpu.get_barrier_semaphore()
    for dev in devices:
        pl.semaphore_signal(barrier, inc=1, device_id=dev, device_id_type=MESH)
    pl.semaphore_wait(barrier, len(devices))


NSEM1 = 128


def train_kernel(len_s, cols_v, rows_v, ev_h, win_h, wout_h, tab_h, lay_o, g_o, h_o,
                 x_v, win, wout, traw, tab, zb, nin, slope, proj, attn, dsl, att, normed, inv, gated, gatedm,
                 res, rlen, yall, ymate, cand, rall, gall, gsend, lbuf, lacc, lsum, lrec, gcol, sfull,
                 wown, wsend, wrec, upb, gg, gatt, gpre, gprem, ninT, ninTm, upT, upTm, st, hsend, hrec, mask_v,
                 lsem, ssem, rsem):
    w = Where()
    net = Links(ssem, rsem)
    z, c, px, py, g = w.z, w.c, w.px, w.py, w.g
    loads = [pltpu.make_async_copy(a, b, lsem.at[i]) for i, (a, b) in enumerate(
        ((tab_h, traw), (ev_h, x_v), (win_h, win), (wout_h, wout)))]
    for copy in loads:
        copy.start()
    greet([w.at(seq=(w.s + k) % 16) for k in range(1, 16)] + [w.xoff(1), w.xoff(3), w.yoff(1), w.yoff(3)])

    cand[pl.ds(0, T)] = cols_v[...]
    rall[0] = rows_v[...]
    cp_cand = net.go(cols_v, cand.at[pl.ds(T, T)], w.mate())
    cp_rows = [net.go(rows_v, rall.at[8 - k], w.zoff(k)) for k in range(1, 8)]

    loads[0].wait()

    def norm_rows(i):
        j = (g + i) % 16
        rows = traw[ds(j, 32)].astype(F32)
        length = lax.rsqrt(jnp.sum(rows * rows, -1, keepdims=True) + EPS)
        tab[0, j // 4, j % 4] = (rows * length).astype(BF)

    norm_rows(0)
    r1 = net.go(tab.at[0, px, py], zb.at[1], w.zoff(1))
    l1 = net.go(tab.at[0, px, py], zb.at[0], w.zoff(-1))
    rep(15, lambda i: norm_rows(i + 1))

    pieces = {6: (6, 0, 1024, "y"), 2: (2, 0, 1024, "x"), 5: (5, 0, 1024, "y"), 3: (3, 0, 1024, "x"),
              "4x": (4, 0, 512, "x"), "4y": (4, 512, 512, "y")}
    flying = {}

    def one(piece, kx, ky, c0, nc):
        return tab.at[piece[0], (px + kx) % 4, (py + ky) % 4, :, pl.ds(c0, nc)]

    def many(piece, k, c0, nc):
        if piece[3] == "x":
            return tab.at[piece[0], :, (py + k) % 4, :, pl.ds(c0, nc)]
        return tab.at[piece[0], (px + k) % 4, :, :, pl.ds(c0, nc)]

    def first_send(name):
        p = pieces[name]
        off = w.xoff if p[3] == "x" else w.yoff
        own = one(p, 0, 0, p[1], p[2])
        flying[name] = [net.go(own, own, off(1)), net.go(own, own, off(-1))]

    def first_forward(name):
        p = pieces[name]
        off = w.xoff if p[3] == "x" else w.yoff
        half = p[2] // 2
        a, b = flying[name]
        at = (lambda k, c0: one(p, k, 0, c0, half)) if p[3] == "x" else (lambda k, c0: one(p, 0, k, c0, half))
        a.wait_recv()
        ref = at(-1, p[1])
        a2 = net.go(ref, ref, off(1))
        b.wait_recv()
        ref = at(1, p[1] + half)
        flying[name] = [a2, net.go(ref, ref, off(-1))]

    def second_send(name):
        p = pieces[name]
        off = w.yoff if p[3] == "x" else w.xoff
        for copy in flying[name]:
            copy.wait_recv()
        own = many(p, 0, p[1], p[2])
        flying[name] = [net.go(own, own, off(1)), net.go(own, own, off(-1))]

    def second_forward(name):
        p = pieces[name]
        off = w.yoff if p[3] == "x" else w.xoff
        half = p[2] // 2
        a, b = flying[name]
        a.wait_recv()
        ref = many(p, -1, p[1], half)
        a2 = net.go(ref, ref, off(1))
        b.wait_recv()
        ref = many(p, 1, p[1] + half, half)
        flying[name] = [a2, net.go(ref, ref, off(-1))]

    direct = []

    def shard_direct(q):
        own = tab.at[0, q]
        direct.append((net.go(own, tab.at[7, q], w.zoff(1)), net.go(own, tab.at[1, q], w.zoff(-1))))

    hop = {}

    def pump1():
        r1.wait_recv()
        hop["r"] = net.go(zb.at[1], tab.at[6, px, py], w.zoff(1))
        l1.wait_recv()
        hop["l"] = net.go(zb.at[0], tab.at[2, px, py], w.zoff(-1))
        shard_direct(0)

    def pump2():
        hop["r"].wait_recv()
        hop["r"] = net.go(tab.at[6, px, py], tab.at[5, px, py], w.zoff(1))
        hop["l"].wait_recv()
        hop["l"] = net.go(tab.at[2, px, py], tab.at[3, px, py], w.zoff(-1))
        first_send(6)
        first_send(2)
        shard_direct(1)

    def pump3():
        hop["r"].wait_recv()
        hop["r"] = net.go(tab.at[5, px, py], tab.at[4, px, py], w.zoff(1))
        hop["l"].wait_recv()
        first_send(5)
        first_send(3)
        first_forward(6)
        first_forward(2)
        shard_direct(2)
        shard_direct(3)

    def pump4():
        hop["r"].wait_recv()
        first_send("4x")
        first_send("4y")
        first_forward(5)
        first_forward(3)
        second_send(6)
        second_send(2)

    def pump5():
        first_forward("4x")
        first_forward("4y")
        second_send(5)
        second_send(3)

    def pump6():
        second_forward(6)
        second_forward(2)
        second_send("4x")
        second_send("4y")

    def pump7():
        second_forward(5)
        second_forward(3)

    def pump8():
        second_forward("4x")
        second_forward("4y")

    ends = []
    for j in range(16):
        ends.append(len_s[0, j] + (ends[-1] if ends else 0))
    tc, tr = iota((T, 128), 0), iota((8, T), 1)
    uid_c, uid_r = jnp.zeros((T, 128), I32), jnp.zeros((8, T), I32)
    for end in ends:
        uid_c = uid_c + (tc >= end).astype(I32)
        uid_r = uid_r + (tr >= end).astype(I32)
    same = (uid_c[:, :1] == uid_r[:1, :]) & (iota((T, T), 1) <= iota((T, T), 0))
    mask_v[...] = same.astype(F32)

    loads[1].wait()

    def norm_in(i):
        v = x_v[ds(i, 32)].astype(F32)
        v = v - jnp.mean(v, -1, keepdims=True)
        nin[ds(i, 32)] = (v * lax.rsqrt(jnp.mean(v * v, -1, keepdims=True) + EPS)).astype(BF)

    rep(8, norm_in)
    pump1()
    loads[2].wait()
    loads[3].wait()

    def project(i):
        pre = mm(nin[...], win[:, ds(i, 256)])
        sg = sigmoid(pre)
        proj[:, ds(i, 256)] = (pre * sg).astype(BF)
        slope[:, ds(i, 256)] = sg * (1.0 + pre * (1.0 - sg))

    rep(4, project)
    pump2()
    rep(4, lambda i: project(i + 4))
    pump3()

    def flip_in(i):
        block = nin[:, ds(i, 128)].astype(F32).T
        ninT[i] = block.astype(BF).reshape(2, 64, T)

    def attend(h):
        col = lambda part: pl.ds(pl.multiple_of(part * HID + h * 128, 128), 128)
        scores = mm_t(proj[:, col(2)], proj[:, col(3)]) * SCALE
        sg = sigmoid(scores)
        mask = mask_v[...]
        weight = (scores * sg * mask).astype(BF)
        attn[h] = weight
        dsl[h] = sg * (1.0 + scores * (1.0 - sg)) * SCALE * mask
        att[:, ds(h, 128)] = mm(weight, proj[:, col(1)])

    rep(2, attend)
    pump4()
    rep(2, lambda h: attend(h + 2))

    def norm_att(i):
        v = att[ds(i, 32)]
        v = v - jnp.mean(v, -1, keepdims=True)
        f = lax.rsqrt(jnp.mean(v * v, -1, keepdims=True) + EPS)
        n = v * f
        normed[ds(i, 32)] = n
        inv[ds(i, 32)] = jnp.broadcast_to(f, (32, 128))
        gated[ds(i, 32)] = (n * proj[ds(i, 32), pl.ds(0, HID)].astype(F32)).astype(BF)

    rep(8, norm_att)
    pump5()

    def result(i):
        res[:, ds(i, 256)] = x_v[:, ds(i, 256)].astype(F32) + mm_t(gated[...], wout[ds(i, 256)])

    rep(4, result)

    def norm_out(i):
        v = res[ds(i, 32)]
        f = lax.rsqrt(jnp.sum(v * v, -1, keepdims=True) + EPS)
        rlen[ds(i, 32)] = jnp.broadcast_to(f, (32, 128))
        yall[0, ds(i, 32)] = (v * f).astype(BF)
        lay_o[ds(i, 32)] = v.astype(BF)

    rep(8, norm_out)
    cp_y = net.go(yall.at[0], ymate, w.mate())
    yr = net.go(yall.at[0], yall.at[7], w.zoff(1))
    yl = net.go(yall.at[0], yall.at[1], w.zoff(-1))
    pump6()
    rep(8, flip_in)
    cp_nin = net.go(ninT.at[:, 1 - c], ninTm, w.mate())
    cp_gated = net.go(gated, gatedm, w.mate())
    pump7()

    lacc[...] = jnp.zeros_like(lacc)
    cp_cand.wait_recv()
    cp_y.wait_recv()

    def base(dz):
        return (((z + dz) % 8) * 2 + c) * 512

    def score(dz):
        shard = tab[dz].reshape(512, D)
        lbuf[pl.ds(0, T)] = mm_t(yall[0], shard)
        lbuf[pl.ds(T, T)] = mm_t(ymate[...], shard)
        v0 = base(dz)

        def pick(i):
            line = lbuf[ds(i, 32)]
            ids = iota((32, 512), 1) + v0
            who = cand[ds(i, 32)]
            for k in range(NCAND):
                got = jnp.where(who[:, k:k + 1] == ids, line, 0.0)
                lacc[k, ds(i, 32)] += got[:, :128] + got[:, 128:256] + got[:, 256:384] + got[:, 384:]

        rep(16, pick)

    score(0)
    pump8()
    yr.wait_recv()
    yr2 = net.go(yall.at[7], yall.at[6], w.zoff(1))
    yl.wait_recv()
    yl2 = net.go(yall.at[1], yall.at[2], w.zoff(-1))
    for a, b in direct:
        a.wait_recv()
        b.wait_recv()
    score(1)
    score(7)

    def settle(name):
        for copy in flying[name]:
            copy.wait_recv()

    settle(6)
    score(6)
    settle(2)
    score(2)
    settle(5)
    score(5)
    settle(3)
    score(3)
    yr2.wait_recv()
    yr3 = net.go(yall.at[6], yall.at[5], w.zoff(1))
    yl2.wait_recv()
    yl3 = net.go(yall.at[2], yall.at[3], w.zoff(-1))
    settle("4x")
    settle("4y")
    score(4)

    lane = iota((2 * T, 128), 1)
    total = jnp.zeros((2 * T, 128), F32)
    for k in range(NCAND):
        total = jnp.where(lane == k, jnp.sum(lacc[k], -1, keepdims=True), total)
    lsum[...] = total
    cp_l = net.go(lsum, lrec, w.mate())
    cp_l.wait_recv()
    lrec_v = lrec[...]
    logits = (lsum[...] + jnp.concatenate([lrec_v[T:], lrec_v[:T]], 0)) / TEMP
    live = lane < NCAND
    ex = jnp.where(live, jnp.exp(jnp.where(live, logits, 0.0)), 0.0)
    soft = ex / jnp.sum(ex, -1, keepdims=True)
    gcol[...] = jnp.where(live, soft - (lane == 0).astype(F32), 0.0) / TEMP

    gsend[...] = gcol[pl.ds(0, T)].T[:8]
    gall[0] = gsend[...]
    cp_g = [net.go(gsend, gall.at[8 - k], w.zoff(k)) for k in range(1, 8)]

    def spread(i):
        dz, j = i // 16, i % 16
        ids = iota((32, 512), 1) + base(dz)
        who, how = cand[ds(j, 32)], gcol[ds(j, 32)]
        out = jnp.zeros((32, 512), F32)
        for k in range(NCAND):
            out = out + jnp.where(who[:, k:k + 1] == ids, how[:, k:k + 1], 0.0)
        sfull[ds(j, 32), ds(dz, 512)] = out.astype(BF)

    rep(128, spread)

    def gather_mate(i):
        rows = tab[:, :, :, :, ds(i, 256)].reshape(4096, 256)
        wsend[:, ds(i, 256)] = mm(sfull[pl.ds(T, T)], rows).astype(BF)

    rep(4, gather_mate)
    cp_w = net.go(wsend, wrec, w.mate())

    def gather_own(i):
        rows = tab[:, :, :, :, ds(i, 256)].reshape(4096, 256)
        wown[:, ds(i, 256)] = mm(sfull[pl.ds(0, T)], rows)

    rep(4, gather_own)
    yr3.wait_recv()
    half = D // 2
    yr4 = net.go(yall.at[5, :, pl.ds(0, half)], yall.at[4, :, pl.ds(0, half)], w.zoff(1))
    yl3.wait_recv()
    yl4 = net.go(yall.at[3, :, pl.ds(half, half)], yall.at[4, :, pl.ds(half, half)], w.zoff(-1))
    cp_w.wait_recv()

    def upstream(i):
        f = rlen[ds(i, 32)][:, :1]
        yn = res[ds(i, 32)] * f
        v = wown[ds(i, 32)] + wrec[ds(i, 32)].astype(F32)
        up = (v - yn * jnp.sum(yn * v, -1, keepdims=True)) * f
        upb[ds(i, 32)] = up.astype(BF)

    rep(8, upstream)

    gg[...] = mm(upb[...], wout[...])

    def back_norm(i):
        n, v = normed[ds(i, 32)], gg[ds(i, 32)]
        gpre[ds(i, 32), pl.ds(0, HID)] = (v * n * slope[ds(i, 32), pl.ds(0, HID)]).astype(BF)
        v = v * proj[ds(i, 32), pl.ds(0, HID)].astype(F32)
        v = v - jnp.mean(v, -1, keepdims=True) - n * jnp.mean(v * n, -1, keepdims=True)
        gatt[ds(i, 32)] = (inv[ds(i, 32)][:, :1] * v).astype(BF)

    rep(8, back_norm)

    def flip_up(i):
        block = upb[:, ds(i, 128)].astype(F32).T
        upT[i] = block.astype(BF).reshape(2, 64, T)

    rep(8, flip_up)
    cp_up = net.go(upT.at[:, 1 - c], upTm, w.mate())

    def back_attend(h):
        col = lambda part: pl.ds(pl.multiple_of(part * HID + h * 128, 128), 128)
        da = gatt[:, ds(h, 128)]
        ds_ = (mm_t(da, proj[:, col(1)]) * dsl[h])
        gv = mm(attn[h].astype(F32).T.astype(BF), da)
        gq = mm(ds_.astype(BF), proj[:, col(3)])
        gk = mm(ds_.T.astype(BF), proj[:, col(2)])
        gpre[:, col(1)] = (gv * slope[:, col(1)]).astype(BF)
        gpre[:, col(2)] = (gq * slope[:, col(2)]).astype(BF)
        gpre[:, col(3)] = (gk * slope[:, col(3)]).astype(BF)

    rep(4, back_attend)
    cp_pre = net.go(gpre, gprem, w.mate())

    def store_g(i, first, block):
        for b in range(block.shape[1] // 128):
            n = first + b
            g_o[n // 5, pl.ds(i * 4, 4), :, pl.ds((n % 5) * 128, 128)] = (
                block[:, b * 128:(b + 1) * 128].astype(BF).reshape(4, 64, 128))

    cp_gated.wait_recv()
    cp_up.wait_recv()

    def grad_out(i):
        a = upT[pl.ds(i * 4, 4), c].reshape(T, T)
        b = upTm[pl.ds(i * 4, 4)].reshape(T, T)
        store_g(i, 16, mm(a, gated[...]) + mm(b, gatedm[...]))

    rep(2, grad_out)
    cp_nin.wait_recv()
    cp_pre.wait_recv()

    def grad_in(i):
        a = ninT[pl.ds(i * 4, 4), c].reshape(T, T)
        b = ninTm[pl.ds(i * 4, 4)].reshape(T, T)
        for n in range(4):
            cols = pl.ds(n * 512, 512)
            store_g(i, n * 4, mm(a, gpre[:, cols]) + mm(b, gprem[:, cols]))

    rep(2, grad_in)

    for copy in cp_rows + cp_g:
        copy.wait_recv()

    def spread_t(i):
        dz, j = i // 8, i % 8
        ids = iota((128, T), 0) + (z * 1024 + j * 128)
        who, how = rall[dz], gall[dz]
        out = jnp.zeros((128, T), F32)
        for k in range(NCAND):
            out = out + jnp.where(who[k:k + 1, :] == ids, how[k:k + 1, :], 0.0)
        st[ds(j, 128), ds(dz, T)] = out.astype(BF)

    rep(64, spread_t)
    yr4.wait_recv()
    yl4.wait_recv()

    def h_mate(i):
        y = yall[:, :, ds(i, 256)].reshape(8 * T, 256)
        hsend[:, ds(i, 256)] = mm(st[ds(1 - c, 512)], y).astype(BF)

    rep(4, h_mate)
    cp_h = net.go(hsend, hrec, w.mate())

    def h_own(i):
        y = yall[:, :, ds(i, 256)].reshape(8 * T, 256)
        lbuf[:, pl.ds(0, 256)] = mm(st[ds(c, 512)], y)
        h_o[:, ds(i, 256)] = lbuf[:, pl.ds(0, 256)].astype(BF)

    rep(4, h_own)
    cp_h.wait_recv()

    def h_add(i):
        h_o[ds(i, 32)] = (h_o[ds(i, 32)].astype(F32) + hrec[ds(i, 32)].astype(F32)).astype(BF)

    rep(16, h_add)
    net.drain()


def train_call(lengths, cols, rows, events, in_weight, out_weight, item_table):
    vm = lambda *shape, dtype=BF: pltpu.VMEM(shape, dtype)
    scratch = [
        vm(T, D), vm(D, 4 * HID), vm(D, HID), vm(512, D), vm(8, 4, 4, 32, D), vm(2, 32, D), vm(T, D),
        vm(T, 4 * HID, dtype=F32), vm(T, 4 * HID), vm(HEADS, T, T), vm(HEADS, T, T, dtype=F32),
        vm(T, HID, dtype=F32), vm(T, HID, dtype=F32), vm(T, 128, dtype=F32), vm(T, HID), vm(T, HID),
        vm(T, D, dtype=F32), vm(T, 128, dtype=F32), vm(8, T, D), vm(T, D), vm(2 * T, 128, dtype=I32),
        vm(8, 8, T, dtype=I32), vm(8, 8, T, dtype=F32), vm(8, T, dtype=F32), vm(2 * T, 512, dtype=F32),
        vm(NCAND, 2 * T, 128, dtype=F32), vm(2 * T, 128, dtype=F32), vm(2 * T, 128, dtype=F32),
        vm(2 * T, 128, dtype=F32), vm(2 * T, 4096), vm(T, D, dtype=F32), vm(T, D), vm(T, D), vm(T, D),
        vm(T, HID, dtype=F32), vm(T, HID), vm(T, 4 * HID), vm(T, 4 * HID), vm(8, 2, 64, T), vm(8, 64, T),
        vm(8, 2, 64, T), vm(8, 64, T), vm(1024, 8 * T), vm(512, D), vm(512, D), vm(T, T, dtype=F32),
        pltpu.SemaphoreType.DMA((4,)), pltpu.SemaphoreType.DMA((NSEM1,)), pltpu.SemaphoreType.DMA((NSEM1,)),
    ]
    any_ = pl.BlockSpec(memory_space=pl.ANY)
    vmem = pl.BlockSpec(memory_space=pltpu.VMEM)
    return pl.pallas_call(
        train_kernel,
        out_shape=(jax.ShapeDtypeStruct((T, D), BF), jax.ShapeDtypeStruct((4, 8, 64, 640), BF),
                   jax.ShapeDtypeStruct((512, D), BF)),
        in_specs=[pl.BlockSpec(memory_space=pltpu.SMEM), vmem, vmem, any_, any_, any_, any_],
        out_specs=(vmem, vmem, vmem),
        scratch_shapes=scratch,
        compiler_params=pltpu.CompilerParams(collective_id=0, has_side_effects=True, vmem_limit_bytes=VMEM_BYTES),
        name="train",
    )(lengths, cols, rows, events, in_weight, out_weight, item_table)


def body(events, lengths, destinations, history, negatives, in_weight, out_weight, item_table):
    cands = jnp.concatenate([history[:, None], negatives], 1)
    cols = jnp.pad(cands, ((0, 0), (0, 124)))
    rows = jnp.pad(cands.T, ((0, 4), (0, 0)))
    result, g, h = train_call(lengths, cols, rows, events, in_weight, out_weight, item_table)
    return finish(result, g, h, lengths, destinations, item_table)


def finish(result, g, h, lengths, destinations, item_table):
    owners = 16
    s = lax.axis_index("seq")
    c = s % 2
    mine = g.transpose(1, 2, 0, 3).reshape(8, 64, 2560)
    zero = jnp.zeros_like(mine)
    whole = jnp.stack([jnp.where(c == 0, mine, zero), jnp.where(c == 1, mine, zero)], 1).reshape(1024, 2560)
    shard = lax.psum_scatter(whole, "seq", scatter_dimension=0, tiled=True)
    h, shard = lax.psum(h, "grp"), lax.psum(shard, "grp")
    e = item_table.astype(F32)
    inv = lax.rsqrt(jnp.sum(e * e, -1, keepdims=True) + EPS)
    en = e * inv
    hf = h.astype(F32)
    table_grad = (hf - en * jnp.sum(en * hf, -1, keepdims=True)) * inv
    shard = shard.astype(F32)
    user_lengths, user_dests = lengths[0], destinations[0]
    starts = jnp.cumsum(user_lengths) - user_lengths
    chosen = (user_dests[None, :] == jnp.arange(owners)[:, None]).astype(I32)
    send_length = jnp.sum(chosen * user_lengths[None, :], 1)
    send_start = jnp.sum(chosen * starts[None, :], 1)
    slot = jnp.arange(24)
    filled = slot[None, :] < send_length[:, None]
    src = jnp.clip(send_start[:, None] + slot[None, :], 0, T - 1)
    out = jnp.where(filled[..., None], result[src], jnp.zeros((), BF))
    got = lax.all_to_all(out, "seq", split_axis=0, concat_axis=0, tiled=True)
    cnt = lax.all_to_all(send_length[:, None], "seq", split_axis=0, concat_axis=0, tiled=True)[:, 0]
    block_ends = jnp.cumsum(cnt)
    offsets = block_ends - cnt
    pos = jnp.arange(T)
    anchor = jnp.minimum(jnp.sum((block_ends[None, :] <= pos[:, None]).astype(I32), 1), owners - 1)
    placed = anchor * 24 + pos - offsets[anchor]
    layer_out = got.reshape(-1, D)[placed]
    return layer_out, shard[:, :2048], shard[:, 2048:], table_grad


def solution(mesh):
    return jax.shard_map(
        body,
        mesh=mesh,
        in_specs=(
            P(("grp", "seq"), None),
            P(("grp", "seq"), None),
            P(("grp", "seq"), None),
            P(("grp", "seq")),
            P(("grp", "seq"), None),
            P(),
            P(),
            P("seq", None),
        ),
        out_specs=(P(("grp", "seq"), None), P("seq", None), P("seq", None), P("seq", None)),
        check_vma=False,
    )
```

time: 401 us -> 330 us (0.82)
  Pallas kernels: 0 us -> 114 us
  waiting for transfers between devices: 216 us -> 131 us
  other arithmetic: 59.3 us -> 23.6 us
  starting transfers between devices: 41.1 us -> 14.5 us
  local copies, waits for them, and re-layouts: 53.1 us -> 32.4 us
  matrix products: 15.2 us -> 0 us
    pallas_call x0 -> x1, Pallas kernels: none -> 114 us  [train_call(): pl.pallas_call(train_kernel, out_shape=(jax.ShapeDtypeStruct((T, D), BF),...]
    all_to_all x6 -> x2, waiting for transfers between devices: 100 us -> 7.16 us  [the longest x1 7.16 us: finish(): got = lax.all_to_all(out, 'seq', split_axis=0, concat_axis=0, tiled=True)]
    reduce_scatter x1, waiting for transfers between devices: 11.9 us -> 50 us  [finish(): shard = lax.psum_scatter(whole, 'seq', scatter_dimension=0, tiled=True)]
    psum x1, waiting for transfers between devices: 103 us -> 74.1 us  [finish(): h, shard = (lax.psum(h, 'grp'), lax.psum(shard, 'grp'))]
    all_to_all x6 -> x2, starting transfers between devices: 40.6 us -> 14.4 us  [the longest x1 8.04 us: finish(): got = lax.all_to_all(out, 'seq', split_axis=0, concat_axis=0, tiled=True)]
    select_n x2 -> x5, local copies, waits for them, and re-layouts: 0.16 us -> 18.7 us  [the longest x2 10.8 us: finish(): jnp.where(c == 1, mine, zero)]
    gather x9 -> x3, local copies, waits for them, and re-layouts: 21.2 us -> 4.76 us  [the longest x1 2.07 us: finish(): out = jnp.where(filled[..., None], result[src], jnp.zeros((), BF))]
    dot_general x29 -> x0, matrix products: 15.2 us -> none  [the longest x24 5.75 us: batch_stacked(): jnp.einsum(pattern, first_operand, second_operand, preferred_element_type...]
  transfers between devices with their start and end apart: 8 -> 4, of which waited for: 7 -> 3; matrix products, arithmetic and copies ran while one was open for 18% -> 6% of each run, Pallas kernels for 0% -> 0%
where the time goes in v1:
time: 330 us
  waiting for transfers between devices  131 us (40%)
  Pallas kernels  114 us (35%)
  local copies, waits for them, and re-layouts  32.4 us (10%)
  other arithmetic  23.6 us (7%)
  starting transfers between devices  14.5 us (4%)
  between operations  14.2 us (4%)
    pallas_call x1, Pallas kernels, train_call(): pl.pallas_call(train_kernel, out_shape=(jax.ShapeDtypeStruct((T, D), BF),...  114 us
    psum x1, waiting for transfers between devices, finish(): h, shard = (lax.psum(h, 'grp'), lax.psum(shard, 'grp'))  74.1 us
    reduce_scatter x1, waiting for transfers between devices, finish(): shard = lax.psum_scatter(whole, 'seq', scatter_dimension=0, tiled=True)  50 us
    select_n x2, local copies, waits for them, and re-layouts, finish(): jnp.where(c == 1, mine, zero)  10.8 us
    gather x3, other arithmetic, finish(): placed = anchor * 24 + pos - offsets[anchor]  10.3 us
    all_to_all x1, starting transfers between devices, finish(): got = lax.all_to_all(out, 'seq', split_axis=0, concat_axis=0, tiled=True)  8.04 us
    select_n x2, local copies, waits for them, and re-layouts, finish(): jnp.where(c == 0, mine, zero)  7.84 us
    all_to_all x1, waiting for transfers between devices, finish(): got = lax.all_to_all(out, 'seq', split_axis=0, concat_axis=0, tiled=True)  7.16 us
  transfers between devices with their start and end apart: 4, of which 3 were waited for; matrix products, arithmetic and copies ran while one was open for 6% of the time, Pallas kernels for 0%

profile of v1, /device:TPU:32, one launch (start us, length us, event | category | flops | bytes accessed | tf_op | source)
XLA Modules:
  0.0 329.5 jit_solution(5206446989598316069)
XLA Ops:
  7.2 0.7 pad_add_fusion
  7.9 0.7 fusion.5
  8.8 0.7 pad.8.clone.cols_v
  9.4 0.6 pad.9.rows_v
  10.0 113.6 %train.1 = (bf16[256,1024]{1,0:T(8,128)(2,1)}, bf16[4,8,64,640]{3,2,1,0:T(8,128)(2,1)}, bf16[512,1024]{1,0:T(8,128)(2,1)}) custom-call(s32[1,16]{1,0:T(1,128)} %len_s.1, s32[256,128]{1,0:T(8,128)} %pad.8.clone.cols_v, s32[8,256]{1,0:T(8,128)} %pad.9.rows_v, bf16[256,1024]{1,0:T(8,128)(2,1)} %ev_h.1, bf16[1024,2048]{1,0:T(8,128)(2,1)} %win_h.1, ...), custom_call_target="tpu_custom_call" | custom-call | tf_op jit(solution)/shard_map/train/pallas_call | solution.py:554
  123.7 3.7 %select_bitcast_fusion.1 = (bf16[8,64,4,640]{3,1,0,2:T(8,128)(2,1)S(1)}, bf16[8,64,4,640]{3,1,0,2:T(8,128)(2,1)}) fusion(bf16[4,8,64,640]{3,2,1,0:T(8,128)(2,1)} %get-tuple-element.8, pred[]{:T(512)S(6)} %eq.27, pred[]{:T(512)S(6)} %eq.28), kind=kLoop, calls=%fused_computation.8 | loop fusion | flops 2621440 | bytes 7864322 | tf_op jit(solution)/shard_map/jit(_where)/select_n | solution.py:580
  127.4 3.6 %copy.38 = bf16[8,64,4,640]{3,2,1,0:T(4,128)(2,1)} copy(bf16[8,64,4,640]{3,1,0,2:T(8,128)(2,1)S(1)} %get-tuple-element.25) | data formatting | bytes 5242880 | tf_op jit(solution)/shard_map/jit(_where)/select_n | solution.py:580
  130.9 4.3 %select_n.89 = bf16[8,1,64,2560]{3,2,0,1:T(8,128)(2,1)S(1)} reshape(bf16[8,64,4,640]{3,2,1,0:T(4,128)(2,1)} %copy.38) | data formatting | bytes 5242880 | tf_op jit(solution)/shard_map/jit(_where)/select_n | solution.py:580
  135.2 5.3 %copy.39 = bf16[8,64,4,640]{3,2,1,0:T(4,128)(2,1)} copy(bf16[8,64,4,640]{3,1,0,2:T(8,128)(2,1)} %get-tuple-element.26) | data formatting | bytes 5242880 | tf_op jit(solution)/shard_map/jit(_where)/select_n | solution.py:580
  140.5 5.5 %select_n.93 = bf16[8,1,64,2560]{3,2,0,1:T(8,128)(2,1)} reshape(bf16[8,64,4,640]{3,2,1,0:T(4,128)(2,1)} %copy.39) | data formatting | bytes 5242880 | tf_op jit(solution)/shard_map/jit(_where)/select_n | solution.py:580
  146.0 2.2 pad_maximum_fusion
  148.2 2.8 copy.40
  151.1 0.6 copy-done.3
  151.7 0.2 reduce-window_clone.1
  152.0 0.7 copy.36
  152.7 6.4 %all-to-all-start.1 = ((s32[16,1,1]{2,1,0:T(1,128)}), s32[16,1,1]{2,1,0:T(1,128)S(1)}, u32[]{:S(2)}, u32[]{:S(2)}) async-start(s32[16,1,1]{2,1,0:T(1,128)} %copy.36), calls=%async_computation.1 | async-start | bytes 16384 | tf_op jit(solution)/shard_map/all_to_all | solution.py:599
  159.3 2.1 gather_fusion
  161.4 0.3 fusion.3
  161.8 1.0 broadcast_select_fusion
  162.8 50.0 %reduce-scatter.2.cloned.1.call-done = bf16[64,2560]{1,0:T(8,128)(2,1)} async-done(((bf16[1024,2560]{1,0:T(8,128)(2,1)}), bf16[64,2560]{1,0:T(8,128)(2,1)}) %reduce-scatter.2.cloned.1.call-update) | async-done | bytes 327696 | tf_op jit(solution)/shard_map/reduce_scatter | solution.py:581
  212.8 8.0 %all-to-all-start = ((bf16[16,24,1024]{2,1,0:T(8,128)(2,1)}), bf16[16,24,1024]{2,1,0:T(8,128)(2,1)S(1)}, u32[]{:S(2)}, u32[]{:S(2)}) async-start(bf16[16,24,1024]{2,1,0:T(8,128)(2,1)} %broadcast_select_fusion), calls=%async_computation | async-start | bytes 1572864 | tf_op jit(solution)/shard_map/all_to_all | solution.py:598
  221.0 0.4 reduce.2
  221.4 0.7 fusion.4
  222.2 4.5 %compare_select_fusion.3 = (s32[256,1]{0,1:T(1,128)S(1)}, s32[256,1]{0,1:T(1,128)S(1)}) fusion(s32[]{:T(128)} %bitcast.19, s32[]{:T(128)} %bitcast.20, s32[]{:T(128)} %bitcast.21, s32[]{:T(128)} %bitcast.22, s32[]{:T(128)} %bitcast.23, s32[]{:T(128)} %bitcast.25, s32[]{:T(128)} %bitcast.24, s32[256,1]{0,1:T(1,128)S(1)} %bitcast.42), kind=kLoop, calls=%fused_computation.35 | loop fusion | flops 3840 | bytes 3100 | tf_op jit(solution)/shard_map/gather | solution.py:604
  226.7 5.8 %select_select_fusion = s32[256]{0:T(256)S(1)} fusion(pred[256]{0:T(512)(128)(4,1)S(1)} %get-tuple-element.18, pred[256]{0:T(512)(128)(4,1)S(1)} %get-tuple-element.17, pred[256]{0:T(512)(128)(4,1)S(1)} %get-tuple-element.16, pred[256]{0:T(512)(128)(4,1)S(1)} %get-tuple-element.15, pred[256]{0:T(512)(128)(4,1)S(1)} %get-tuple-element.14, ...), kind=kLoop, calls=%fused_computation.42 | loop fusion | flops 2304 | bytes 4388 | tf_op jit(solution)/shard_map/gather | solution.py:604
  232.5 7.2 %all-to-all-done = bf16[16,24,1024]{2,1,0:T(8,128)(2,1)S(1)} async-done(((bf16[16,24,1024]{2,1,0:T(8,128)(2,1)}), bf16[16,24,1024]{2,1,0:T(8,128)(2,1)S(1)}, u32[]{:S(2)}, u32[]{:S(2)}) %all-to-all-start) | async-done | bytes 786464 | tf_op jit(solution)/shard_map/all_to_all | solution.py:598
  239.7 2.0 gather_fusion.1
  241.7 74.1 %all-reduce.5.cloned.1.call-done = (bf16[64,2560]{1,0:T(8,128)(2,1)}, bf16[512,1024]{1,0:T(8,128)(2,1)}) async-done(((bf16[64,2560]{1,0:T(8,128)(2,1)}, bf16[512,1024]{1,0:T(8,128)(2,1)}), (bf16[64,2560]{1,0:T(8,128)(2,1)}, bf16[512,1024]{1,0:T(8,128)(2,1)})) %all-reduce.5.cloned.1.call-update) | async-done | bytes 1376272 | tf_op jit(solution)/shard_map/psum | solution.py:582
  315.8 1.9 slice.29
  317.7 1.5 slice.30
  319.2 1.7 fusion.1
  320.9 1.8 fusion.2
  (30 shorter events, 0.9 us)
Async XLA Ops:
  7.2 205.6 %reduce-scatter.2.cloned.1.call-start = ((), (), s32[]{:S(2)}) async-start(), calls=%async_computation.3 | async-start | bytes 5570560 | tf_op jit(solution)/shard_map/reduce_scatter | solution.py:581
  151.0 0.7 copy-start.3
  151.0 0.9 copy-start.4
  151.0 8.3 %copy-start = (bf16[256,1024]{1,0:T(8,128)(2,1)S(1)}, bf16[256,1024]{1,0:T(8,128)(2,1)}, u32[]{:S(2)}) copy-start(bf16[256,1024]{1,0:T(8,128)(2,1)} %get-tuple-element.7) | copy-start | bytes 1572868
  152.7 60.1 %all-to-all-start.1 = ((s32[16,1,1]{2,1,0:T(1,128)}), s32[16,1,1]{2,1,0:T(1,128)S(1)}, u32[]{:S(2)}, u32[]{:S(2)}) async-start(s32[16,1,1]{2,1,0:T(1,128)} %copy.36), calls=%async_computation.1 | async-start | bytes 16384 | tf_op jit(solution)/shard_map/all_to_all | solution.py:599
  159.1 156.7 %all-reduce.5.cloned.1.call-start = ((), (), s32[]{:S(2)}) async-start(), calls=%async_computation.4 | async-start | bytes 2752512 | tf_op jit(solution)/shard_map/psum | solution.py:582
  159.3 2.1 copy-start.1
  212.8 26.9 %all-to-all-start = ((bf16[16,24,1024]{2,1,0:T(8,128)(2,1)}), bf16[16,24,1024]{2,1,0:T(8,128)(2,1)S(1)}, u32[]{:S(2)}, u32[]{:S(2)}) async-start(bf16[16,24,1024]{2,1,0:T(8,128)(2,1)} %broadcast_select_fusion), calls=%async_computation | async-start | bytes 1572864 | tf_op jit(solution)/shard_map/all_to_all | solution.py:598
  315.8 5.1 %copy-start.2 = (bf16[512,1024]{1,0:T(8,128)(2,1)S(1)}, bf16[512,1024]{1,0:T(8,128)(2,1)}, u32[]{:S(2)}) copy-start(bf16[512,1024]{1,0:T(8,128)(2,1)} %get-tuple-element.22) | copy-start | bytes 3145732
Sparse Core Ops, SparseCore 0:
  151.2 61.4 reduce-scatter.1
  216.1 99.6 all-reduce.4

commit v2 on v1

--- a/solution.py
+++ b/solution.py
@@ -563,47 +563,172 @@
     )(lengths, cols, rows, events, in_weight, out_weight, item_table)
 
 
+class Ring:
+    def __init__(self, net, off, i, src, bufs, out):
+        self.net, self.off, self.i, self.src, self.out = net, off, i, src, out
+        self.t, self.u, self.v, self.r = bufs
+
+    def start(self):
+        far, right, left = (self.i + 2) % 4, (self.i + 1) % 4, (self.i + 3) % 4
+        go, off, src = self.net.go, self.off, self.src
+        self.ct = [go(src(far, 0), self.t.at[0], off(1)), go(src(far, 1), self.t.at[1], off(-1))]
+        self.cu = [go(src(left, 0), self.u.at[0], off(-1)), go(src(right, 1), self.u.at[1], off(1))]
+
+    def relay(self):
+        self.cr = []
+        for k, j in ((0, (self.i + 1) % 4), (1, (self.i + 3) % 4)):
+            self.ct[k].wait_recv()
+            self.v[k] = (self.t[k].astype(F32) + self.src(j, k)[...].astype(F32)).astype(BF)
+            self.cr.append(self.net.go(self.v.at[k], self.r.at[k], self.off(1 - 2 * k)))
+
+    def finish(self):
+        for k in range(2):
+            self.cr[k].wait_recv()
+            self.cu[k].wait_recv()
+            total = self.src(self.i, k)[...].astype(F32) + self.r[k].astype(F32) + self.u[k].astype(F32)
+            self.out(k)[...] = total.astype(BF)
+
+
+NSEM2 = 128
+
+
+def reduce_kernel(len_s, dst_s, res_v, g_v, h_v, lay_o, w_o, h_o,
+                  *refs):
+    (ga_b, gb_b, ha_b, hb_b, ga2_b, gb2_b, ha2_b, hb2_b) = [refs[4 * i:4 * i + 4] for i in range(8)]
+    (a1, b1, ha1, hb1, piece, zbuf, wpiece, hpiece, wall, hall, slots_s, slots_r, csend, cbuf, ssem, rsem) = refs[32:]
+    w = Where()
+    net = Links(ssem, rsem)
+    z, s, px, py = w.z, w.s, w.px, w.py
+    plane = [(i, j) for i in range(4) for j in range(4) if (i, j) != (0, 0)]
+
+    def peer(i, j):
+        return w.at(grp=((px + i) % 4) * 4 + (py + j) % 4)
+
+    for k in range(16):
+        slots_r[k, pl.ds(24, 8)] = jnp.zeros((8, D), BF)
+    lane = iota((8, 128), 1)
+    counts = jnp.zeros((8, 128), F32)
+    tr = iota((8, T), 1)
+    place = jnp.zeros((8, T), I32)
+    start = 0
+    for j in range(16):
+        n, d = len_s[0, j], dst_s[0, j]
+        counts = counts + jnp.where(lane == d, n, 0).astype(F32)
+        place = jnp.where((tr >= start) & (tr < start + n), d * 32 + tr - start, place)
+        start = start + n
+    csend[...] = counts
+    greet([w.at(seq=(s + k) % 16) for k in range(1, 16)] + [peer(i, j) for i, j in plane])
+
+    two = lambda k: pl.ds(2 * k, 2)
+    cut = lambda k: pl.ds(256 * k, 256)
+    hicut = lambda k: pl.ds(512 + 256 * k, 256)
+    ga = Ring(net, w.xoff, px, lambda j, k: g_v.at[j, two(k)], ga_b, lambda k: a1.at[two(k)])
+    gb = Ring(net, w.yoff, py, lambda j, k: g_v.at[:, pl.ds(4 + 2 * k, 2), j], gb_b, lambda k: b1.at[:, two(k)])
+    ha = Ring(net, w.xoff, px, lambda j, k: h_v.at[j, :, :, cut(k)], ha_b, lambda k: ha1.at[:, :, cut(k)])
+    hb = Ring(net, w.yoff, py, lambda j, k: h_v.at[:, j, :, hicut(k)], hb_b, lambda k: hb1.at[:, :, cut(k)])
+    ga2 = Ring(net, w.yoff, py, lambda j, k: a1.at[two(k), j], ga2_b, lambda k: piece.at[two(k)])
+    gb2 = Ring(net, w.xoff, px, lambda j, k: b1.at[j, two(k)], gb2_b, lambda k: piece.at[pl.ds(4 + 2 * k, 2)])
+    ha2 = Ring(net, w.yoff, py, lambda j, k: ha1.at[j, :, cut(k)], ha2_b, lambda k: hpiece.at[:, cut(k)])
+    hb2 = Ring(net, w.xoff, px, lambda j, k: hb1.at[j, :, cut(k)], hb2_b, lambda k: hpiece.at[:, hicut(k)])
+
+    for ring in (ga, gb, ha, hb):
+        ring.start()
+
+    cp_count = [net.go(csend, cbuf.at[s], w.at(seq=(s + k) % 16)) for k in range(1, 16)]
+    cbuf[s] = csend[...]
+
+    def fill(i):
+        pick = jnp.where(iota((128, T), 0) + i * 128 == place[:1, :], 1.0, 0.0).astype(BF)
+        slots_s[pl.ds(i * 4, 4)] = mm(pick, res_v[...]).astype(BF).reshape(4, 32, D)
+
+    rep(4, fill)
+    used = pl.ds(0, 24)
+    cp_slot = [net.go(slots_s.at[(s + k) % 16, used], slots_r.at[s, used], w.at(seq=(s + k) % 16))
+               for k in range(1, 16)]
+    slots_r[s, used] = slots_s[s, used]
+
+    for ring in (ga, gb, ha, hb):
+        ring.relay()
+    for ring, after in ((ga, ga2), (gb, gb2), (ha, ha2), (hb, hb2)):
+        ring.finish()
+        after.start()
+    for ring in (ga2, gb2, ha2, hb2):
+        ring.relay()
+    ga2.finish()
+    gb2.finish()
+    cp_z = [net.go(piece.at[(z + k) % 8], zbuf.at[k], w.zoff(k)) for k in range(1, 8)]
+    ha2.finish()
+    hb2.finish()
+    cp_h = [net.go(hpiece, hall.at[px, py], peer(i, j)) for i, j in plane]
+    hall[px, py] = hpiece[...]
+    total = piece[z].astype(F32)
+    for k in range(1, 8):
+        cp_z[k - 1].wait_recv()
+        total = total + zbuf[k].astype(F32)
+    wpiece[...] = total.astype(BF)
+    cp_w = [net.go(wpiece, wall.at[px, py], peer(i, j)) for i, j in plane]
+    wall[px, py] = wpiece[...]
+
+    for copy in cp_count + cp_slot:
+        copy.wait_recv()
+    cnt = jnp.sum(jnp.where(iota((16, 128), 1) == s, cbuf[:, 0, :], 0.0), -1, keepdims=True)
+    row, col = iota((16, 512), 0), iota((16, 512), 1)
+    slot = col >> 5
+    before = jnp.sum(jnp.where(row < slot, cnt, 0.0), 0, keepdims=True)
+    here = jnp.sum(jnp.where(row == slot, cnt, 0.0), 0, keepdims=True)
+    inside = (col[:1] & 31).astype(F32)
+    goal = jnp.where(inside < here, before + inside, -1.0)
+    picks = jnp.where(iota((T, 512), 0).astype(F32) == goal, 1.0, 0.0).astype(BF)
+
+    def land(i):
+        lay_o[:, ds(i, 256)] = mm(picks, slots_r[:, :, ds(i, 256)].reshape(512, 256)).astype(BF)
+
+    rep(4, land)
+    for copy in cp_w:
+        copy.wait_recv()
+    w_o[...] = wall[...]
+    for copy in cp_h:
+        copy.wait_recv()
+    h_o[...] = hall[...]
+    net.drain()
+
+
+def reduce_call(lengths, destinations, result, g, h):
+    vm = lambda *shape, dtype=BF: pltpu.VMEM(shape, dtype)
+    halves = [(2, 4, 16, 640), (4, 2, 16, 640), (4, 32, 256), (4, 32, 256), (2, 16, 640), (2, 16, 640), (32, 256), (32, 256)]
+    scratch = [vm(2, *shape) for shape in halves for _ in range(4)] + [
+        vm(4, 4, 16, 640), vm(4, 4, 16, 640), vm(4, 32, 512), vm(4, 32, 512), vm(8, 16, 640), vm(8, 16, 640),
+        vm(16, 640), vm(32, D), vm(4, 4, 16, 640), vm(4, 4, 32, D), vm(16, 32, D), vm(16, 32, D),
+        vm(8, 128, dtype=F32), vm(16, 8, 128, dtype=F32),
+        pltpu.SemaphoreType.DMA((NSEM2,)), pltpu.SemaphoreType.DMA((NSEM2,)),
+    ]
+    vmem = pl.BlockSpec(memory_space=pltpu.VMEM)
+    smem = pl.BlockSpec(memory_space=pltpu.SMEM)
+    return pl.pallas_call(
+        reduce_kernel,
+        out_shape=(jax.ShapeDtypeStruct((T, D), BF), jax.ShapeDtypeStruct((4, 4, 16, 640), BF),
+                   jax.ShapeDtypeStruct((4, 4, 32, D), BF)),
+        in_specs=[smem, smem, vmem, vmem, vmem],
+        out_specs=(vmem, vmem, vmem),
+        scratch_shapes=scratch,
+        compiler_params=pltpu.CompilerParams(collective_id=1, has_side_effects=True, vmem_limit_bytes=VMEM_BYTES),
+        name="reduce",
+    )(lengths, destinations, result, g.reshape(4, 8, 4, 16, 640), h.reshape(4, 4, 32, D))
+
+
 def body(events, lengths, destinations, history, negatives, in_weight, out_weight, item_table):
     cands = jnp.concatenate([history[:, None], negatives], 1)
     cols = jnp.pad(cands, ((0, 0), (0, 124)))
     rows = jnp.pad(cands.T, ((0, 4), (0, 0)))
     result, g, h = train_call(lengths, cols, rows, events, in_weight, out_weight, item_table)
-    return finish(result, g, h, lengths, destinations, item_table)
-
-
-def finish(result, g, h, lengths, destinations, item_table):
-    owners = 16
-    s = lax.axis_index("seq")
-    c = s % 2
-    mine = g.transpose(1, 2, 0, 3).reshape(8, 64, 2560)
-    zero = jnp.zeros_like(mine)
-    whole = jnp.stack([jnp.where(c == 0, mine, zero), jnp.where(c == 1, mine, zero)], 1).reshape(1024, 2560)
-    shard = lax.psum_scatter(whole, "seq", scatter_dimension=0, tiled=True)
-    h, shard = lax.psum(h, "grp"), lax.psum(shard, "grp")
+    layer_out, wsum, hsum = reduce_call(lengths, destinations, result, g, h)
+    wsum = wsum.astype(F32).transpose(1, 2, 0, 3).reshape(64, 2560)
     e = item_table.astype(F32)
     inv = lax.rsqrt(jnp.sum(e * e, -1, keepdims=True) + EPS)
     en = e * inv
-    hf = h.astype(F32)
+    hf = hsum.astype(F32).reshape(512, D)
     table_grad = (hf - en * jnp.sum(en * hf, -1, keepdims=True)) * inv
-    shard = shard.astype(F32)
-    user_lengths, user_dests = lengths[0], destinations[0]
-    starts = jnp.cumsum(user_lengths) - user_lengths
-    chosen = (user_dests[None, :] == jnp.arange(owners)[:, None]).astype(I32)
-    send_length = jnp.sum(chosen * user_lengths[None, :], 1)
-    send_start = jnp.sum(chosen * starts[None, :], 1)
-    slot = jnp.arange(24)
-    filled = slot[None, :] < send_length[:, None]
-    src = jnp.clip(send_start[:, None] + slot[None, :], 0, T - 1)
-    out = jnp.where(filled[..., None], result[src], jnp.zeros((), BF))
-    got = lax.all_to_all(out, "seq", split_axis=0, concat_axis=0, tiled=True)
-    cnt = lax.all_to_all(send_length[:, None], "seq", split_axis=0, concat_axis=0, tiled=True)[:, 0]
-    block_ends = jnp.cumsum(cnt)
-    offsets = block_ends - cnt
-    pos = jnp.arange(T)
-    anchor = jnp.minimum(jnp.sum((block_ends[None, :] <= pos[:, None]).astype(I32), 1), owners - 1)
-    placed = anchor * 24 + pos - offsets[anchor]
-    layer_out = got.reshape(-1, D)[placed]
-    return layer_out, shard[:, :2048], shard[:, 2048:], table_grad
+    return layer_out, wsum[:, :2048], wsum[:, 2048:], table_grad
 
 
 def solution(mesh):

time: 330 us -> 178 us (0.54)
  waiting for transfers between devices: 131 us -> 0 us
  Pallas kernels: 114 us -> 166 us
  local copies, waits for them, and re-layouts: 32.4 us -> 4.18 us
  other arithmetic: 23.6 us -> 5.34 us
  starting transfers between devices: 14.5 us -> 0 us
  between operations: 14.2 us -> 0.73 us
    psum x1 -> x0, waiting for transfers between devices: 74.1 us -> none  [finish(): h, shard = (lax.psum(h, 'grp'), lax.psum(shard, 'grp'))]
    pallas_call x0 -> x1, Pallas kernels: none -> 52.5 us  [reduce_call(): pl.pallas_call(reduce_kernel, out_shape=(jax.ShapeDtypeStruct((T, D), BF)...]
    reduce_scatter x1 -> x0, waiting for transfers between devices: 50 us -> none  [finish(): shard = lax.psum_scatter(whole, 'seq', scatter_dimension=0, tiled=True)]
    select_n x5 -> x0, local copies, waits for them, and re-layouts: 18.7 us -> none  [the longest x2 10.8 us: finish(): jnp.where(c == 1, mine, zero)]
    all_to_all x2 -> x0, starting transfers between devices: 14.4 us -> none  [the longest x1 8.04 us: finish(): got = lax.all_to_all(out, 'seq', split_axis=0, concat_axis=0, tiled=True)]
    gather x5 -> x0, other arithmetic: 10.3 us -> none  [the longest x3 10.3 us: finish(): placed = anchor * 24 + pos - offsets[anchor]]
    all_to_all x2 -> x0, waiting for transfers between devices: 7.16 us -> none  [the longest x1 7.16 us: finish(): got = lax.all_to_all(out, 'seq', split_axis=0, concat_axis=0, tiled=True)]
    select_n x4 -> x0, other arithmetic: 4.79 us -> none  [the longest x1 3.69 us: finish(): jnp.where(c == 0, mine, zero)]
  transfers between devices with their start and end apart: 4 -> 0, of which waited for: 3 -> 0; matrix products, arithmetic and copies ran while one was open for 6% -> 0% of each run, Pallas kernels for 0% -> 0%
where the time goes in v2:
time: 178 us; the launch traced here: 176 us
  Pallas kernels  166 us (93%)
  other arithmetic  5.34 us (3%)
  local copies, waits for them, and re-layouts  4.18 us (2%)
    pallas_call x1, Pallas kernels, train_call(): pl.pallas_call(train_kernel, out_shape=(jax.ShapeDtypeStruct((T, D), BF),...  114 us
    pallas_call x1, Pallas kernels, reduce_call(): pl.pallas_call(reduce_kernel, out_shape=(jax.ShapeDtypeStruct((T, D), BF)...  52.5 us

profile of v2, /device:TPU:32, one launch (start us, length us, event | category | flops | bytes accessed | tf_op | source)
XLA Modules:
  0.0 176.3 jit_solution(5353909975706529143)
XLA Ops:
  0.6 0.7 pad_add_fusion
  1.3 0.1 copy.15
  1.5 0.7 pad.8.clone.cols_v
  2.2 0.7 fusion.4
  2.9 0.6 pad.9.rows_v
  3.5 113.6 %train.1 = (bf16[256,1024]{1,0:T(8,128)(2,1)}, bf16[4,8,64,640]{3,2,1,0:T(8,128)(2,1)}, bf16[512,1024]{1,0:T(8,128)(2,1)}) custom-call(s32[1,16]{1,0:T(1,128)} %len_s.3, s32[256,128]{1,0:T(8,128)} %pad.8.clone.cols_v, s32[8,256]{1,0:T(8,128)} %pad.9.rows_v, bf16[256,1024]{1,0:T(8,128)(2,1)} %ev_h.1, bf16[1024,2048]{1,0:T(8,128)(2,1)} %win_h.1, ...), custom_call_target="tpu_custom_call" | custom-call | tf_op jit(solution)/shard_map/train/pallas_call | solution.py:554
  117.1 0.0 copy-start
  117.1 52.5 %reduce.1 = (bf16[256,1024]{1,0:T(8,128)(2,1)}, bf16[4,4,16,640]{3,2,1,0:T(8,128)(2,1)}, bf16[4,4,32,1024]{3,2,1,0:T(8,128)(2,1)}) custom-call(s32[1,16]{1,0:T(1,128)} %len_s.3, s32[1,16]{1,0:T(1,128)} %dst_s.1, bf16[256,1024]{1,0:T(8,128)(2,1)} %get-tuple-element.10.res_v, bf16[4,8,4,16,640]{4,3,2,1,0:T(8,128)(2,1)} %bitcast.14, ...), custom_call_target="tpu_custom_call" | custom-call | tf_op jit(solution)/shard_map/reduce/pallas_call | solution.py:707
  169.5 0.0 copy-start.1
  169.5 0.0 copy-done
  169.6 0.3 fusion.1
  169.8 1.8 %fusion.2 = f32[512]{0:T(512)S(1)} fusion(bf16[512,1024]{1,0:T(8,128)(2,1)S(1)} %copy-done, bf16[4,4,32,1024]{3,2,1,0:T(8,128)(2,1)} %get-tuple-element.15, f32[512]{0:T(512)S(1)} %add_rsqrt_fusion), kind=kLoop, calls=%fused_computation.6 | loop fusion | flops 2620928 | bytes 2101248 | tf_op jit(solution)/shard_map/reduce_sum | solution.py:730
  171.6 0.0 copy-done.1
  171.6 0.0 copy-start.3
  171.6 1.8 %fusion.3 = f32[512,1024]{1,0:T(8,128)} fusion(bf16[512,1024]{1,0:T(8,128)(2,1)S(1)} %copy-done, bf16[4,4,32,1024]{3,2,1,0:T(8,128)(2,1)S(1)} %copy-done.1, f32[512]{0:T(512)S(1)} %fusion.2, f32[512]{0:T(512)S(1)} %add_rsqrt_fusion), kind=kLoop, calls=%fused_computation.7 | loop fusion | flops 3145728 | bytes 4198400 | tf_op jit(solution)/shard_map/mul | solution.py:730
  173.5 0.0 copy-done.3
  173.5 0.0 copy-start.2
  173.5 0.4 copy.14
  174.0 0.8 slice.8
  174.8 0.7 slice.9
  175.5 0.0 copy-done.2
  175.5 0.8 copy.18
  (3 shorter events, 0.1 us)
Async XLA Ops:
  117.1 52.5 %copy-start = (bf16[512,1024]{1,0:T(8,128)(2,1)S(1)}, bf16[512,1024]{1,0:T(8,128)(2,1)}, u32[]{:S(2)}) copy-start(bf16[512,1024]{1,0:T(8,128)(2,1)} %tab_h.1) | copy-start | bytes 3145732
  169.5 2.1 %copy-start.1 = (bf16[4,4,32,1024]{3,2,1,0:T(8,128)(2,1)S(1)}, bf16[4,4,32,1024]{3,2,1,0:T(8,128)(2,1)}, u32[]{:S(2)}) copy-start(bf16[4,4,32,1024]{3,2,1,0:T(8,128)(2,1)} %get-tuple-element.15) | copy-start | bytes 3145732
  171.6 1.8 %copy-start.3 = (bf16[4,4,16,640]{3,2,1,0:T(8,128)(2,1)S(1)}, bf16[4,4,16,640]{3,2,1,0:T(8,128)(2,1)}, u32[]{:S(2)}) copy-start(bf16[4,4,16,640]{3,2,1,0:T(8,128)(2,1)} %get-tuple-element.14) | copy-start | bytes 983044
  173.5 2.0 %copy-start.2 = (bf16[256,1024]{1,0:T(8,128)(2,1)S(1)}, bf16[256,1024]{1,0:T(8,128)(2,1)}, u32[]{:S(2)}) copy-start(bf16[256,1024]{1,0:T(8,128)(2,1)} %get-tuple-element.20) | copy-start | bytes 1572868

commit v3 on v1

--- a/solution.py
+++ b/solution.py
@@ -83,6 +83,32 @@
             copy.wait_send()
 
 
+class Ring:
+    def __init__(self, net, off, i, src, bufs, out):
+        self.net, self.off, self.i, self.src, self.out = net, off, i, src, out
+        self.t, self.u, self.v, self.r = bufs
+
+    def start(self):
+        far, right, left = (self.i + 2) % 4, (self.i + 1) % 4, (self.i + 3) % 4
+        go, off, src = self.net.go, self.off, self.src
+        self.ct = [go(src(far, 0), self.t.at[0], off(1)), go(src(far, 1), self.t.at[1], off(-1))]
+        self.cu = [go(src(left, 0), self.u.at[0], off(-1)), go(src(right, 1), self.u.at[1], off(1))]
+
+    def relay(self):
+        self.cr = []
+        for k, j in ((0, (self.i + 1) % 4), (1, (self.i + 3) % 4)):
+            self.ct[k].wait_recv()
+            self.v[k] = (self.t[k].astype(F32) + self.src(j, k)[...].astype(F32)).astype(BF)
+            self.cr.append(self.net.go(self.v.at[k], self.r.at[k], self.off(1 - 2 * k)))
+
+    def finish(self):
+        for k in range(2):
+            self.cr[k].wait_recv()
+            self.cu[k].wait_recv()
+            total = self.src(self.i, k)[...].astype(F32) + self.r[k].astype(F32) + self.u[k].astype(F32)
+            self.out(k)[...] = total.astype(BF)
+
+
 def greet(devices):
     barrier = pltpu.get_barrier_semaphore()
     for dev in devices:
@@ -90,27 +116,32 @@
     pl.semaphore_wait(barrier, len(devices))
 
 
-NSEM1 = 128
-
-
-def train_kernel(len_s, cols_v, rows_v, ev_h, win_h, wout_h, tab_h, lay_o, g_o, h_o,
-                 x_v, win, wout, traw, tab, zb, nin, slope, proj, attn, dsl, att, normed, inv, gated, gatedm,
-                 res, rlen, yall, ymate, cand, rall, gall, gsend, lbuf, lacc, lsum, lrec, gcol, sfull,
-                 wown, wsend, wrec, upb, gg, gatt, gpre, gprem, ninT, ninTm, upT, upTm, st, hsend, hrec, mask_v,
-                 lsem, ssem, rsem):
+NSEM = 256
+
+
+def train_kernel(len_s, dst_s, hist_v, neg_v, ev_h, win_h, wout_h, tab_h, lay_o, w_o, h_o, *refs):
+    (x_v, win, wout, traw, tab, zb, nin, slope, proj, attn, dsl, att, normed, inv, gated, gatedm,
+     res, rlen, yall, ymate, ids_f, cand, rall, gall, gsend, lbuf, lsum, lrec, gcol, whob, sfull,
+     wown, wsend, wrec, upb, gg, gatt, gpre, gprem, ninT, ninTm, upT, upTm, hsend, hrec, mask_v, lout,
+     g_v, h_v, a1, b1, ha1, hb1, piece, zbuf, wpiece, wall, hall, slots_s, slots_r, csend, cbuf,
+     lsem, ssem, rsem) = refs[:len(refs) - 32]
+    bufs = refs[len(refs) - 32:]
+    (ga_b, gb_b, ha_b, hb_b, ga2_b, gb2_b, ha2_b, hb2_b) = [bufs[4 * i:4 * i + 4] for i in range(8)]
     w = Where()
     net = Links(ssem, rsem)
-    z, c, px, py, g = w.z, w.c, w.px, w.py, w.g
+    s, z, c, px, py, g = w.s, w.z, w.c, w.px, w.py, w.g
+    plane = [(i, j) for i in range(4) for j in range(4) if (i, j) != (0, 0)]
+
+    def peer(i, j):
+        return w.at(grp=((px + i) % 4) * 4 + (py + j) % 4)
+
     loads = [pltpu.make_async_copy(a, b, lsem.at[i]) for i, (a, b) in enumerate(
         ((tab_h, traw), (ev_h, x_v), (win_h, win), (wout_h, wout)))]
     for copy in loads:
         copy.start()
-    greet([w.at(seq=(w.s + k) % 16) for k in range(1, 16)] + [w.xoff(1), w.xoff(3), w.yoff(1), w.yoff(3)])
-
-    cand[pl.ds(0, T)] = cols_v[...]
-    rall[0] = rows_v[...]
-    cp_cand = net.go(cols_v, cand.at[pl.ds(T, T)], w.mate())
-    cp_rows = [net.go(rows_v, rall.at[8 - k], w.zoff(k)) for k in range(1, 8)]
+    for k in range(16):
+        slots_r[k, pl.ds(24, 8)] = jnp.zeros((8, D), BF)
+    greet([w.at(seq=(s + k) % 16) for k in range(1, 16)] + [peer(i, j) for i, j in plane])
 
     loads[0].wait()
 
@@ -124,6 +155,13 @@
     r1 = net.go(tab.at[0, px, py], zb.at[1], w.zoff(1))
     l1 = net.go(tab.at[0, px, py], zb.at[0], w.zoff(-1))
     rep(15, lambda i: norm_rows(i + 1))
+
+    ids_f[...] = jnp.full((128, T), -1.0, F32)
+    ids_f[pl.ds(0, 1)] = hist_v[...].astype(F32)
+    ids_f[pl.ds(1, 3)] = neg_v[...].astype(F32)
+    rall[0] = ids_f[pl.ds(0, 8)].astype(I32)
+    cand[pl.ds(0, T)] = ids_f[...].T.astype(I32)
+    cp_cand = net.go(cand.at[pl.ds(0, T)], cand.at[pl.ds(T, T)], w.mate())
 
     pieces = {6: (6, 0, 1024, "y"), 2: (2, 0, 1024, "x"), 5: (5, 0, 1024, "y"), 3: (3, 0, 1024, "x"),
               "4x": (4, 0, 512, "x"), "4y": (4, 512, 512, "y")}
@@ -189,7 +227,6 @@
         hop["r"] = net.go(zb.at[1], tab.at[6, px, py], w.zoff(1))
         l1.wait_recv()
         hop["l"] = net.go(zb.at[0], tab.at[2, px, py], w.zoff(-1))
-        shard_direct(0)
 
     def pump2():
         hop["r"].wait_recv()
@@ -198,7 +235,6 @@
         hop["l"] = net.go(tab.at[2, px, py], tab.at[3, px, py], w.zoff(-1))
         first_send(6)
         first_send(2)
-        shard_direct(1)
 
     def pump3():
         hop["r"].wait_recv()
@@ -206,12 +242,14 @@
         hop["l"].wait_recv()
         first_send(5)
         first_send(3)
+        for q in range(4):
+            shard_direct(q)
+
+    def pump4():
         first_forward(6)
         first_forward(2)
-        shard_direct(2)
-        shard_direct(3)
-
-    def pump4():
+
+    def pump5():
         hop["r"].wait_recv()
         first_send("4x")
         first_send("4y")
@@ -220,23 +258,23 @@
         second_send(6)
         second_send(2)
 
-    def pump5():
+    def pump6():
         first_forward("4x")
         first_forward("4y")
         second_send(5)
         second_send(3)
 
-    def pump6():
+    def pump7():
+        second_send("4x")
+        second_send("4y")
         second_forward(6)
         second_forward(2)
-        second_send("4x")
-        second_send("4y")
-
-    def pump7():
+
+    def pump8():
         second_forward(5)
         second_forward(3)
 
-    def pump8():
+    def pump9():
         second_forward("4x")
         second_forward("4y")
 
@@ -289,8 +327,8 @@
         att[:, ds(h, 128)] = mm(weight, proj[:, col(1)])
 
     rep(2, attend)
+    rep(2, lambda h: attend(h + 2))
     pump4()
-    rep(2, lambda h: attend(h + 2))
 
     def norm_att(i):
         v = att[ds(i, 32)]
@@ -314,61 +352,70 @@
         f = lax.rsqrt(jnp.sum(v * v, -1, keepdims=True) + EPS)
         rlen[ds(i, 32)] = jnp.broadcast_to(f, (32, 128))
         yall[0, ds(i, 32)] = (v * f).astype(BF)
-        lay_o[ds(i, 32)] = v.astype(BF)
+        lout[ds(i, 32)] = v.astype(BF)
 
     rep(8, norm_out)
     cp_y = net.go(yall.at[0], ymate, w.mate())
     yr = net.go(yall.at[0], yall.at[7], w.zoff(1))
     yl = net.go(yall.at[0], yall.at[1], w.zoff(-1))
+    cp_rows = [net.go(rall.at[0], rall.at[8 - k], w.zoff(k)) for k in range(1, 8)]
     pump6()
     rep(8, flip_in)
     cp_nin = net.go(ninT.at[:, 1 - c], ninTm, w.mate())
     cp_gated = net.go(gated, gatedm, w.mate())
-    pump7()
-
-    lacc[...] = jnp.zeros_like(lacc)
+
+    lsum[...] = jnp.zeros_like(lsum)
     cp_cand.wait_recv()
+
+    def owner(dz):
+        return ((z + dz) % 8) * 2 + c
+
+    def locate(i):
+        dz, j = i // 8, i % 8
+        who = cand[ds(j, 64)]
+        spot = jnp.where((who >> 9) == owner(dz), (who & 511) + 1, 0).astype(F32)
+        whob[dz, ds(j, 64)] = jnp.broadcast_to(jnp.sum(spot, -1, keepdims=True) - 1.0, (64, 128))
+
+    rep(64, locate)
     cp_y.wait_recv()
-
-    def base(dz):
-        return (((z + dz) % 8) * 2 + c) * 512
+    lanes = iota((64, 128), 1).astype(F32)
 
     def score(dz):
         shard = tab[dz].reshape(512, D)
         lbuf[pl.ds(0, T)] = mm_t(yall[0], shard)
         lbuf[pl.ds(T, T)] = mm_t(ymate[...], shard)
-        v0 = base(dz)
 
         def pick(i):
-            line = lbuf[ds(i, 32)]
-            ids = iota((32, 512), 1) + v0
-            who = cand[ds(i, 32)]
-            for k in range(NCAND):
-                got = jnp.where(who[:, k:k + 1] == ids, line, 0.0)
-                lacc[k, ds(i, 32)] += got[:, :128] + got[:, 128:256] + got[:, 256:384] + got[:, 384:]
-
-        rep(16, pick)
+            who = whob[dz, ds(i, 64)]
+            got = jnp.zeros((64, 128), F32)
+            for q in range(4):
+                got = got + jnp.where(who == lanes + 128.0 * q, lbuf[ds(i, 64), pl.ds(q * 128, 128)], 0.0)
+            value = jnp.sum(got, -1, keepdims=True)
+            lsum[ds(i, 64)] += jnp.where((cand[ds(i, 64)] >> 9) == owner(dz), value, 0.0)
+
+        rep(8, pick)
+
+    def settle(name):
+        for copy in flying[name]:
+            copy.wait_recv()
 
     score(0)
-    pump8()
+    pump7()
     yr.wait_recv()
     yr2 = net.go(yall.at[7], yall.at[6], w.zoff(1))
     yl.wait_recv()
     yl2 = net.go(yall.at[1], yall.at[2], w.zoff(-1))
+    pump8()
+    settle(6)
+    score(6)
+    settle(2)
+    score(2)
+    pump9()
     for a, b in direct:
         a.wait_recv()
         b.wait_recv()
     score(1)
     score(7)
-
-    def settle(name):
-        for copy in flying[name]:
-            copy.wait_recv()
-
-    settle(6)
-    score(6)
-    settle(2)
-    score(2)
     settle(5)
     score(5)
     settle(3)
@@ -382,10 +429,6 @@
     score(4)
 
     lane = iota((2 * T, 128), 1)
-    total = jnp.zeros((2 * T, 128), F32)
-    for k in range(NCAND):
-        total = jnp.where(lane == k, jnp.sum(lacc[k], -1, keepdims=True), total)
-    lsum[...] = total
     cp_l = net.go(lsum, lrec, w.mate())
     cp_l.wait_recv()
     lrec_v = lrec[...]
@@ -400,15 +443,15 @@
     cp_g = [net.go(gsend, gall.at[8 - k], w.zoff(k)) for k in range(1, 8)]
 
     def spread(i):
-        dz, j = i // 16, i % 16
-        ids = iota((32, 512), 1) + base(dz)
-        who, how = cand[ds(j, 32)], gcol[ds(j, 32)]
-        out = jnp.zeros((32, 512), F32)
-        for k in range(NCAND):
-            out = out + jnp.where(who[:, k:k + 1] == ids, how[:, k:k + 1], 0.0)
-        sfull[ds(j, 32), ds(dz, 512)] = out.astype(BF)
-
-    rep(128, spread)
+        dz, j = i // 8, i % 8
+        how = jnp.where((cand[ds(j, 64)] >> 9) == owner(dz), gcol[ds(j, 64)], 0.0)
+        how = jnp.broadcast_to(jnp.sum(how, -1, keepdims=True), (64, 128))
+        who = whob[dz, ds(j, 64)]
+        for q in range(4):
+            part = jnp.where(who == lanes + 128.0 * q, how, 0.0).astype(BF)
+            sfull[ds(j, 64), ds(dz * 4 + q, 128)] = part
+
+    rep(64, spread)
 
     def gather_mate(i):
         rows = tab[:, :, :, :, ds(i, 256)].reshape(4096, 256)
@@ -473,8 +516,8 @@
     def store_g(i, first, block):
         for b in range(block.shape[1] // 128):
             n = first + b
-            g_o[n // 5, pl.ds(i * 4, 4), :, pl.ds((n % 5) * 128, 128)] = (
-                block[:, b * 128:(b + 1) * 128].astype(BF).reshape(4, 64, 128))
+            g_v[n // 5, pl.ds(i * 4, 4), :, :, pl.ds((n % 5) * 128, 128)] = (
+                block[:, b * 128:(b + 1) * 128].astype(BF).reshape(4, 4, 16, 128))
 
     cp_gated.wait_recv()
     cp_up.wait_recv()
@@ -497,113 +540,202 @@
 
     rep(2, grad_in)
 
+    two = lambda k: pl.ds(2 * k, 2)
+    cut = lambda k: pl.ds(256 * k, 256)
+    hicut = lambda k: pl.ds(512 + 256 * k, 256)
+    ga = Ring(net, w.xoff, px, lambda j, k: g_v.at[j, two(k)], ga_b, lambda k: a1.at[two(k)])
+    gb = Ring(net, w.yoff, py, lambda j, k: g_v.at[:, pl.ds(4 + 2 * k, 2), j], gb_b, lambda k: b1.at[:, two(k)])
+    ha = Ring(net, w.xoff, px, lambda j, k: h_v.at[j, :, :, cut(k)], ha_b, lambda k: ha1.at[:, :, cut(k)])
+    hb = Ring(net, w.yoff, py, lambda j, k: h_v.at[:, j, :, hicut(k)], hb_b, lambda k: hb1.at[:, :, cut(k)])
+    ga2 = Ring(net, w.yoff, py, lambda j, k: a1.at[two(k), j], ga2_b, lambda k: piece.at[two(k)])
+    gb2 = Ring(net, w.xoff, px, lambda j, k: b1.at[j, two(k)], gb2_b, lambda k: piece.at[pl.ds(4 + 2 * k, 2)])
+    mine = hall.at[px, py]
+    ha2 = Ring(net, w.yoff, py, lambda j, k: ha1.at[j, :, cut(k)], ha2_b, lambda k: mine.at[:, cut(k)])
+    hb2 = Ring(net, w.xoff, px, lambda j, k: hb1.at[j, :, cut(k)], hb2_b, lambda k: mine.at[:, hicut(k)])
+    ga.start()
+    gb.start()
+
     for copy in cp_rows + cp_g:
         copy.wait_recv()
 
-    def spread_t(i):
-        dz, j = i // 8, i % 8
-        ids = iota((128, T), 0) + (z * 1024 + j * 128)
+    def spread_t(dz):
         who, how = rall[dz], gall[dz]
-        out = jnp.zeros((128, T), F32)
-        for k in range(NCAND):
-            out = out + jnp.where(who[k:k + 1, :] == ids, how[k:k + 1, :], 0.0)
-        st[ds(j, 128), ds(dz, T)] = out.astype(BF)
-
-    rep(64, spread_t)
+        for o in range(2):
+            hit = (who >> 9) == z * 2 + o
+            spot = jnp.sum(jnp.where(hit, (who & 511) + 1, 0).astype(F32), 0, keepdims=True) - 1.0
+            much = jnp.sum(jnp.where(hit, how, 0.0), 0, keepdims=True)
+            for j in range(4):
+                line = (iota((128, T), 0) + j * 128).astype(F32)
+                sfull[pl.ds(j * 128, 128), ds(dz + 8 * o, T)] = jnp.where(line == spot, much, 0.0).astype(BF)
+
+    rep(8, spread_t)
     yr4.wait_recv()
     yl4.wait_recv()
 
     def h_mate(i):
         y = yall[:, :, ds(i, 256)].reshape(8 * T, 256)
-        hsend[:, ds(i, 256)] = mm(st[ds(1 - c, 512)], y).astype(BF)
+        hsend[:, ds(i, 256)] = mm(sfull[:, ds(1 - c, 2048)], y).astype(BF)
 
     rep(4, h_mate)
     cp_h = net.go(hsend, hrec, w.mate())
+    ga.relay()
+    gb.relay()
 
     def h_own(i):
         y = yall[:, :, ds(i, 256)].reshape(8 * T, 256)
-        lbuf[:, pl.ds(0, 256)] = mm(st[ds(c, 512)], y)
-        h_o[:, ds(i, 256)] = lbuf[:, pl.ds(0, 256)].astype(BF)
+        lbuf[:, pl.ds(0, 256)] = mm(sfull[:, ds(c, 2048)], y)
+        wown[:, ds(i, 256)] = lbuf[pl.ds(0, T), pl.ds(0, 256)]
+        res[:, ds(i, 256)] = lbuf[pl.ds(T, T), pl.ds(0, 256)]
 
     rep(4, h_own)
     cp_h.wait_recv()
-
-    def h_add(i):
-        h_o[ds(i, 32)] = (h_o[ds(i, 32)].astype(F32) + hrec[ds(i, 32)].astype(F32)).astype(BF)
-
-    rep(16, h_add)
+    for part, src in ((0, wown), (1, res)):
+        for i in range(8):
+            total = src[pl.ds(i * 32, 32)] + hrec[pl.ds(part * T + i * 32, 32)].astype(F32)
+            h_v[part * 2 + i // 4, i % 4] = total.astype(BF)
+    ha.start()
+    hb.start()
+
+    lane8 = iota((8, 128), 1)
+    counts = jnp.zeros((8, 128), F32)
+    place = jnp.zeros((8, T), I32)
+    start = 0
+    for j in range(16):
+        n, d = len_s[0, j], dst_s[0, j]
+        counts = counts + jnp.where(lane8 == d, n, 0).astype(F32)
+        place = jnp.where((tr >= start) & (tr < start + n), d * 32 + tr - start, place)
+        start = start + n
+    csend[...] = counts
+    cp_count = [net.go(csend, cbuf.at[s], w.at(seq=(s + k) % 16)) for k in range(1, 16)]
+    cbuf[s] = csend[...]
+
+    def fill(i):
+        pick = jnp.where(iota((128, T), 0) + i * 128 == place[:1, :], 1.0, 0.0).astype(BF)
+        slots_s[pl.ds(i * 4, 4)] = mm(pick, lout[...]).astype(BF).reshape(4, 32, D)
+
+    rep(4, fill)
+    used = pl.ds(0, 24)
+    cp_slot = [net.go(slots_s.at[(s + k) % 16, used], slots_r.at[s, used], w.at(seq=(s + k) % 16))
+               for k in range(1, 16)]
+    slots_r[s, used] = slots_s[s, used]
+
+    ga.finish()
+    ga2.start()
+    gb.finish()
+    gb2.start()
+    ha.relay()
+    hb.relay()
+    ga2.relay()
+    gb2.relay()
+    ha.finish()
+    ha2.start()
+    hb.finish()
+    hb2.start()
+    ga2.finish()
+    gb2.finish()
+    cp_z = [net.go(piece.at[(z + k) % 8], zbuf.at[k], w.zoff(k)) for k in range(1, 8)]
+    ha2.relay()
+    hb2.relay()
+    total = piece[z].astype(F32)
+    for k in range(1, 8):
+        cp_z[k - 1].wait_recv()
+        total = total + zbuf[k].astype(F32)
+    wpiece[...] = total.astype(BF)
+    cp_w = [net.go(wpiece, wall.at[px, py], peer(i, j)) for i, j in plane]
+    wall[px, py] = wpiece[...]
+    ha2.finish()
+    hb2.finish()
+    cp_ha = [net.go(mine, mine, peer(i, j)) for i, j in plane]
+
+    for copy in cp_count + cp_slot:
+        copy.wait_recv()
+    cnt = jnp.sum(jnp.where(iota((16, 128), 1) == s, cbuf[:, 0, :], 0.0), -1, keepdims=True)
+    row, col16 = iota((16, 512), 0), iota((16, 512), 1)
+    slot = col16 >> 5
+    before = jnp.sum(jnp.where(row < slot, cnt, 0.0), 0, keepdims=True)
+    here = jnp.sum(jnp.where(row == slot, cnt, 0.0), 0, keepdims=True)
+    inside = (col16[:1] & 31).astype(F32)
+    goal = jnp.where(inside < here, before + inside, -1.0)
+    picks = jnp.where(iota((T, 512), 0).astype(F32) == goal, 1.0, 0.0).astype(BF)
+
+    def land(i):
+        lay_o[:, ds(i, 256)] = mm(picks, slots_r[:, :, ds(i, 256)].reshape(512, 256)).astype(BF)
+
+    rep(4, land)
+    for copy in cp_w:
+        copy.wait_recv()
+    w_o[...] = wall[...]
+    for copy in cp_ha:
+        copy.wait_recv()
+    h_o[...] = hall[...]
     net.drain()
 
 
-def train_call(lengths, cols, rows, events, in_weight, out_weight, item_table):
+def train_call(lengths, destinations, hist, neg, events, in_weight, out_weight, item_table):
     vm = lambda *shape, dtype=BF: pltpu.VMEM(shape, dtype)
+    f32 = dict(dtype=F32)
+    halves = [(2, 4, 16, 640), (4, 2, 16, 640), (4, 32, 256), (4, 32, 256), (2, 16, 640), (2, 16, 640), (32, 256), (32, 256)]
+    sem = pltpu.SemaphoreType.DMA
     scratch = [
         vm(T, D), vm(D, 4 * HID), vm(D, HID), vm(512, D), vm(8, 4, 4, 32, D), vm(2, 32, D), vm(T, D),
-        vm(T, 4 * HID, dtype=F32), vm(T, 4 * HID), vm(HEADS, T, T), vm(HEADS, T, T, dtype=F32),
-        vm(T, HID, dtype=F32), vm(T, HID, dtype=F32), vm(T, 128, dtype=F32), vm(T, HID), vm(T, HID),
-        vm(T, D, dtype=F32), vm(T, 128, dtype=F32), vm(8, T, D), vm(T, D), vm(2 * T, 128, dtype=I32),
-        vm(8, 8, T, dtype=I32), vm(8, 8, T, dtype=F32), vm(8, T, dtype=F32), vm(2 * T, 512, dtype=F32),
-        vm(NCAND, 2 * T, 128, dtype=F32), vm(2 * T, 128, dtype=F32), vm(2 * T, 128, dtype=F32),
-        vm(2 * T, 128, dtype=F32), vm(2 * T, 4096), vm(T, D, dtype=F32), vm(T, D), vm(T, D), vm(T, D),
-        vm(T, HID, dtype=F32), vm(T, HID), vm(T, 4 * HID), vm(T, 4 * HID), vm(8, 2, 64, T), vm(8, 64, T),
-        vm(8, 2, 64, T), vm(8, 64, T), vm(1024, 8 * T), vm(512, D), vm(512, D), vm(T, T, dtype=F32),
-        pltpu.SemaphoreType.DMA((4,)), pltpu.SemaphoreType.DMA((NSEM1,)), pltpu.SemaphoreType.DMA((NSEM1,)),
-    ]
+        vm(T, 4 * HID, **f32), vm(T, 4 * HID), vm(HEADS, T, T), vm(HEADS, T, T, **f32),
+        vm(T, HID, **f32), vm(T, HID, **f32), vm(T, 128, **f32), vm(T, HID), vm(T, HID),
+        vm(T, D, **f32), vm(T, 128, **f32), vm(8, T, D), vm(T, D), vm(128, T, **f32), vm(2 * T, 128, dtype=I32),
+        vm(8, 8, T, dtype=I32), vm(8, 8, T, **f32), vm(8, T, **f32), vm(2 * T, 512, **f32),
+        vm(2 * T, 128, **f32), vm(2 * T, 128, **f32), vm(2 * T, 128, **f32), vm(8, 2 * T, 128, **f32),
+        vm(2 * T, 4096), vm(T, D, **f32), vm(T, D), vm(T, D), vm(T, D),
+        vm(T, HID, **f32), vm(T, HID), vm(T, 4 * HID), vm(T, 4 * HID), vm(8, 2, 64, T), vm(8, 64, T),
+        vm(8, 2, 64, T), vm(8, 64, T), vm(512, D), vm(512, D), vm(T, T, **f32), vm(T, D),
+        vm(4, 8, 4, 16, 640), vm(4, 4, 32, D),
+        vm(4, 4, 16, 640), vm(4, 4, 16, 640), vm(4, 32, 512), vm(4, 32, 512), vm(8, 16, 640), vm(8, 16, 640),
+        vm(16, 640), vm(4, 4, 16, 640), vm(4, 4, 32, D), vm(16, 32, D), vm(16, 32, D),
+        vm(8, 128, **f32), vm(16, 8, 128, **f32),
+        sem((4,)), sem((NSEM,)), sem((NSEM,)),
+    ] + [vm(2, *shape) for shape in halves for _ in range(4)]
     any_ = pl.BlockSpec(memory_space=pl.ANY)
     vmem = pl.BlockSpec(memory_space=pltpu.VMEM)
+    smem = pl.BlockSpec(memory_space=pltpu.SMEM)
     return pl.pallas_call(
         train_kernel,
-        out_shape=(jax.ShapeDtypeStruct((T, D), BF), jax.ShapeDtypeStruct((4, 8, 64, 640), BF),
-                   jax.ShapeDtypeStruct((512, D), BF)),
-        in_specs=[pl.BlockSpec(memory_space=pltpu.SMEM), vmem, vmem, any_, any_, any_, any_],
+        out_shape=(jax.ShapeDtypeStruct((T, D), BF), jax.ShapeDtypeStruct((4, 4, 16, 640), BF),
+                   jax.ShapeDtypeStruct((4, 4, 32, D), BF)),
+        in_specs=[smem, smem, vmem, vmem, any_, any_, any_, any_],
         out_specs=(vmem, vmem, vmem),
         scratch_shapes=scratch,
         compiler_params=pltpu.CompilerParams(collective_id=0, has_side_effects=True, vmem_limit_bytes=VMEM_BYTES),
         name="train",
-    )(lengths, cols, rows, events, in_weight, out_weight, item_table)
+    )(lengths, destinations, hist, neg, events, in_weight, out_weight, item_table)
+
+
+def last_kernel(lay, w, h, e, lay_o, in_o, out_o, tab_o):
+    lay_o[...] = lay[...]
+    rows = jnp.concatenate([w[i, 0] for i in range(4)], 1).astype(F32)
+    in_o[...] = rows[:, :4 * HID]
+    out_o[...] = rows[:, 4 * HID:]
+    item, total = e[...].astype(F32), h[0].reshape(128, D).astype(F32)
+    length = lax.rsqrt(jnp.sum(item * item, -1, keepdims=True) + EPS)
+    item = item * length
+    tab_o[...] = (total - item * jnp.sum(item * total, -1, keepdims=True)) * length
+
+
+def last_call(lay, w, h, item_table):
+    rows = lambda n, m: pl.BlockSpec((n, m), lambda i: (i, 0))
+    return pl.pallas_call(
+        last_kernel,
+        grid=(4,),
+        out_shape=(jax.ShapeDtypeStruct((T, D), BF), jax.ShapeDtypeStruct((64, 4 * HID), F32),
+                   jax.ShapeDtypeStruct((64, HID), F32), jax.ShapeDtypeStruct((512, D), F32)),
+        in_specs=[rows(64, D), pl.BlockSpec((4, 1, 16, 640), lambda i: (0, i, 0, 0)),
+                  pl.BlockSpec((1, 4, 32, D), lambda i: (i, 0, 0, 0)), rows(128, D)],
+        out_specs=(rows(64, D), rows(16, 4 * HID), rows(16, HID), rows(128, D)),
+        name="last",
+    )(lay, w, h, item_table)
 
 
 def body(events, lengths, destinations, history, negatives, in_weight, out_weight, item_table):
-    cands = jnp.concatenate([history[:, None], negatives], 1)
-    cols = jnp.pad(cands, ((0, 0), (0, 124)))
-    rows = jnp.pad(cands.T, ((0, 4), (0, 0)))
-    result, g, h = train_call(lengths, cols, rows, events, in_weight, out_weight, item_table)
-    return finish(result, g, h, lengths, destinations, item_table)
-
-
-def finish(result, g, h, lengths, destinations, item_table):
-    owners = 16
-    s = lax.axis_index("seq")
-    c = s % 2
-    mine = g.transpose(1, 2, 0, 3).reshape(8, 64, 2560)
-    zero = jnp.zeros_like(mine)
-    whole = jnp.stack([jnp.where(c == 0, mine, zero), jnp.where(c == 1, mine, zero)], 1).reshape(1024, 2560)
-    shard = lax.psum_scatter(whole, "seq", scatter_dimension=0, tiled=True)
-    h, shard = lax.psum(h, "grp"), lax.psum(shard, "grp")
-    e = item_table.astype(F32)
-    inv = lax.rsqrt(jnp.sum(e * e, -1, keepdims=True) + EPS)
-    en = e * inv
-    hf = h.astype(F32)
-    table_grad = (hf - en * jnp.sum(en * hf, -1, keepdims=True)) * inv
-    shard = shard.astype(F32)
-    user_lengths, user_dests = lengths[0], destinations[0]
-    starts = jnp.cumsum(user_lengths) - user_lengths
-    chosen = (user_dests[None, :] == jnp.arange(owners)[:, None]).astype(I32)
-    send_length = jnp.sum(chosen * user_lengths[None, :], 1)
-    send_start = jnp.sum(chosen * starts[None, :], 1)
-    slot = jnp.arange(24)
-    filled = slot[None, :] < send_length[:, None]
-    src = jnp.clip(send_start[:, None] + slot[None, :], 0, T - 1)
-    out = jnp.where(filled[..., None], result[src], jnp.zeros((), BF))
-    got = lax.all_to_all(out, "seq", split_axis=0, concat_axis=0, tiled=True)
-    cnt = lax.all_to_all(send_length[:, None], "seq", split_axis=0, concat_axis=0, tiled=True)[:, 0]
-    block_ends = jnp.cumsum(cnt)
-    offsets = block_ends - cnt
-    pos = jnp.arange(T)
-    anchor = jnp.minimum(jnp.sum((block_ends[None, :] <= pos[:, None]).astype(I32), 1), owners - 1)
-    placed = anchor * 24 + pos - offsets[anchor]
-    layer_out = got.reshape(-1, D)[placed]
-    return layer_out, shard[:, :2048], shard[:, 2048:], table_grad
+    result, wsum, hsum = train_call(lengths, destinations, history.reshape(1, T), negatives.T, events,
+                                    in_weight, out_weight, item_table)
+    return last_call(result, wsum, hsum, item_table)
 
 
 def solution(mesh):

time: 330 us -> 156 us (0.47)
  waiting for transfers between devices: 131 us -> 0 us
  Pallas kernels: 114 us -> 154 us
  local copies, waits for them, and re-layouts: 32.4 us -> 0 us
  other arithmetic: 23.6 us -> 0 us
  starting transfers between devices: 14.5 us -> 0 us
  between operations: 14.2 us -> 0.64 us
    psum x1 -> x0, waiting for transfers between devices: 74.1 us -> none  [finish(): h, shard = (lax.psum(h, 'grp'), lax.psum(shard, 'grp'))]
    reduce_scatter x1 -> x0, waiting for transfers between devices: 50 us -> none  [finish(): shard = lax.psum_scatter(whole, 'seq', scatter_dimension=0, tiled=True)]
    pallas_call x1, Pallas kernels: 114 us -> 150 us  [train_call(): pl.pallas_call(train_kernel, out_shape=(jax.ShapeDtypeStruct((T, D), BF),...]
    select_n x5 -> x0, local copies, waits for them, and re-layouts: 18.7 us -> none  [the longest x2 10.8 us: finish(): jnp.where(c == 1, mine, zero)]
    all_to_all x2 -> x0, starting transfers between devices: 14.4 us -> none  [the longest x1 8.04 us: finish(): got = lax.all_to_all(out, 'seq', split_axis=0, concat_axis=0, tiled=True)]
    gather x5 -> x0, other arithmetic: 10.3 us -> none  [the longest x3 10.3 us: finish(): placed = anchor * 24 + pos - offsets[anchor]]
    all_to_all x2 -> x0, waiting for transfers between devices: 7.16 us -> none  [the longest x1 7.16 us: finish(): got = lax.all_to_all(out, 'seq', split_axis=0, concat_axis=0, tiled=True)]
    select_n x4 -> x0, other arithmetic: 4.79 us -> none  [the longest x1 3.69 us: finish(): jnp.where(c == 0, mine, zero)]
  transfers between devices with their start and end apart: 4 -> 0, of which waited for: 3 -> 0; matrix products, arithmetic and copies ran while one was open for 6% -> 0% of each run, Pallas kernels for 0% -> 0%
where the time goes in v3:
time: 156 us; the launch traced here: 155 us
  Pallas kernels  154 us (99%)
    pallas_call x1, Pallas kernels, train_call(): pl.pallas_call(train_kernel, out_shape=(jax.ShapeDtypeStruct((T, D), BF),...  150 us
    pallas_call x1, Pallas kernels, last_call(): pl.pallas_call(last_kernel, grid=(4,), out_shape=(jax.ShapeDtypeStruct((T...  4.44 us

profile of v3, /device:TPU:32, one launch (start us, length us, event | category | flops | bytes accessed | tf_op | source)
XLA Modules:
  0.0 155.1 jit_solution(5152524172612702735)
XLA Ops:
  0.6 150.0 %train.1 = (bf16[256,1024]{1,0:T(8,128)(2,1)}, bf16[4,4,16,640]{3,2,1,0:T(8,128)(2,1)}, bf16[4,4,32,1024]{3,2,1,0:T(8,128)(2,1)}) custom-call(s32[1,16]{1,0:T(1,128)} %len_s.1, s32[1,16]{1,0:T(1,128)} %dst_s.1, s32[1,256]{1,0:T(1,128)} %bitcast.3, s32[3,256]{1,0:T(4,128)} %bitcast.2, bf16[256,1024]{1,0:T(8,128)(2,1)} %ev_h.1, bf16[1024,2048]{1,0:T(8,128)(2,1)} %win_h.1, ...), custom_call_target="tpu_custom_call" | custom-call | tf_op jit(solution)/shard_map/train/pallas_call | solution.py:698
  150.7 4.4 %last.1 = (bf16[256,1024]{1,0:T(8,128)(2,1)}, f32[64,2048]{1,0:T(8,128)}, f32[64,512]{1,0:T(8,128)}, f32[512,1024]{1,0:T(8,128)}) custom-call(bf16[256,1024]{1,0:T(8,128)(2,1)} %get-tuple-element.7.lay, bf16[4,4,16,640]{3,2,1,0:T(8,128)(2,1)} %get-tuple-element.8.w, bf16[4,4,32,1024]{3,2,1,0:T(8,128)(2,1)} %get-tuple-element.9.h, bf16[512,1024]{1,0:T(8,128)(2,1)} %e.1), custom_call_target="tpu_custom_call" | custom-call | tf_op jit(solution)/shard_map/last/pallas_call | solution.py:723

commit v4 on v3

v4 whole, which is shorter than its diff:
```python
import jax
import jax.numpy as jnp
from jax import lax
from jax.experimental import pallas as pl
from jax.experimental.pallas import tpu as pltpu
from jax.sharding import PartitionSpec as P

F32, BF, I32 = jnp.float32, jnp.bfloat16, jnp.int32
MESH = pl.DeviceIdType.MESH
T, D, HID = 256, 1024, 512
HEADS, HEAD_DIM, NCAND = 4, 128, 4
EPS = 1e-5
TEMP = 0.05
SCALE = HEAD_DIM ** -0.5
VMEM_BYTES = 67_000_000


def rep(n, body, unroll=1):
    def step(i, carry):
        body(i)
        return carry

    lax.fori_loop(0, n, step, 0, unroll=unroll)


def ds(i, size):
    return pl.ds(pl.multiple_of(i * size, size), size)


def iota(shape, dim):
    return lax.broadcasted_iota(I32, shape, dim)


def mm(a, b):
    return jnp.dot(a, b, preferred_element_type=F32)


def mm_t(a, b):
    return lax.dot_general(a, b, (((1,), (1,)), ((), ())), preferred_element_type=F32)


def sigmoid(v):
    return 1.0 / (1.0 + jnp.exp(-v))


class Where:
    def __init__(self):
        self.g, self.s = lax.axis_index("grp"), lax.axis_index("seq")
        self.px, self.py = self.g // 4, self.g % 4
        self.z, self.c = self.s // 2, self.s % 2

    def at(self, grp=None, seq=None):
        return {"grp": self.g if grp is None else grp, "seq": self.s if seq is None else seq}

    def zoff(self, k):
        return self.at(seq=((self.z + k) % 8) * 2 + self.c)

    def mate(self):
        return self.at(seq=self.z * 2 + 1 - self.c)

    def xoff(self, k):
        return self.at(grp=((self.px + k) % 4) * 4 + self.py)

    def yoff(self, k):
        return self.at(grp=self.px * 4 + (self.py + k) % 4)


class Links:
    def __init__(self, send, recv):
        self.send, self.recv, self.n, self.sent = send, recv, 0, []

    def describe(self, src, dst, dev):
        return pltpu.make_async_remote_copy(
            src_ref=src, dst_ref=dst, send_sem=self.send.at[self.n], recv_sem=self.recv.at[self.n],
            device_id=dev, device_id_type=MESH)

    def go(self, src, dst, dev):
        return self.bundle(dst, (src, dst, dev))

    def bundle(self, whole, *copies):
        for copy in copies:
            self.describe(*copy).start()
        wait = self.describe(whole, whole, copies[0][2])
        self.n += 1
        self.sent.append(wait)
        return wait

    def drain(self):
        for copy in self.sent:
            copy.wait_send()


class Ring:
    def __init__(self, net, off, i, src, bufs, out):
        self.net, self.off, self.i, self.src, self.out = net, off, i, src, out
        self.t, self.u, self.v, self.r = bufs

    def start(self):
        far, right, left = (self.i + 2) % 4, (self.i + 1) % 4, (self.i + 3) % 4
        off, src, t, u = self.off, self.src, self.t, self.u
        self.ct = self.net.bundle(t, (src(far, 0), t.at[0], off(1)), (src(far, 1), t.at[1], off(-1)))
        self.cu = self.net.bundle(u, (src(left, 0), u.at[0], off(-1)), (src(right, 1), u.at[1], off(1)))

    def relay(self):
        self.ct.wait_recv()
        for k, j in ((0, (self.i + 1) % 4), (1, (self.i + 3) % 4)):
            self.v[k] = (self.t[k].astype(F32) + self.src(j, k)[...].astype(F32)).astype(BF)
        v, r, off = self.v, self.r, self.off
        self.cr = self.net.bundle(r, (v.at[0], r.at[0], off(1)), (v.at[1], r.at[1], off(-1)))

    def finish(self):
        self.cr.wait_recv()
        self.cu.wait_recv()
        for k in range(2):
            total = self.src(self.i, k)[...].astype(F32) + self.r[k].astype(F32) + self.u[k].astype(F32)
            self.out(k)[...] = total.astype(BF)


def call_out(devices):
    barrier = pltpu.get_barrier_semaphore()
    for dev in devices:
        pl.semaphore_signal(barrier, inc=1, device_id=dev, device_id_type=MESH)
    return lambda: pl.semaphore_wait(barrier, len(devices))


NSEM = 88


def train_kernel(len_s, dst_s, hist_v, neg_v, ev_h, win_h, wout_h, tab_h, lay_o, w_o, h_o, *refs):
    (x_v, win, wout, traw, tab, nin, slope, proj, attn, dsl, att, normed, inv, gated, gatedm,
     res, rlen, yall, ymate, ids_f, cand, rall, gall, gsend, lacc, lsum, lrec, gcol, picks, found,
     wown, wsend, wrec, upb, gg, gatt, gpre, gprem, ninT, ninTm, upT, upTm, hsend, hrec, mask_v, lout,
     g_v, h_v, a1, b1, ha1, hb1, piece, zbuf, wpiece, wall, hall, slots_s, slots_r, csend, cbuf,
     lsem, ssem, rsem) = refs[:len(refs) - 32]
    bufs = refs[len(refs) - 32:]
    (ga_b, gb_b, ha_b, hb_b, ga2_b, gb2_b, ha2_b, hb2_b) = [bufs[4 * i:4 * i + 4] for i in range(8)]
    w = Where()
    net = Links(ssem, rsem)
    s, z, c, px, py, g = w.s, w.z, w.c, w.px, w.py, w.g
    plane = [(i, j) for i in range(4) for j in range(4) if (i, j) != (0, 0)]

    def peer(i, j):
        return w.at(grp=((px + i) % 4) * 4 + (py + j) % 4)

    loads = [pltpu.make_async_copy(a, b, lsem.at[i]) for i, (a, b) in enumerate(
        ((tab_h, traw), (ev_h, x_v), (win_h, win), (wout_h, wout)))]
    for copy in loads:
        copy.start()
    for k in range(16):
        slots_r[k, pl.ds(24, 8)] = jnp.zeros((8, D), BF)
    everyone = call_out([w.at(seq=(s + k) % 16) for k in range(1, 16)] + [peer(i, j) for i, j in plane])

    ids_f[...] = jnp.full((128, T), -1.0, F32)
    ids_f[pl.ds(0, 1)] = hist_v[...].astype(F32)
    ids_f[pl.ds(1, 3)] = neg_v[...].astype(F32)
    rall[0] = ids_f[pl.ds(0, 8)].astype(I32)
    cand[pl.ds(0, T)] = ids_f[...].T.astype(I32)

    loads[0].wait()

    def norm_rows(i):
        j = (g + i) % 16
        rows = traw[ds(j, 32)].astype(F32)
        length = lax.rsqrt(jnp.sum(rows * rows, -1, keepdims=True) + EPS)
        tab[0, j // 4, j % 4] = (rows * length).astype(BF)

    norm_rows(0)
    everyone()
    low, high = pl.ds(0, 512), pl.ds(512, 512)
    mine_at = lambda dz, cols: tab.at[dz, px, py, :, cols]
    slice_in = {(1, 7): net.bundle(
        tab.at[0, 0, pl.ds(0, 2), :, high],
        *[(mine_at(0, high), mine_at(8 - k, high), w.zoff(k)) for k in (1, 7)])}
    for a, b in ((2, 6), (3, 5)):
        slice_in[a, b] = net.bundle(
            tab.at[0, 0, pl.ds(0, 2)],
            *[(tab.at[0, px, py], tab.at[8 - k, px, py], w.zoff(k)) for k in (a, b)])
    rep(15, lambda i: norm_rows(i + 1))
    cp_cand = net.go(cand.at[pl.ds(0, T)], cand.at[pl.ds(T, T)], w.mate())

    pieces = {7: (tab.at[7], 512, 512, "y"), 1: (tab.at[1], 512, 512, "x"),
              6: (tab.at[6], 0, 1024, "y"), 2: (tab.at[2], 0, 1024, "x"),
              5: (tab.at[5], 0, 1024, "y"), 3: (tab.at[3], 0, 1024, "x"),
              "4x": (tab.at[4], 0, 512, "x"), "4y": (tab.at[4], 512, 512, "y"),
              "hx": (hall, 0, 512, "x"), "hy": (hall, 512, 512, "y")}
    flying = {}

    def one(piece, kx, ky, c0, nc):
        return piece[0].at[(px + kx) % 4, (py + ky) % 4, :, pl.ds(c0, nc)]

    def many(piece, k, c0, nc):
        if piece[3] == "x":
            return piece[0].at[:, (py + k) % 4, :, pl.ds(c0, nc)]
        return piece[0].at[(px + k) % 4, :, :, pl.ds(c0, nc)]

    def pair(name, whole, right, left, off):
        flying[name] = net.bundle(whole, (right, right, off(1)), (left, left, off(-1)))

    def first_send(name):
        p = pieces[name]
        own = one(p, 0, 0, p[1], p[2])
        pair(name, p[0].at[0, pl.ds(0, 2), :, pl.ds(p[1], p[2])], own, own, w.xoff if p[3] == "x" else w.yoff)

    def first_forward(name):
        p = pieces[name]
        half = p[2] // 2
        at = (lambda k, c0: one(p, k, 0, c0, half)) if p[3] == "x" else (lambda k, c0: one(p, 0, k, c0, half))
        flying[name].wait_recv()
        pair(name, one(p, 0, 0, p[1], p[2]), at(-1, p[1]), at(1, p[1] + half), w.xoff if p[3] == "x" else w.yoff)

    def second_send(name):
        p = pieces[name]
        flying[name].wait_recv()
        own = many(p, 0, p[1], p[2])
        pair(name, p[0].at[pl.ds(0, 2), :, :, pl.ds(p[1], p[2])], own, own, w.yoff if p[3] == "x" else w.xoff)

    def second_forward(name):
        p = pieces[name]
        half = p[2] // 2
        flying[name].wait_recv()
        pair(name, many(p, 0, p[1], p[2]), many(p, -1, p[1], half), many(p, 1, p[1] + half, half),
             w.yoff if p[3] == "x" else w.xoff)

    def step(stage, *names):
        for name in names:
            stage(name)

    def slices(a, b):
        slice_in[a, b].wait_recv()

    ends = []
    for j in range(16):
        ends.append(len_s[0, j] + (ends[-1] if ends else 0))
    tc, tr = iota((T, 128), 0), iota((8, T), 1)
    uid_c, uid_r = jnp.zeros((T, 128), I32), jnp.zeros((8, T), I32)
    for end in ends:
        uid_c = uid_c + (tc >= end).astype(I32)
        uid_r = uid_r + (tr >= end).astype(I32)
    same = (uid_c[:, :1] == uid_r[:1, :]) & (iota((T, T), 1) <= iota((T, T), 0))
    mask_v[...] = same.astype(F32)

    loads[1].wait()

    def norm_in(i):
        v = x_v[ds(i, 32)].astype(F32)
        v = v - jnp.mean(v, -1, keepdims=True)
        nin[ds(i, 32)] = (v * lax.rsqrt(jnp.mean(v * v, -1, keepdims=True) + EPS)).astype(BF)

    rep(8, norm_in, 2)
    loads[2].wait()
    loads[3].wait()

    def project(i):
        pre = mm(nin[...], win[:, ds(i, 256)])
        sg = sigmoid(pre)
        proj[:, ds(i, 256)] = (pre * sg).astype(BF)
        slope[:, ds(i, 256)] = sg * (1.0 + pre * (1.0 - sg))

    rep(2, project)
    slices(1, 7)
    step(first_send, 1, 7)
    rep(3, lambda i: project(i + 2))
    slices(2, 6)
    step(first_send, 2, 6)
    rep(3, lambda i: project(i + 5))
    step(first_forward, 1, 7)

    def flip_in(i):
        block = nin[:, ds(i, 128)].astype(F32).T
        ninT[i] = block.astype(BF).reshape(2, 64, T)

    def attend(h):
        col = lambda part: pl.ds(pl.multiple_of(part * HID + h * 128, 128), 128)
        scores = mm_t(proj[:, col(2)], proj[:, col(3)]) * SCALE
        sg = sigmoid(scores)
        mask = mask_v[...]
        weight = (scores * sg * mask).astype(BF)
        attn[h] = weight
        dsl[h] = sg * (1.0 + scores * (1.0 - sg)) * SCALE * mask
        att[:, ds(h, 128)] = mm(weight, proj[:, col(1)])

    rep(2, attend)
    slices(3, 5)
    slice_in["4r", "4l"] = net.bundle(
        tab.at[0, 0, 0], (mine_at(5, low), mine_at(4, low), w.zoff(1)), (mine_at(3, high), mine_at(4, high), w.zoff(-1)))
    direct = net.bundle(
        tab.at[pl.ds(0, 2), :, :, :, low], (tab.at[0, :, :, :, low], tab.at[7, :, :, :, low], w.zoff(1)),
        (tab.at[0, :, :, :, low], tab.at[1, :, :, :, low], w.zoff(-1)))
    step(first_send, 3, 5)
    step(first_forward, 2, 6)
    rep(2, lambda h: attend(h + 2))
    step(second_send, 1, 7)

    def norm_att(i):
        v = att[ds(i, 32)]
        v = v - jnp.mean(v, -1, keepdims=True)
        f = lax.rsqrt(jnp.mean(v * v, -1, keepdims=True) + EPS)
        n = v * f
        normed[ds(i, 32)] = n
        inv[ds(i, 32)] = jnp.broadcast_to(f, (32, 128))
        gated[ds(i, 32)] = (n * proj[ds(i, 32), pl.ds(0, HID)].astype(F32)).astype(BF)

    rep(8, norm_att, 2)
    slices("4r", "4l")
    step(first_send, "4x", "4y")
    step(first_forward, 3, 5)
    step(second_send, 2, 6)

    def result(i):
        res[:, ds(i, 256)] = x_v[:, ds(i, 256)].astype(F32) + mm_t(gated[...], wout[ds(i, 256)])

    rep(4, result)

    def norm_out(i):
        v = res[ds(i, 32)]
        f = lax.rsqrt(jnp.sum(v * v, -1, keepdims=True) + EPS)
        rlen[ds(i, 32)] = jnp.broadcast_to(f, (32, 128))
        yall[0, ds(i, 32)] = (v * f).astype(BF)
        lout[ds(i, 32)] = v.astype(BF)

    rep(8, norm_out, 2)
    cp_y = net.go(yall.at[0], ymate, w.mate())
    two_y = yall.at[pl.ds(0, 2)]
    hop = net.bundle(two_y, (yall.at[0], yall.at[7], w.zoff(1)), (yall.at[0], yall.at[1], w.zoff(-1)))
    cp_rows = net.bundle(rall.at[pl.ds(0, 7)], *[(rall.at[0], rall.at[8 - k], w.zoff(k)) for k in range(1, 8)])
    step(first_forward, "4x", "4y")
    rep(8, flip_in)
    step(second_forward, 1, 7)
    step(second_send, 3, 5)
    cp_nin = net.go(ninT.at[:, 1 - c], ninTm, w.mate())
    cp_gated = net.go(gated, gatedm, w.mate())

    lsum[...] = jnp.zeros_like(lsum)
    lanes = iota((256, 128), 1).astype(F32)
    cp_cand.wait_recv()

    def owner(dz):
        return ((z + dz) % 8) * 2 + c

    def aim(dz):
        def part(i):
            who = cand[ds(i, 256)]
            spot = jnp.where((who >> 9) == owner(dz), (who & 511) + 1, 0).astype(F32)
            spot = jnp.broadcast_to(jnp.sum(spot, -1, keepdims=True) - 1.0, (256, 128))
            for q in range(4):
                picks[ds(i, 256), pl.ds(q * 128, 128)] = jnp.where(spot == lanes + 128.0 * q, 1.0, 0.0).astype(BF)
            lacc[ds(i, 256)] = jnp.zeros((256, 128), F32)

        rep(2, part)

    def score(dz):
        def part(i):
            rows = mm(picks[...], tab[dz, :, :, :, ds(i, 256)].reshape(512, 256))
            found[dz, :, ds(i, 256)] = rows.astype(BF)
            for first, y in ((0, yall[0, :, ds(i, 256)]), (T, ymate[:, ds(i, 256)])):
                got = rows[first:first + T] * y.astype(F32)
                lacc[pl.ds(first, T)] += got[:, :128] + got[:, 128:]

        rep(4, part)

        def close(i):
            value = jnp.sum(lacc[ds(i, 256)], -1, keepdims=True)
            lsum[ds(i, 256)] += jnp.where((cand[ds(i, 256)] >> 9) == owner(dz), value, 0.0)

        rep(2, close)

    def settle(*names):
        for name in names:
            flying[name].wait_recv()

    aim(0)
    cp_y.wait_recv()
    score(0)
    step(second_send, "4x", "4y")
    aim(1)
    direct.wait_recv()
    settle(1, 7)
    step(second_forward, 2, 6)
    score(1)
    aim(7)
    score(7)
    hop.wait_recv()
    hop = net.bundle(two_y, (yall.at[7], yall.at[6], w.zoff(1)), (yall.at[1], yall.at[2], w.zoff(-1)))
    aim(2)
    settle(2, 6)
    step(second_forward, 3, 5)
    score(2)
    aim(6)
    score(6)
    step(second_forward, "4x", "4y")
    aim(3)
    settle(3, 5)
    score(3)
    aim(5)
    score(5)
    aim(4)
    settle("4x", "4y")
    score(4)
    lane = iota((2 * T, 128), 1)
    cp_l = net.go(lsum, lrec, w.mate())
    hop.wait_recv()
    hop = net.bundle(two_y, (yall.at[6], yall.at[5], w.zoff(1)), (yall.at[2], yall.at[3], w.zoff(-1)))
    cp_l.wait_recv()
    lrec_v = lrec[...]
    logits = (lsum[...] + jnp.concatenate([lrec_v[T:], lrec_v[:T]], 0)) / TEMP
    live = lane < NCAND
    ex = jnp.where(live, jnp.exp(jnp.where(live, logits, 0.0)), 0.0)
    soft = ex / jnp.sum(ex, -1, keepdims=True)
    gcol[...] = jnp.where(live, soft - (lane == 0).astype(F32), 0.0) / TEMP

    gsend[...] = gcol[pl.ds(0, T)].T[:8]
    gall[0] = gsend[...]
    cp_g = net.bundle(gall.at[pl.ds(0, 7)], *[(gsend, gall.at[8 - k], w.zoff(k)) for k in range(1, 8)])

    def blend(at):
        who, how = cand[at] >> 9, gcol[at]
        total = jnp.zeros((32, D), F32)
        for dz in range(8):
            much = jnp.sum(jnp.where(who == owner(dz), how, 0.0), -1, keepdims=True)
            total = total + much * found[dz, at].astype(F32)
        return total

    def gather_mate(i):
        wsend[ds(i, 32)] = blend(ds(i + 8, 32)).astype(BF)

    rep(8, gather_mate)
    cp_w = net.go(wsend, wrec, w.mate())

    def gather_own(i):
        wown[ds(i, 32)] = blend(ds(i, 32))

    rep(8, gather_own)
    cp_w.wait_recv()

    def upstream(i):
        f = rlen[ds(i, 32)][:, :1]
        yn = res[ds(i, 32)] * f
        v = wown[ds(i, 32)] + wrec[ds(i, 32)].astype(F32)
        up = (v - yn * jnp.sum(yn * v, -1, keepdims=True)) * f
        upb[ds(i, 32)] = up.astype(BF)

    rep(8, upstream, 2)

    gg[...] = mm(upb[...], wout[...])

    def back_norm(i):
        n, v = normed[ds(i, 32)], gg[ds(i, 32)]
        gpre[ds(i, 32), pl.ds(0, HID)] = (v * n * slope[ds(i, 32), pl.ds(0, HID)]).astype(BF)
        v = v * proj[ds(i, 32), pl.ds(0, HID)].astype(F32)
        v = v - jnp.mean(v, -1, keepdims=True) - n * jnp.mean(v * n, -1, keepdims=True)
        gatt[ds(i, 32)] = (inv[ds(i, 32)][:, :1] * v).astype(BF)

    rep(8, back_norm, 2)

    def flip_up(i):
        block = upb[:, ds(i, 128)].astype(F32).T
        upT[i] = block.astype(BF).reshape(2, 64, T)

    rep(8, flip_up)
    cp_up = net.go(upT.at[:, 1 - c], upTm, w.mate())

    def back_attend(h):
        col = lambda part: pl.ds(pl.multiple_of(part * HID + h * 128, 128), 128)
        da = gatt[:, ds(h, 128)]
        ds_ = (mm_t(da, proj[:, col(1)]) * dsl[h])
        gv = mm(attn[h].astype(F32).T.astype(BF), da)
        gq = mm(ds_.astype(BF), proj[:, col(3)])
        gk = mm(ds_.T.astype(BF), proj[:, col(2)])
        gpre[:, col(1)] = (gv * slope[:, col(1)]).astype(BF)
        gpre[:, col(2)] = (gq * slope[:, col(2)]).astype(BF)
        gpre[:, col(3)] = (gk * slope[:, col(3)]).astype(BF)

    rep(4, back_attend)
    cp_pre = net.go(gpre, gprem, w.mate())
    hop.wait_recv()
    a, b = pl.ds(0, 512), pl.ds(512, 512)
    hop = net.bundle(yall.at[0], (yall.at[5, :, a], yall.at[4, :, a], w.zoff(1)),
                     (yall.at[3, :, b], yall.at[4, :, b], w.zoff(-1)))

    def store_g(i, first, block):
        for b in range(block.shape[1] // 128):
            n = first + b
            g_v[n // 5, pl.ds(i * 4, 4), :, :, pl.ds((n % 5) * 128, 128)] = (
                block[:, b * 128:(b + 1) * 128].astype(BF).reshape(4, 4, 16, 128))

    cp_gated.wait_recv()
    cp_up.wait_recv()

    def grad_out(i):
        a = upT[pl.ds(i * 4, 4), c].reshape(T, T)
        b = upTm[pl.ds(i * 4, 4)].reshape(T, T)
        store_g(i, 16, mm(a, gated[...]) + mm(b, gatedm[...]))

    rep(2, grad_out)
    cp_nin.wait_recv()
    cp_pre.wait_recv()

    def grad_in(i):
        a = ninT[pl.ds(i * 4, 4), c].reshape(T, T)
        b = ninTm[pl.ds(i * 4, 4)].reshape(T, T)
        for n in range(4):
            cols = pl.ds(n * 512, 512)
            store_g(i, n * 4, mm(a, gpre[:, cols]) + mm(b, gprem[:, cols]))

    rep(2, grad_in)

    two = lambda k: pl.ds(2 * k, 2)
    cut = lambda k: pl.ds(256 * k, 256)
    hicut = lambda k: pl.ds(512 + 256 * k, 256)
    ga = Ring(net, w.xoff, px, lambda j, k: g_v.at[j, two(k)], ga_b, lambda k: a1.at[two(k)])
    gb = Ring(net, w.yoff, py, lambda j, k: g_v.at[:, pl.ds(4 + 2 * k, 2), j], gb_b, lambda k: b1.at[:, two(k)])
    ha = Ring(net, w.xoff, px, lambda j, k: h_v.at[j, :, :, cut(k)], ha_b, lambda k: ha1.at[:, :, cut(k)])
    hb = Ring(net, w.yoff, py, lambda j, k: h_v.at[:, j, :, hicut(k)], hb_b, lambda k: hb1.at[:, :, cut(k)])
    ga2 = Ring(net, w.yoff, py, lambda j, k: a1.at[two(k), j], ga2_b, lambda k: piece.at[two(k)])
    gb2 = Ring(net, w.xoff, px, lambda j, k: b1.at[j, two(k)], gb2_b, lambda k: piece.at[pl.ds(4 + 2 * k, 2)])
    mine = hall.at[px, py]
    ha2 = Ring(net, w.yoff, py, lambda j, k: ha1.at[j, :, cut(k)], ha2_b, lambda k: mine.at[:, cut(k)])
    hb2 = Ring(net, w.xoff, px, lambda j, k: hb1.at[j, :, cut(k)], hb2_b, lambda k: mine.at[:, hicut(k)])
    ga.start()
    gb.start()

    lane8 = iota((8, 128), 1)
    counts = jnp.zeros((8, 128), F32)
    place = jnp.zeros((8, T), I32)
    start = 0
    for j in range(16):
        n, d = len_s[0, j], dst_s[0, j]
        counts = counts + jnp.where(lane8 == d, n, 0).astype(F32)
        place = jnp.where((tr >= start) & (tr < start + n), d * 32 + tr - start, place)
        start = start + n
    csend[...] = counts
    cp_count = net.bundle(cbuf.at[pl.ds(0, 15)], *[(csend, cbuf.at[s], w.at(seq=(s + k) % 16)) for k in range(1, 16)])
    cbuf[s] = csend[...]

    def fill(i):
        pick = jnp.where(iota((128, T), 0) + i * 128 == place[:1, :], 1.0, 0.0).astype(BF)
        slots_s[pl.ds(i * 4, 4)] = mm(pick, lout[...]).astype(BF).reshape(4, 32, D)

    rep(4, fill)
    used = pl.ds(0, 24)
    cp_slot = net.bundle(
        slots_r.at[pl.ds(0, 15), used],
        *[(slots_s.at[(s + k) % 16, used], slots_r.at[s, used], w.at(seq=(s + k) % 16)) for k in range(1, 16)])
    slots_r[s, used] = slots_s[s, used]

    cp_rows.wait_recv()
    cp_g.wait_recv()

    def spread_t(dz):
        who, how = rall[dz], gall[dz]
        for o in range(2):
            hit = (who >> 9) == z * 2 + o
            spot = jnp.sum(jnp.where(hit, (who & 511) + 1, 0).astype(F32), 0, keepdims=True) - 1.0
            much = jnp.sum(jnp.where(hit, how, 0.0), 0, keepdims=True)
            for j in range(4):
                line = (iota((128, T), 0) + j * 128).astype(F32)
                found[dz // 4 + 2 * o, pl.ds(j * 128, 128), ds(dz % 4, T)] = jnp.where(line == spot, much, 0.0).astype(BF)

    rep(8, spread_t)

    def h_part(o, i):
        y = [yall[pl.ds(4 * k, 4), :, ds(i, 256)].reshape(4 * T, 256) for k in range(2)]
        return mm(found[2 * o], y[0]) + mm(found[2 * o + 1], y[1])

    def h_mate(i):
        hsend[:, ds(i, 256)] = h_part(1 - c, i).astype(BF)

    hop.wait_recv()
    rep(4, h_mate)
    cp_h = net.go(hsend, hrec, w.mate())
    ga.relay()
    gb.relay()

    def h_own(i):
        part = h_part(c, i)
        wown[:, ds(i, 256)] = part[:T]
        res[:, ds(i, 256)] = part[T:]

    rep(4, h_own)
    cp_h.wait_recv()
    for part, src in ((0, wown), (1, res)):
        for i in range(8):
            total = src[pl.ds(i * 32, 32)] + hrec[pl.ds(part * T + i * 32, 32)].astype(F32)
            h_v[part * 2 + i // 4, i % 4] = total.astype(BF)
    ha.start()
    hb.start()

    ga.finish()
    ga2.start()
    gb.finish()
    gb2.start()
    ha.relay()
    hb.relay()
    ga2.relay()
    gb2.relay()
    ha.finish()
    ha2.start()
    hb.finish()
    hb2.start()
    ga2.finish()
    gb2.finish()
    cp_z = net.bundle(zbuf.at[pl.ds(0, 7)], *[(piece.at[(z + k) % 8], zbuf.at[k], w.zoff(k)) for k in range(1, 8)])
    ha2.relay()
    hb2.relay()
    ha2.finish()
    first_send("hx")
    hb2.finish()
    first_send("hy")
    total = piece[z].astype(F32)
    cp_z.wait_recv()
    for k in range(1, 8):
        total = total + zbuf[k].astype(F32)
    wpiece[...] = total.astype(BF)
    cp_sum = net.bundle(wall.at[pl.ds(0, 15)], *[(wpiece, wall.at[g], peer(i, j)) for i, j in plane])
    wall[g] = wpiece[...]
    step(first_forward, "hx", "hy")
    step(second_send, "hx", "hy")

    cp_count.wait_recv()
    cp_slot.wait_recv()
    cnt = jnp.sum(jnp.where(iota((16, 128), 1) == s, cbuf[:, 0, :], 0.0), -1, keepdims=True)
    row, col16 = iota((16, 512), 0), iota((16, 512), 1)
    slot = col16 >> 5
    before = jnp.sum(jnp.where(row < slot, cnt, 0.0), 0, keepdims=True)
    here = jnp.sum(jnp.where(row == slot, cnt, 0.0), 0, keepdims=True)
    inside = (col16[:1] & 31).astype(F32)
    goal = jnp.where(inside < here, before + inside, -1.0)
    chosen = jnp.where(iota((T, 512), 0).astype(F32) == goal, 1.0, 0.0).astype(BF)

    def land(i):
        lay_o[:, ds(i, 256)] = mm(chosen, slots_r[:, :, ds(i, 256)].reshape(512, 256)).astype(BF)

    rep(4, land)
    step(second_forward, "hx", "hy")
    cp_sum.wait_recv()
    w_o[...] = wall[...]
    settle("hx", "hy")
    h_o[...] = hall[...]
    assert net.n == NSEM, net.n
    net.drain()


def train_call(lengths, destinations, hist, neg, events, in_weight, out_weight, item_table):
    vm = lambda *shape, dtype=BF: pltpu.VMEM(shape, dtype)
    f32 = dict(dtype=F32)
    halves = [(2, 4, 16, 640), (4, 2, 16, 640), (4, 32, 256), (4, 32, 256), (2, 16, 640), (2, 16, 640), (32, 256), (32, 256)]
    sem = pltpu.SemaphoreType.DMA
    scratch = [
        vm(T, D), vm(D, 4 * HID), vm(D, HID), vm(512, D), vm(8, 4, 4, 32, D), vm(T, D),
        vm(T, 4 * HID, **f32), vm(T, 4 * HID), vm(HEADS, T, T), vm(HEADS, T, T, **f32),
        vm(T, HID, **f32), vm(T, HID, **f32), vm(T, 128, **f32), vm(T, HID), vm(T, HID),
        vm(T, D, **f32), vm(T, 128, **f32), vm(8, T, D), vm(T, D), vm(128, T, **f32), vm(2 * T, 128, dtype=I32),
        vm(8, 8, T, dtype=I32), vm(8, 8, T, **f32), vm(8, T, **f32), vm(2 * T, 128, **f32),
        vm(2 * T, 128, **f32), vm(2 * T, 128, **f32), vm(2 * T, 128, **f32), vm(2 * T, 512),
        vm(8, 2 * T, D), vm(T, D, **f32), vm(T, D), vm(T, D), vm(T, D),
        vm(T, HID, **f32), vm(T, HID), vm(T, 4 * HID), vm(T, 4 * HID), vm(8, 2, 64, T), vm(8, 64, T),
        vm(8, 2, 64, T), vm(8, 64, T), vm(512, D), vm(512, D), vm(T, T, **f32), vm(T, D),
        vm(4, 8, 4, 16, 640), vm(4, 4, 32, D),
        vm(4, 4, 16, 640), vm(4, 4, 16, 640), vm(4, 32, 512), vm(4, 32, 512), vm(8, 16, 640), vm(8, 16, 640),
        vm(16, 640), vm(16, 16, 640), vm(4, 4, 32, D), vm(16, 32, D), vm(16, 32, D),
        vm(8, 128, **f32), vm(16, 8, 128, **f32),
        sem((4,)), sem((NSEM,)), sem((NSEM,)),
    ] + [vm(2, *shape) for shape in halves for _ in range(4)]
    any_ = pl.BlockSpec(memory_space=pl.ANY)
    vmem = pl.BlockSpec(memory_space=pltpu.VMEM)
    smem = pl.BlockSpec(memory_space=pltpu.SMEM)
    return pl.pallas_call(
        train_kernel,
        out_shape=(jax.ShapeDtypeStruct((T, D), BF), jax.ShapeDtypeStruct((16, 16, 640), BF),
                   jax.ShapeDtypeStruct((4, 4, 32, D), BF)),
        in_specs=[smem, smem, vmem, vmem, any_, any_, any_, any_],
        out_specs=(vmem, vmem, vmem),
        scratch_shapes=scratch,
        compiler_params=pltpu.CompilerParams(collective_id=0, has_side_effects=True, vmem_limit_bytes=VMEM_BYTES),
        name="train",
    )(lengths, destinations, hist, neg, events, in_weight, out_weight, item_table)


def last_kernel(lay, w, h, e, lay_o, in_o, out_o, tab_o):
    lay_o[...] = lay[...]
    rows = jnp.concatenate([w[i, 0] for i in range(4)], 1).astype(F32)
    in_o[...] = rows[:, :4 * HID]
    out_o[...] = rows[:, 4 * HID:]
    item, total = e[...].astype(F32), h[0].reshape(128, D).astype(F32)
    length = lax.rsqrt(jnp.sum(item * item, -1, keepdims=True) + EPS)
    item = item * length
    tab_o[...] = (total - item * jnp.sum(item * total, -1, keepdims=True)) * length


def last_call(lay, w, h, item_table):
    rows = lambda n, m: pl.BlockSpec((n, m), lambda i: (i, 0))
    return pl.pallas_call(
        last_kernel,
        grid=(4,),
        out_shape=(jax.ShapeDtypeStruct((T, D), BF), jax.ShapeDtypeStruct((64, 4 * HID), F32),
                   jax.ShapeDtypeStruct((64, HID), F32), jax.ShapeDtypeStruct((512, D), F32)),
        in_specs=[rows(64, D), pl.BlockSpec((4, 1, 16, 640), lambda i: (0, i, 0, 0)),
                  pl.BlockSpec((1, 4, 32, D), lambda i: (i, 0, 0, 0)), rows(128, D)],
        out_specs=(rows(64, D), rows(16, 4 * HID), rows(16, HID), rows(128, D)),
        name="last",
    )(lay, w, h, item_table)


def body(events, lengths, destinations, history, negatives, in_weight, out_weight, item_table):
    result, wsum, hsum = train_call(lengths, destinations, history.reshape(1, T), negatives.T, events,
                                    in_weight, out_weight, item_table)
    return last_call(result, wsum.reshape(4, 4, 16, 640), hsum, item_table)


def solution(mesh):
    return jax.shard_map(
        body,
        mesh=mesh,
        in_specs=(
            P(("grp", "seq"), None),
            P(("grp", "seq"), None),
            P(("grp", "seq"), None),
            P(("grp", "seq")),
            P(("grp", "seq"), None),
            P(),
            P(),
            P("seq", None),
        ),
        out_specs=(P(("grp", "seq"), None), P("seq", None), P("seq", None), P("seq", None)),
        check_vma=False,
    )
```

time: 156 us -> 134 us (0.86)
  Pallas kernels: 154 us -> 133 us
    pallas_call x1, Pallas kernels: 150 us -> 129 us  [train_call(): pl.pallas_call(train_kernel, out_shape=(jax.ShapeDtypeStruct((T, D), BF),...]
where the time goes in v4:
time: 134 us
  Pallas kernels  133 us (99%)
    pallas_call x1, Pallas kernels, train_call(): pl.pallas_call(train_kernel, out_shape=(jax.ShapeDtypeStruct((T, D), BF),...  129 us
    pallas_call x1, Pallas kernels, last_call(): pl.pallas_call(last_kernel, grid=(4,), out_shape=(jax.ShapeDtypeStruct((T...  4.44 us

profile of v4, /device:TPU:32, one launch (start us, length us, event | category | flops | bytes accessed | tf_op | source)
XLA Modules:
  0.0 133.6 jit_solution(9575081229512301326)
XLA Ops:
  0.6 128.5 %train.1 = (bf16[256,1024]{1,0:T(8,128)(2,1)}, bf16[16,16,640]{2,1,0:T(8,128)(2,1)}, bf16[4,4,32,1024]{3,2,1,0:T(8,128)(2,1)}) custom-call(s32[1,16]{1,0:T(1,128)} %len_s.1, s32[1,16]{1,0:T(1,128)} %dst_s.1, s32[1,256]{1,0:T(1,128)} %bitcast.5, s32[3,256]{1,0:T(4,128)} %bitcast.4, bf16[256,1024]{1,0:T(8,128)(2,1)} %ev_h.1, bf16[1024,2048]{1,0:T(8,128)(2,1)} %win_h.1, ...), custom_call_target="tpu_custom_call" | custom-call | tf_op jit(solution)/shard_map/train/pallas_call | solution.py:667
  129.2 4.4 %last.1 = (bf16[256,1024]{1,0:T(8,128)(2,1)}, f32[64,2048]{1,0:T(8,128)}, f32[64,512]{1,0:T(8,128)}, f32[512,1024]{1,0:T(8,128)}) custom-call(bf16[256,1024]{1,0:T(8,128)(2,1)} %get-tuple-element.7.lay, bf16[4,4,16,640]{3,2,1,0:T(8,128)(2,1)} %bitcast.3, bf16[4,4,32,1024]{3,2,1,0:T(8,128)(2,1)} %get-tuple-element.9.h, bf16[512,1024]{1,0:T(8,128)(2,1)} %e.1), custom_call_target="tpu_custom_call" | custom-call | tf_op jit(solution)/shard_map/last/pallas_call | solution.py:692

commit v5 on v4

--- a/solution.py
+++ b/solution.py
@@ -116,6 +116,23 @@
             self.out(k)[...] = total.astype(BF)
 
 
+class Swap:
+    def __init__(self, net, off, i, src, buf, out):
+        self.net, self.off, self.i, self.src, self.buf, self.out = net, off, i, src, buf, out
+
+    def start(self):
+        buf = self.buf
+        self.got = self.net.bundle(
+            buf.at[pl.ds(1, 3)], *[(self.src((self.i + k) % 4), buf.at[k], self.off(k)) for k in (2, 1, 3)])
+
+    def finish(self):
+        self.got.wait_recv()
+        total = self.src(self.i)[...].astype(F32)
+        for k in range(1, 4):
+            total = total + self.buf[k].astype(F32)
+        self.out[...] = total.astype(BF)
+
+
 def call_out(devices):
     barrier = pltpu.get_barrier_semaphore()
     for dev in devices:
@@ -123,7 +140,7 @@
     return lambda: pl.semaphore_wait(barrier, len(devices))
 
 
-NSEM = 88
+NSEM = 84
 
 
 def train_kernel(len_s, dst_s, hist_v, neg_v, ev_h, win_h, wout_h, tab_h, lay_o, w_o, h_o, *refs):
@@ -131,9 +148,10 @@
      res, rlen, yall, ymate, ids_f, cand, rall, gall, gsend, lacc, lsum, lrec, gcol, picks, found,
      wown, wsend, wrec, upb, gg, gatt, gpre, gprem, ninT, ninTm, upT, upTm, hsend, hrec, mask_v, lout,
      g_v, h_v, a1, b1, ha1, hb1, piece, zbuf, wpiece, wall, hall, slots_s, slots_r, csend, cbuf,
-     lsem, ssem, rsem) = refs[:len(refs) - 32]
-    bufs = refs[len(refs) - 32:]
-    (ga_b, gb_b, ha_b, hb_b, ga2_b, gb2_b, ha2_b, hb2_b) = [bufs[4 * i:4 * i + 4] for i in range(8)]
+     lsem, ssem, rsem) = refs[:len(refs) - 20]
+    bufs = refs[len(refs) - 20:]
+    (ga_b, gb_b, ha_b, hb_b) = [bufs[4 * i:4 * i + 4] for i in range(4)]
+    ga2_b, gb2_b, ha2_b, hb2_b = bufs[16:]
     w = Where()
     net = Links(ssem, rsem)
     s, z, c, px, py, g = w.s, w.z, w.c, w.px, w.py, w.g
@@ -168,22 +186,19 @@
     everyone()
     low, high = pl.ds(0, 512), pl.ds(512, 512)
     mine_at = lambda dz, cols: tab.at[dz, px, py, :, cols]
-    slice_in = {(1, 7): net.bundle(
-        tab.at[0, 0, pl.ds(0, 2), :, high],
-        *[(mine_at(0, high), mine_at(8 - k, high), w.zoff(k)) for k in (1, 7)])}
-    for a, b in ((2, 6), (3, 5)):
+    slice_in = {}
+    for a, b in ((1, 7), (2, 6), (3, 5)):
         slice_in[a, b] = net.bundle(
             tab.at[0, 0, pl.ds(0, 2)],
             *[(tab.at[0, px, py], tab.at[8 - k, px, py], w.zoff(k)) for k in (a, b)])
     rep(15, lambda i: norm_rows(i + 1))
     cp_cand = net.go(cand.at[pl.ds(0, T)], cand.at[pl.ds(T, T)], w.mate())
 
-    pieces = {7: (tab.at[7], 512, 512, "y"), 1: (tab.at[1], 512, 512, "x"),
+    pieces = {7: (tab.at[7], 0, 1024, "y"), 1: (tab.at[1], 0, 1024, "x"),
               6: (tab.at[6], 0, 1024, "y"), 2: (tab.at[2], 0, 1024, "x"),
               5: (tab.at[5], 0, 1024, "y"), 3: (tab.at[3], 0, 1024, "x"),
-              "4x": (tab.at[4], 0, 512, "x"), "4y": (tab.at[4], 512, 512, "y"),
-              "hx": (hall, 0, 512, "x"), "hy": (hall, 512, 512, "y")}
-    flying = {}
+              "4x": (tab.at[4], 0, 512, "x"), "4y": (tab.at[4], 512, 512, "y")}
+    flying, early = {}, {}
 
     def one(piece, kx, ky, c0, nc):
         return piece[0].at[(px + kx) % 4, (py + ky) % 4, :, pl.ds(c0, nc)]
@@ -199,7 +214,10 @@
     def first_send(name):
         p = pieces[name]
         own = one(p, 0, 0, p[1], p[2])
-        pair(name, p[0].at[0, pl.ds(0, 2), :, pl.ds(p[1], p[2])], own, own, w.xoff if p[3] == "x" else w.yoff)
+        whole = p[0].at[0, pl.ds(0, 2), :, pl.ds(p[1], p[2])]
+        across = w.yoff if p[3] == "x" else w.xoff
+        pair(name, whole, own, own, w.xoff if p[3] == "x" else w.yoff)
+        early[name] = net.bundle(whole, (own, own, across(1)), (own, own, across(-1)))
 
     def first_forward(name):
         p = pieces[name]
@@ -211,12 +229,16 @@
     def second_send(name):
         p = pieces[name]
         flying[name].wait_recv()
-        own = many(p, 0, p[1], p[2])
-        pair(name, p[0].at[pl.ds(0, 2), :, :, pl.ds(p[1], p[2])], own, own, w.yoff if p[3] == "x" else w.xoff)
+        across = w.yoff if p[3] == "x" else w.xoff
+        others = [one(p, k, 0, p[1], p[2]) if p[3] == "x" else one(p, 0, k, p[1], p[2]) for k in (1, 3, 2)]
+        flying[name] = net.bundle(
+            p[0].at[pl.ds(0, 2), pl.ds(0, 3), :, pl.ds(p[1], p[2])],
+            *[(ref, ref, across(d)) for ref in others for d in (1, -1)])
 
     def second_forward(name):
         p = pieces[name]
         half = p[2] // 2
+        early[name].wait_recv()
         flying[name].wait_recv()
         pair(name, many(p, 0, p[1], p[2]), many(p, -1, p[1], half), many(p, 1, p[1] + half, half),
              w.yoff if p[3] == "x" else w.xoff)
@@ -283,9 +305,6 @@
     slices(3, 5)
     slice_in["4r", "4l"] = net.bundle(
         tab.at[0, 0, 0], (mine_at(5, low), mine_at(4, low), w.zoff(1)), (mine_at(3, high), mine_at(4, high), w.zoff(-1)))
-    direct = net.bundle(
-        tab.at[pl.ds(0, 2), :, :, :, low], (tab.at[0, :, :, :, low], tab.at[7, :, :, :, low], w.zoff(1)),
-        (tab.at[0, :, :, :, low], tab.at[1, :, :, :, low], w.zoff(-1)))
     step(first_send, 3, 5)
     step(first_forward, 2, 6)
     rep(2, lambda h: attend(h + 2))
@@ -323,6 +342,34 @@
     two_y = yall.at[pl.ds(0, 2)]
     hop = net.bundle(two_y, (yall.at[0], yall.at[7], w.zoff(1)), (yall.at[0], yall.at[1], w.zoff(-1)))
     cp_rows = net.bundle(rall.at[pl.ds(0, 7)], *[(rall.at[0], rall.at[8 - k], w.zoff(k)) for k in range(1, 8)])
+    lane8 = iota((8, 128), 1)
+    counts = jnp.zeros((8, 128), F32)
+    place = jnp.zeros((8, T), I32)
+    start = 0
+    for j in range(16):
+        n, d = len_s[0, j], dst_s[0, j]
+        counts = counts + jnp.where(lane8 == d, n, 0).astype(F32)
+        place = jnp.where((tr >= start) & (tr < start + n), d * 32 + tr - start, place)
+        start = start + n
+    csend[...] = counts
+    cbuf[s] = csend[...]
+
+    def fill(i):
+        pick = jnp.where(iota((128, T), 0) + i * 128 == place[:1, :], 1.0, 0.0).astype(BF)
+        slots_s[pl.ds(i * 4, 4)] = mm(pick, lout[...]).astype(BF).reshape(4, 32, D)
+
+    used = pl.ds(0, 24)
+    rep(4, fill)
+    slots_r[s, used] = slots_s[s, used]
+    cp_count = net.bundle(cbuf.at[pl.ds(0, 15)], *[(csend, cbuf.at[s], w.at(seq=(s + k) % 16)) for k in range(1, 16)])
+
+    def slots(*ks):
+        return net.bundle(
+            slots_r.at[pl.ds(0, len(ks)), used],
+            *[(slots_s.at[(s + k) % 16, used], slots_r.at[s, used], w.at(seq=(s + k) % 16)) for k in ks])
+
+    cp_slot = [slots(8, 1, 15, 2, 14)]
+
     step(first_forward, "4x", "4y")
     rep(8, flip_in)
     step(second_forward, 1, 7)
@@ -373,7 +420,6 @@
     score(0)
     step(second_send, "4x", "4y")
     aim(1)
-    direct.wait_recv()
     settle(1, 7)
     step(second_forward, 2, 6)
     score(1)
@@ -391,6 +437,8 @@
     aim(3)
     settle(3, 5)
     score(3)
+    hop.wait_recv()
+    hop = net.bundle(two_y, (yall.at[6], yall.at[5], w.zoff(1)), (yall.at[2], yall.at[3], w.zoff(-1)))
     aim(5)
     score(5)
     aim(4)
@@ -398,8 +446,6 @@
     score(4)
     lane = iota((2 * T, 128), 1)
     cp_l = net.go(lsum, lrec, w.mate())
-    hop.wait_recv()
-    hop = net.bundle(two_y, (yall.at[6], yall.at[5], w.zoff(1)), (yall.at[2], yall.at[3], w.zoff(-1)))
     cp_l.wait_recv()
     lrec_v = lrec[...]
     logits = (lsum[...] + jnp.concatenate([lrec_v[T:], lrec_v[:T]], 0)) / TEMP
@@ -472,10 +518,6 @@
 
     rep(4, back_attend)
     cp_pre = net.go(gpre, gprem, w.mate())
-    hop.wait_recv()
-    a, b = pl.ds(0, 512), pl.ds(512, 512)
-    hop = net.bundle(yall.at[0], (yall.at[5, :, a], yall.at[4, :, a], w.zoff(1)),
-                     (yall.at[3, :, b], yall.at[4, :, b], w.zoff(-1)))
 
     def store_g(i, first, block):
         for b in range(block.shape[1] // 128):
@@ -494,6 +536,10 @@
     rep(2, grad_out)
     cp_nin.wait_recv()
     cp_pre.wait_recv()
+    hop.wait_recv()
+    a, b = pl.ds(0, 512), pl.ds(512, 512)
+    hop = net.bundle(yall.at[0], (yall.at[5, :, a], yall.at[4, :, a], w.zoff(1)),
+                     (yall.at[3, :, b], yall.at[4, :, b], w.zoff(-1)))
 
     def grad_in(i):
         a = ninT[pl.ds(i * 4, 4), c].reshape(T, T)
@@ -511,38 +557,13 @@
     gb = Ring(net, w.yoff, py, lambda j, k: g_v.at[:, pl.ds(4 + 2 * k, 2), j], gb_b, lambda k: b1.at[:, two(k)])
     ha = Ring(net, w.xoff, px, lambda j, k: h_v.at[j, :, :, cut(k)], ha_b, lambda k: ha1.at[:, :, cut(k)])
     hb = Ring(net, w.yoff, py, lambda j, k: h_v.at[:, j, :, hicut(k)], hb_b, lambda k: hb1.at[:, :, cut(k)])
-    ga2 = Ring(net, w.yoff, py, lambda j, k: a1.at[two(k), j], ga2_b, lambda k: piece.at[two(k)])
-    gb2 = Ring(net, w.xoff, px, lambda j, k: b1.at[j, two(k)], gb2_b, lambda k: piece.at[pl.ds(4 + 2 * k, 2)])
+    ga2 = Swap(net, w.yoff, py, lambda j: a1.at[:, j], ga2_b, piece.at[pl.ds(0, 4)])
+    gb2 = Swap(net, w.xoff, px, lambda j: b1.at[j], gb2_b, piece.at[pl.ds(4, 4)])
     mine = hall.at[px, py]
-    ha2 = Ring(net, w.yoff, py, lambda j, k: ha1.at[j, :, cut(k)], ha2_b, lambda k: mine.at[:, cut(k)])
-    hb2 = Ring(net, w.xoff, px, lambda j, k: hb1.at[j, :, cut(k)], hb2_b, lambda k: mine.at[:, hicut(k)])
+    ha2 = Swap(net, w.yoff, py, lambda j: ha1.at[j], ha2_b, mine.at[:, low])
+    hb2 = Swap(net, w.xoff, px, lambda j: hb1.at[j], hb2_b, mine.at[:, high])
     ga.start()
     gb.start()
-
-    lane8 = iota((8, 128), 1)
-    counts = jnp.zeros((8, 128), F32)
-    place = jnp.zeros((8, T), I32)
-    start = 0
-    for j in range(16):
-        n, d = len_s[0, j], dst_s[0, j]
-        counts = counts + jnp.where(lane8 == d, n, 0).astype(F32)
-        place = jnp.where((tr >= start) & (tr < start + n), d * 32 + tr - start, place)
-        start = start + n
-    csend[...] = counts
-    cp_count = net.bundle(cbuf.at[pl.ds(0, 15)], *[(csend, cbuf.at[s], w.at(seq=(s + k) % 16)) for k in range(1, 16)])
-    cbuf[s] = csend[...]
-
-    def fill(i):
-        pick = jnp.where(iota((128, T), 0) + i * 128 == place[:1, :], 1.0, 0.0).astype(BF)
-        slots_s[pl.ds(i * 4, 4)] = mm(pick, lout[...]).astype(BF).reshape(4, 32, D)
-
-    rep(4, fill)
-    used = pl.ds(0, 24)
-    cp_slot = net.bundle(
-        slots_r.at[pl.ds(0, 15), used],
-        *[(slots_s.at[(s + k) % 16, used], slots_r.at[s, used], w.at(seq=(s + k) % 16)) for k in range(1, 16)])
-    slots_r[s, used] = slots_s[s, used]
-
     cp_rows.wait_recv()
     cp_g.wait_recv()
 
@@ -566,10 +587,15 @@
         hsend[:, ds(i, 256)] = h_part(1 - c, i).astype(BF)
 
     hop.wait_recv()
+    cp_slot.append(slots(7, 9, 6, 10, 5, 11, 4, 12, 3, 13))
+    ga.relay()
+    gb.relay()
     rep(4, h_mate)
     cp_h = net.go(hsend, hrec, w.mate())
-    ga.relay()
-    gb.relay()
+    ga.finish()
+    ga2.start()
+    gb.finish()
+    gb2.start()
 
     def h_own(i):
         part = h_part(c, i)
@@ -585,27 +611,15 @@
     ha.start()
     hb.start()
 
-    ga.finish()
-    ga2.start()
-    gb.finish()
-    gb2.start()
+    ga2.finish()
+    gb2.finish()
+    cp_z = net.bundle(zbuf.at[pl.ds(0, 7)], *[(piece.at[(z + k) % 8], zbuf.at[k], w.zoff(k)) for k in range(1, 8)])
     ha.relay()
     hb.relay()
-    ga2.relay()
-    gb2.relay()
     ha.finish()
     ha2.start()
     hb.finish()
     hb2.start()
-    ga2.finish()
-    gb2.finish()
-    cp_z = net.bundle(zbuf.at[pl.ds(0, 7)], *[(piece.at[(z + k) % 8], zbuf.at[k], w.zoff(k)) for k in range(1, 8)])
-    ha2.relay()
-    hb2.relay()
-    ha2.finish()
-    first_send("hx")
-    hb2.finish()
-    first_send("hy")
     total = piece[z].astype(F32)
     cp_z.wait_recv()
     for k in range(1, 8):
@@ -613,11 +627,19 @@
     wpiece[...] = total.astype(BF)
     cp_sum = net.bundle(wall.at[pl.ds(0, 15)], *[(wpiece, wall.at[g], peer(i, j)) for i, j in plane])
     wall[g] = wpiece[...]
-    step(first_forward, "hx", "hy")
-    step(second_send, "hx", "hy")
+    ha2.finish()
+    spread_x = net.bundle(hall.at[0, pl.ds(0, 3), :, low], *[(mine.at[:, low], mine.at[:, low], w.xoff(k)) for k in (2, 1, 3)])
+    hb2.finish()
+    spread_y = net.bundle(hall.at[0, pl.ds(0, 3), :, high], *[(mine.at[:, high], mine.at[:, high], w.yoff(k)) for k in (2, 1, 3)])
+    line_x, line_y = hall.at[:, py, :, low], hall.at[px, :, :, high]
+    spread_x.wait_recv()
+    cover_x = net.bundle(hall.at[pl.ds(0, 3), :, :, low], *[(line_x, line_x, w.yoff(k)) for k in (2, 1, 3)])
+    spread_y.wait_recv()
+    cover_y = net.bundle(hall.at[pl.ds(0, 3), :, :, high], *[(line_y, line_y, w.xoff(k)) for k in (2, 1, 3)])
 
     cp_count.wait_recv()
-    cp_slot.wait_recv()
+    for copy in cp_slot:
+        copy.wait_recv()
     cnt = jnp.sum(jnp.where(iota((16, 128), 1) == s, cbuf[:, 0, :], 0.0), -1, keepdims=True)
     row, col16 = iota((16, 512), 0), iota((16, 512), 1)
     slot = col16 >> 5
@@ -631,10 +653,10 @@
         lay_o[:, ds(i, 256)] = mm(chosen, slots_r[:, :, ds(i, 256)].reshape(512, 256)).astype(BF)
 
     rep(4, land)
-    step(second_forward, "hx", "hy")
     cp_sum.wait_recv()
     w_o[...] = wall[...]
-    settle("hx", "hy")
+    cover_x.wait_recv()
+    cover_y.wait_recv()
     h_o[...] = hall[...]
     assert net.n == NSEM, net.n
     net.drain()
@@ -643,7 +665,8 @@
 def train_call(lengths, destinations, hist, neg, events, in_weight, out_weight, item_table):
     vm = lambda *shape, dtype=BF: pltpu.VMEM(shape, dtype)
     f32 = dict(dtype=F32)
-    halves = [(2, 4, 16, 640), (4, 2, 16, 640), (4, 32, 256), (4, 32, 256), (2, 16, 640), (2, 16, 640), (32, 256), (32, 256)]
+    halves = [(2, 4, 16, 640), (4, 2, 16, 640), (4, 32, 256), (4, 32, 256)]
+    wholes = [(4, 16, 640), (4, 16, 640), (32, 512), (32, 512)]
     sem = pltpu.SemaphoreType.DMA
     scratch = [
         vm(T, D), vm(D, 4 * HID), vm(D, HID), vm(512, D), vm(8, 4, 4, 32, D), vm(T, D),
@@ -660,7 +683,7 @@
         vm(16, 640), vm(16, 16, 640), vm(4, 4, 32, D), vm(16, 32, D), vm(16, 32, D),
         vm(8, 128, **f32), vm(16, 8, 128, **f32),
         sem((4,)), sem((NSEM,)), sem((NSEM,)),
-    ] + [vm(2, *shape) for shape in halves for _ in range(4)]
+    ] + [vm(2, *shape) for shape in halves for _ in range(4)] + [vm(4, *shape) for shape in wholes]
     any_ = pl.BlockSpec(memory_space=pl.ANY)
     vmem = pl.BlockSpec(memory_space=pltpu.VMEM)
     smem = pl.BlockSpec(memory_space=pltpu.SMEM)

time: 134 us -> 126 us (0.940); the launches traced: 134 us -> 124 us
  Pallas kernels: 133 us -> 123 us
    pallas_call x1, Pallas kernels: 129 us -> 119 us  [train_call(): pl.pallas_call(train_kernel, out_shape=(jax.ShapeDtypeStruct((T, D), BF),...]
where the time goes in v5:
time: 126 us; the launch traced here: 124 us
  Pallas kernels  123 us (98%)
    pallas_call x1, Pallas kernels, train_call(): pl.pallas_call(train_kernel, out_shape=(jax.ShapeDtypeStruct((T, D), BF),...  119 us
    pallas_call x1, Pallas kernels, last_call(): pl.pallas_call(last_kernel, grid=(4,), out_shape=(jax.ShapeDtypeStruct((T...  4.44 us

profile of v5, /device:TPU:32, one launch (start us, length us, event | category | flops | bytes accessed | tf_op | source)
XLA Modules:
  0.0 124.1 jit_solution(6063454421983021479)
XLA Ops:
  0.6 119.0 %train.1 = (bf16[256,1024]{1,0:T(8,128)(2,1)}, bf16[16,16,640]{2,1,0:T(8,128)(2,1)}, bf16[4,4,32,1024]{3,2,1,0:T(8,128)(2,1)}) custom-call(s32[1,16]{1,0:T(1,128)} %len_s.1, s32[1,16]{1,0:T(1,128)} %dst_s.1, s32[1,256]{1,0:T(1,128)} %bitcast.5, s32[3,256]{1,0:T(4,128)} %bitcast.4, bf16[256,1024]{1,0:T(8,128)(2,1)} %ev_h.1, bf16[1024,2048]{1,0:T(8,128)(2,1)} %win_h.1, ...), custom_call_target="tpu_custom_call" | custom-call | tf_op jit(solution)/shard_map/train/pallas_call | solution.py:690
  119.7 4.4 %last.1 = (bf16[256,1024]{1,0:T(8,128)(2,1)}, f32[64,2048]{1,0:T(8,128)}, f32[64,512]{1,0:T(8,128)}, f32[512,1024]{1,0:T(8,128)}) custom-call(bf16[256,1024]{1,0:T(8,128)(2,1)} %get-tuple-element.7.lay, bf16[4,4,16,640]{3,2,1,0:T(8,128)(2,1)} %bitcast.3, bf16[4,4,32,1024]{3,2,1,0:T(8,128)(2,1)} %get-tuple-element.9.h, bf16[512,1024]{1,0:T(8,128)(2,1)} %e.1), custom_call_target="tpu_custom_call" | custom-call | tf_op jit(solution)/shard_map/last/pallas_call | solution.py:715

commit v6 on v5

--- a/solution.py
+++ b/solution.py
@@ -140,14 +140,14 @@
     return lambda: pl.semaphore_wait(barrier, len(devices))
 
 
-NSEM = 84
+NSEM = 93
 
 
 def train_kernel(len_s, dst_s, hist_v, neg_v, ev_h, win_h, wout_h, tab_h, lay_o, w_o, h_o, *refs):
     (x_v, win, wout, traw, tab, nin, slope, proj, attn, dsl, att, normed, inv, gated, gatedm,
-     res, rlen, yall, ymate, ids_f, cand, rall, gall, gsend, lacc, lsum, lrec, gcol, picks, found,
+     res, rlen, yall, ymate, ids_f, cand, rall, gall, gsend, lacc, lsum, lsend, lrec, gcol, picks, found,
      wown, wsend, wrec, upb, gg, gatt, gpre, gprem, ninT, ninTm, upT, upTm, hsend, hrec, mask_v, lout,
-     g_v, h_v, a1, b1, ha1, hb1, piece, zbuf, wpiece, wall, hall, slots_s, slots_r, csend, cbuf,
+     g_v, h_v, a1, b1, ha1, hb1, piece, zbuf, wpiece, hpiece, wall, hall, slots_s, slots_r, csend, cbuf,
      lsem, ssem, rsem) = refs[:len(refs) - 20]
     bufs = refs[len(refs) - 20:]
     (ga_b, gb_b, ha_b, hb_b) = [bufs[4 * i:4 * i + 4] for i in range(4)]
@@ -437,26 +437,29 @@
     aim(3)
     settle(3, 5)
     score(3)
-    hop.wait_recv()
-    hop = net.bundle(two_y, (yall.at[6], yall.at[5], w.zoff(1)), (yall.at[2], yall.at[3], w.zoff(-1)))
     aim(5)
     score(5)
     aim(4)
     settle("4x", "4y")
     score(4)
-    lane = iota((2 * T, 128), 1)
-    cp_l = net.go(lsum, lrec, w.mate())
+    lsend[...] = lsum[...].T[:8]
+    cp_l = net.go(lsend, lrec, w.mate())
     cp_l.wait_recv()
-    lrec_v = lrec[...]
-    logits = (lsum[...] + jnp.concatenate([lrec_v[T:], lrec_v[:T]], 0)) / TEMP
-    live = lane < NCAND
+    other = lrec[...]
+    logits = (lsend[...] + jnp.concatenate([other[:, T:], other[:, :T]], 1)) / TEMP
+    cand_no = iota((8, 2 * T), 0)
+    live = cand_no < NCAND
     ex = jnp.where(live, jnp.exp(jnp.where(live, logits, 0.0)), 0.0)
-    soft = ex / jnp.sum(ex, -1, keepdims=True)
-    gcol[...] = jnp.where(live, soft - (lane == 0).astype(F32), 0.0) / TEMP
-
-    gsend[...] = gcol[pl.ds(0, T)].T[:8]
-    gall[0] = gsend[...]
+    soft = ex / jnp.sum(ex, 0, keepdims=True)
+    coef = jnp.where(live, soft - (cand_no == 0).astype(F32), 0.0) / TEMP
+    gsend[...] = coef[:, :T]
+    gall[0] = coef[:, :T]
+    gcol[...] = jnp.concatenate([coef, jnp.zeros((120, 2 * T), F32)], 0).T
+
     cp_g = net.bundle(gall.at[pl.ds(0, 7)], *[(gsend, gall.at[8 - k], w.zoff(k)) for k in range(1, 8)])
+
+    hop.wait_recv()
+    hop = net.bundle(two_y, (yall.at[6], yall.at[5], w.zoff(1)), (yall.at[2], yall.at[3], w.zoff(-1)))
 
     def blend(at):
         who, how = cand[at] >> 9, gcol[at]
@@ -502,6 +505,7 @@
         block = upb[:, ds(i, 128)].astype(F32).T
         upT[i] = block.astype(BF).reshape(2, 64, T)
 
+    cp_pre = net.go(gpre.at[:, pl.ds(0, HID)], gprem.at[:, pl.ds(0, HID)], w.mate())
     rep(8, flip_up)
     cp_up = net.go(upT.at[:, 1 - c], upTm, w.mate())
 
@@ -517,51 +521,64 @@
         gpre[:, col(3)] = (gk * slope[:, col(3)]).astype(BF)
 
     rep(4, back_attend)
-    cp_pre = net.go(gpre, gprem, w.mate())
+    rest = pl.ds(HID, 3 * HID)
+    cp_rest = net.go(gpre.at[:, rest], gprem.at[:, rest], w.mate())
 
     def store_g(i, first, block):
         for b in range(block.shape[1] // 128):
             n = first + b
-            g_v[n // 5, pl.ds(i * 4, 4), :, :, pl.ds((n % 5) * 128, 128)] = (
+            if n < 4:
+                group, at = n // 2, n % 2
+            elif n < 16:
+                group, at = (n - 4) // 3, 2 + (n - 4) % 3
+            else:
+                group, at = 2 + (n - 16) // 2, n % 2
+            g_v[group, pl.ds(i * 4, 4), :, :, pl.ds(at * 128, 128)] = (
                 block[:, b * 128:(b + 1) * 128].astype(BF).reshape(4, 4, 16, 128))
-
-    cp_gated.wait_recv()
-    cp_up.wait_recv()
-
-    def grad_out(i):
-        a = upT[pl.ds(i * 4, 4), c].reshape(T, T)
-        b = upTm[pl.ds(i * 4, 4)].reshape(T, T)
-        store_g(i, 16, mm(a, gated[...]) + mm(b, gatedm[...]))
-
-    rep(2, grad_out)
-    cp_nin.wait_recv()
-    cp_pre.wait_recv()
-    hop.wait_recv()
-    a, b = pl.ds(0, 512), pl.ds(512, 512)
-    hop = net.bundle(yall.at[0], (yall.at[5, :, a], yall.at[4, :, a], w.zoff(1)),
-                     (yall.at[3, :, b], yall.at[4, :, b], w.zoff(-1)))
-
-    def grad_in(i):
-        a = ninT[pl.ds(i * 4, 4), c].reshape(T, T)
-        b = ninTm[pl.ds(i * 4, 4)].reshape(T, T)
-        for n in range(4):
-            cols = pl.ds(n * 512, 512)
-            store_g(i, n * 4, mm(a, gpre[:, cols]) + mm(b, gprem[:, cols]))
-
-    rep(2, grad_in)
 
     two = lambda k: pl.ds(2 * k, 2)
     cut = lambda k: pl.ds(256 * k, 256)
     hicut = lambda k: pl.ds(512 + 256 * k, 256)
-    ga = Ring(net, w.xoff, px, lambda j, k: g_v.at[j, two(k)], ga_b, lambda k: a1.at[two(k)])
-    gb = Ring(net, w.yoff, py, lambda j, k: g_v.at[:, pl.ds(4 + 2 * k, 2), j], gb_b, lambda k: b1.at[:, two(k)])
+
+    def g_rings(cols):
+        cut = lambda bufs: [buf.at[:, :, :, :, cols] for buf in bufs]
+        return (
+            Ring(net, w.xoff, px, lambda j, k: g_v.at[j, two(k), :, :, cols], cut(ga_b),
+                 lambda k: a1.at[two(k), :, :, cols]),
+            Ring(net, w.yoff, py, lambda j, k: g_v.at[:, pl.ds(4 + 2 * k, 2), j, :, cols], cut(gb_b),
+                 lambda k: b1.at[:, two(k), :, cols]))
+
+    ga, gb = g_rings(pl.ds(0, 256))
+    gc, gd = g_rings(pl.ds(256, 384))
     ha = Ring(net, w.xoff, px, lambda j, k: h_v.at[j, :, :, cut(k)], ha_b, lambda k: ha1.at[:, :, cut(k)])
     hb = Ring(net, w.yoff, py, lambda j, k: h_v.at[:, j, :, hicut(k)], hb_b, lambda k: hb1.at[:, :, cut(k)])
     ga2 = Swap(net, w.yoff, py, lambda j: a1.at[:, j], ga2_b, piece.at[pl.ds(0, 4)])
     gb2 = Swap(net, w.xoff, px, lambda j: b1.at[j], gb2_b, piece.at[pl.ds(4, 4)])
     mine = hall.at[px, py]
-    ha2 = Swap(net, w.yoff, py, lambda j: ha1.at[j], ha2_b, mine.at[:, low])
-    hb2 = Swap(net, w.xoff, px, lambda j: hb1.at[j], hb2_b, mine.at[:, high])
+    ha2 = Swap(net, w.yoff, py, lambda j: ha1.at[j], ha2_b, hpiece.at[:, low])
+    hb2 = Swap(net, w.xoff, px, lambda j: hb1.at[j], hb2_b, hpiece.at[:, high])
+    cp_gated.wait_recv()
+    cp_up.wait_recv()
+    cp_nin.wait_recv()
+    cp_pre.wait_recv()
+
+    def grad_out(i):
+        a = upT[pl.ds(i * 4, 4), c].reshape(T, T)
+        b = upTm[pl.ds(i * 4, 4)].reshape(T, T)
+        store_g(i, 16, mm(a, gated[...]) + mm(b, gatedm[...]))
+
+    def grad_in(i, blocks):
+        a = ninT[pl.ds(i * 4, 4), c].reshape(T, T)
+        b = ninTm[pl.ds(i * 4, 4)].reshape(T, T)
+        for n in blocks:
+            cols = pl.ds(n * 512, 512)
+            store_g(i, n * 4, mm(a, gpre[:, cols]) + mm(b, gprem[:, cols]))
+
+    def grad_first(i):
+        grad_out(i)
+        grad_in(i, (0,))
+
+    rep(2, grad_first)
     ga.start()
     gb.start()
     cp_rows.wait_recv()
@@ -579,29 +596,50 @@
 
     rep(8, spread_t)
 
-    def h_part(o, i):
-        y = [yall[pl.ds(4 * k, 4), :, ds(i, 256)].reshape(4 * T, 256) for k in range(2)]
-        return mm(found[2 * o], y[0]) + mm(found[2 * o + 1], y[1])
+    cp_rest.wait_recv()
+    rep(2, lambda i: grad_in(i, (1, 2, 3)))
+    gc.start()
+    gd.start()
+
+    def h_part(o, k, i):
+        total = jnp.zeros((2 * T, 256), F32)
+        for plane_no, first, n in ((0, 0, 3), (1, 2, 2)) if k == 0 else ((0, 3, 1), (1, 0, 2)):
+            y = yall[pl.ds(plane_no * 4 + first, n), :, ds(i, 256)].reshape(n * T, 256)
+            total = total + mm(found[2 * o + plane_no, :, pl.ds(first * T, n * T)], y)
+        return total
+
+    def h_first(i):
+        part = h_part(1 - c, 0, i)
+        slope[:, ds(i, 256)] = part[:T]
+        slope[:, ds(i + 4, 256)] = part[T:]
+        part = h_part(c, 0, i)
+        wown[:, ds(i, 256)] = part[:T]
+        res[:, ds(i, 256)] = part[T:]
 
     def h_mate(i):
-        hsend[:, ds(i, 256)] = h_part(1 - c, i).astype(BF)
-
+        part = h_part(1 - c, 1, i)
+        hsend[pl.ds(0, T), ds(i, 256)] = (part[:T] + slope[:, ds(i, 256)]).astype(BF)
+        hsend[pl.ds(T, T), ds(i, 256)] = (part[T:] + slope[:, ds(i + 4, 256)]).astype(BF)
+
+    def h_own(i):
+        part = h_part(c, 1, i)
+        wown[:, ds(i, 256)] += part[:T]
+        res[:, ds(i, 256)] += part[T:]
+
+    rep(4, h_first)
     hop.wait_recv()
-    cp_slot.append(slots(7, 9, 6, 10, 5, 11, 4, 12, 3, 13))
-    ga.relay()
-    gb.relay()
+    a, b = pl.ds(0, 512), pl.ds(512, 512)
+    hop = net.bundle(yall.at[0], (yall.at[5, :, a], yall.at[4, :, a], w.zoff(1)),
+                     (yall.at[3, :, b], yall.at[4, :, b], w.zoff(-1)))
+    for ring in (ga, gb, gc, gd):
+        ring.relay()
+    for ring in (ga, gb, gc, gd):
+        ring.finish()
+    ga2.start()
+    gb2.start()
+    hop.wait_recv()
     rep(4, h_mate)
     cp_h = net.go(hsend, hrec, w.mate())
-    ga.finish()
-    ga2.start()
-    gb.finish()
-    gb2.start()
-
-    def h_own(i):
-        part = h_part(c, i)
-        wown[:, ds(i, 256)] = part[:T]
-        res[:, ds(i, 256)] = part[T:]
-
     rep(4, h_own)
     cp_h.wait_recv()
     for part, src in ((0, wown), (1, res)):
@@ -610,32 +648,42 @@
             h_v[part * 2 + i // 4, i % 4] = total.astype(BF)
     ha.start()
     hb.start()
-
     ga2.finish()
     gb2.finish()
     cp_z = net.bundle(zbuf.at[pl.ds(0, 7)], *[(piece.at[(z + k) % 8], zbuf.at[k], w.zoff(k)) for k in range(1, 8)])
     ha.relay()
     hb.relay()
+    total = piece[z].astype(F32)
+    cp_z.wait_recv()
+    cp_slot.append(slots(7, 9, 6, 10, 5, 11, 4, 12, 3, 13))
+    for k in range(1, 8):
+        total = total + zbuf[k].astype(F32)
+    wpiece[...] = total.astype(BF)
     ha.finish()
     ha2.start()
     hb.finish()
     hb2.start()
-    total = piece[z].astype(F32)
-    cp_z.wait_recv()
-    for k in range(1, 8):
-        total = total + zbuf[k].astype(F32)
-    wpiece[...] = total.astype(BF)
     cp_sum = net.bundle(wall.at[pl.ds(0, 15)], *[(wpiece, wall.at[g], peer(i, j)) for i, j in plane])
     wall[g] = wpiece[...]
     ha2.finish()
-    spread_x = net.bundle(hall.at[0, pl.ds(0, 3), :, low], *[(mine.at[:, low], mine.at[:, low], w.xoff(k)) for k in (2, 1, 3)])
     hb2.finish()
-    spread_y = net.bundle(hall.at[0, pl.ds(0, 3), :, high], *[(mine.at[:, high], mine.at[:, high], w.yoff(k)) for k in (2, 1, 3)])
-    line_x, line_y = hall.at[:, py, :, low], hall.at[px, :, :, high]
-    spread_x.wait_recv()
-    cover_x = net.bundle(hall.at[pl.ds(0, 3), :, :, low], *[(line_x, line_x, w.yoff(k)) for k in (2, 1, 3)])
-    spread_y.wait_recv()
-    cover_y = net.bundle(hall.at[pl.ds(0, 3), :, :, high], *[(line_y, line_y, w.xoff(k)) for k in (2, 1, 3)])
+    rows = traw[ds(g, 32)].astype(F32)
+    length = lax.rsqrt(jnp.sum(rows * rows, -1, keepdims=True) + EPS)
+    rows, total = rows * length, hpiece[...].astype(F32)
+    mine[...] = ((total - rows * jnp.sum(rows * total, -1, keepdims=True)) * length).astype(BF)
+    hops = (2, 1, 3)
+    plans = (("x", low, w.xoff, w.yoff), ("y", high, w.yoff, w.xoff))
+    spread, cross = {}, {}
+    for name, cols, along, over in plans:
+        part, whole = mine.at[:, cols], hall.at[0, pl.ds(0, 3), :, cols]
+        spread[name] = net.bundle(whole, *[(part, part, along(k)) for k in hops])
+        cross[name] = net.bundle(whole, *[(part, part, over(k)) for k in hops])
+    cover = []
+    for name, cols, along, over in plans:
+        parts = [hall.at[(px + k) % 4, py, :, cols] if name == "x" else hall.at[px, (py + k) % 4, :, cols] for k in hops]
+        spread[name].wait_recv()
+        cover.append(net.bundle(hall.at[pl.ds(0, 3), pl.ds(0, 3), :, cols],
+                                *[(part, part, over(k)) for k in hops for part in parts]))
 
     cp_count.wait_recv()
     for copy in cp_slot:
@@ -655,8 +703,8 @@
     rep(4, land)
     cp_sum.wait_recv()
     w_o[...] = wall[...]
-    cover_x.wait_recv()
-    cover_y.wait_recv()
+    for copy in cover + [cross["x"], cross["y"]]:
+        copy.wait_recv()
     h_o[...] = hall[...]
     assert net.n == NSEM, net.n
     net.drain()
@@ -674,13 +722,13 @@
         vm(T, HID, **f32), vm(T, HID, **f32), vm(T, 128, **f32), vm(T, HID), vm(T, HID),
         vm(T, D, **f32), vm(T, 128, **f32), vm(8, T, D), vm(T, D), vm(128, T, **f32), vm(2 * T, 128, dtype=I32),
         vm(8, 8, T, dtype=I32), vm(8, 8, T, **f32), vm(8, T, **f32), vm(2 * T, 128, **f32),
-        vm(2 * T, 128, **f32), vm(2 * T, 128, **f32), vm(2 * T, 128, **f32), vm(2 * T, 512),
+        vm(2 * T, 128, **f32), vm(8, 2 * T, **f32), vm(8, 2 * T, **f32), vm(2 * T, 128, **f32), vm(2 * T, 512),
         vm(8, 2 * T, D), vm(T, D, **f32), vm(T, D), vm(T, D), vm(T, D),
         vm(T, HID, **f32), vm(T, HID), vm(T, 4 * HID), vm(T, 4 * HID), vm(8, 2, 64, T), vm(8, 64, T),
         vm(8, 2, 64, T), vm(8, 64, T), vm(512, D), vm(512, D), vm(T, T, **f32), vm(T, D),
         vm(4, 8, 4, 16, 640), vm(4, 4, 32, D),
         vm(4, 4, 16, 640), vm(4, 4, 16, 640), vm(4, 32, 512), vm(4, 32, 512), vm(8, 16, 640), vm(8, 16, 640),
-        vm(16, 640), vm(16, 16, 640), vm(4, 4, 32, D), vm(16, 32, D), vm(16, 32, D),
+        vm(16, 640), vm(32, D), vm(16, 16, 640), vm(4, 4, 32, D), vm(16, 32, D), vm(16, 32, D),
         vm(8, 128, **f32), vm(16, 8, 128, **f32),
         sem((4,)), sem((NSEM,)), sem((NSEM,)),
     ] + [vm(2, *shape) for shape in halves for _ in range(4)] + [vm(4, *shape) for shape in wholes]
@@ -699,18 +747,15 @@
     )(lengths, destinations, hist, neg, events, in_weight, out_weight, item_table)
 
 
-def last_kernel(lay, w, h, e, lay_o, in_o, out_o, tab_o):
+def last_kernel(lay, w, h, lay_o, in_o, out_o, tab_o):
     lay_o[...] = lay[...]
-    rows = jnp.concatenate([w[i, 0] for i in range(4)], 1).astype(F32)
-    in_o[...] = rows[:, :4 * HID]
-    out_o[...] = rows[:, 4 * HID:]
-    item, total = e[...].astype(F32), h[0].reshape(128, D).astype(F32)
-    length = lax.rsqrt(jnp.sum(item * item, -1, keepdims=True) + EPS)
-    item = item * length
-    tab_o[...] = (total - item * jnp.sum(item * total, -1, keepdims=True)) * length
-
-
-def last_call(lay, w, h, item_table):
+    part = lambda i, a, b: w[i, 0][:, a:b].astype(F32)
+    in_o[...] = jnp.concatenate([part(0, 0, 256), part(1, 0, 256)] + [part(i, 256, 640) for i in range(4)], 1)
+    out_o[...] = jnp.concatenate([part(2, 0, 256), part(3, 0, 256)], 1)
+    tab_o[...] = h[0].reshape(128, D).astype(F32)
+
+
+def last_call(lay, w, h):
     rows = lambda n, m: pl.BlockSpec((n, m), lambda i: (i, 0))
     return pl.pallas_call(
         last_kernel,
@@ -718,16 +763,16 @@
         out_shape=(jax.ShapeDtypeStruct((T, D), BF), jax.ShapeDtypeStruct((64, 4 * HID), F32),
                    jax.ShapeDtypeStruct((64, HID), F32), jax.ShapeDtypeStruct((512, D), F32)),
         in_specs=[rows(64, D), pl.BlockSpec((4, 1, 16, 640), lambda i: (0, i, 0, 0)),
-                  pl.BlockSpec((1, 4, 32, D), lambda i: (i, 0, 0, 0)), rows(128, D)],
+                  pl.BlockSpec((1, 4, 32, D), lambda i: (i, 0, 0, 0))],
         out_specs=(rows(64, D), rows(16, 4 * HID), rows(16, HID), rows(128, D)),
         name="last",
-    )(lay, w, h, item_table)
+    )(lay, w, h)
 
 
 def body(events, lengths, destinations, history, negatives, in_weight, out_weight, item_table):
     result, wsum, hsum = train_call(lengths, destinations, history.reshape(1, T), negatives.T, events,
                                     in_weight, out_weight, item_table)
-    return last_call(result, wsum.reshape(4, 4, 16, 640), hsum, item_table)
+    return last_call(result, wsum.reshape(4, 4, 16, 640), hsum)
 
 
 def solution(mesh):

time: 126 us -> 121 us (0.960)
  Pallas kernels: 123 us -> 119 us
    pallas_call x1, Pallas kernels: 119 us -> 115 us  [train_call(): pl.pallas_call(train_kernel, out_shape=(jax.ShapeDtypeStruct((T, D), BF),...]
where the time goes in v6:
time: 121 us; the launch traced here: 119 us
  Pallas kernels  119 us (98%)
    pallas_call x1, Pallas kernels, train_call(): pl.pallas_call(train_kernel, out_shape=(jax.ShapeDtypeStruct((T, D), BF),...  115 us
    pallas_call x1, Pallas kernels, last_call(): pl.pallas_call(last_kernel, grid=(4,), out_shape=(jax.ShapeDtypeStruct((T...  4.02 us

profile of v6, /device:TPU:32, one launch (start us, length us, event | category | flops | bytes accessed | tf_op | source)
XLA Modules:
  0.0 119.3 jit_solution(15981801585915833227)
XLA Ops:
  0.6 114.6 %train.1 = (bf16[256,1024]{1,0:T(8,128)(2,1)}, bf16[16,16,640]{2,1,0:T(8,128)(2,1)}, bf16[4,4,32,1024]{3,2,1,0:T(8,128)(2,1)}) custom-call(s32[1,16]{1,0:T(1,128)} %len_s.1, s32[1,16]{1,0:T(1,128)} %dst_s.1, s32[1,256]{1,0:T(1,128)} %bitcast.5, s32[3,256]{1,0:T(4,128)} %bitcast.4, bf16[256,1024]{1,0:T(8,128)(2,1)} %ev_h.1, bf16[1024,2048]{1,0:T(8,128)(2,1)} %win_h.1, ...), custom_call_target="tpu_custom_call" | custom-call | tf_op jit(solution)/shard_map/train/pallas_call | solution.py:738
  115.3 4.0 %last.1 = (bf16[256,1024]{1,0:T(8,128)(2,1)}, f32[64,2048]{1,0:T(8,128)}, f32[64,512]{1,0:T(8,128)}, f32[512,1024]{1,0:T(8,128)}) custom-call(bf16[256,1024]{1,0:T(8,128)(2,1)} %get-tuple-element.7.lay, bf16[4,4,16,640]{3,2,1,0:T(8,128)(2,1)} %bitcast.3, bf16[4,4,32,1024]{3,2,1,0:T(8,128)(2,1)} %get-tuple-element.9.h), custom_call_target="tpu_custom_call" | custom-call | tf_op jit(solution)/shard_map/last/pallas_call | solution.py:760

commit v7 on v6

--- a/solution.py
+++ b/solution.py
@@ -164,8 +164,6 @@
         ((tab_h, traw), (ev_h, x_v), (win_h, win), (wout_h, wout)))]
     for copy in loads:
         copy.start()
-    for k in range(16):
-        slots_r[k, pl.ds(24, 8)] = jnp.zeros((8, D), BF)
     everyone = call_out([w.at(seq=(s + k) % 16) for k in range(1, 16)] + [peer(i, j) for i, j in plane])
 
     ids_f[...] = jnp.full((128, T), -1.0, F32)
@@ -301,13 +299,13 @@
         dsl[h] = sg * (1.0 + scores * (1.0 - sg)) * SCALE * mask
         att[:, ds(h, 128)] = mm(weight, proj[:, col(1)])
 
-    rep(2, attend)
+    rep(2, attend, 2)
     slices(3, 5)
     slice_in["4r", "4l"] = net.bundle(
         tab.at[0, 0, 0], (mine_at(5, low), mine_at(4, low), w.zoff(1)), (mine_at(3, high), mine_at(4, high), w.zoff(-1)))
     step(first_send, 3, 5)
     step(first_forward, 2, 6)
-    rep(2, lambda h: attend(h + 2))
+    rep(2, lambda h: attend(h + 2), 2)
     step(second_send, 1, 7)
 
     def norm_att(i):
@@ -360,6 +358,8 @@
 
     used = pl.ds(0, 24)
     rep(4, fill)
+    for k in range(16):
+        slots_r[k, pl.ds(24, 8)] = jnp.zeros((8, D), BF)
     slots_r[s, used] = slots_s[s, used]
     cp_count = net.bundle(cbuf.at[pl.ds(0, 15)], *[(csend, cbuf.at[s], w.at(seq=(s + k) % 16)) for k in range(1, 16)])
 
@@ -371,7 +371,7 @@
     cp_slot = [slots(8, 1, 15, 2, 14)]
 
     step(first_forward, "4x", "4y")
-    rep(8, flip_in)
+    rep(8, flip_in, 2)
     step(second_forward, 1, 7)
     step(second_send, 3, 5)
     cp_nin = net.go(ninT.at[:, 1 - c], ninTm, w.mate())
@@ -403,7 +403,7 @@
                 got = rows[first:first + T] * y.astype(F32)
                 lacc[pl.ds(first, T)] += got[:, :128] + got[:, 128:]
 
-        rep(4, part)
+        rep(4, part, 2)
 
         def close(i):
             value = jnp.sum(lacc[ds(i, 256)], -1, keepdims=True)
@@ -458,6 +458,7 @@
 
     cp_g = net.bundle(gall.at[pl.ds(0, 7)], *[(gsend, gall.at[8 - k], w.zoff(k)) for k in range(1, 8)])
 
+
     hop.wait_recv()
     hop = net.bundle(two_y, (yall.at[6], yall.at[5], w.zoff(1)), (yall.at[2], yall.at[3], w.zoff(-1)))
 
@@ -472,13 +473,13 @@
     def gather_mate(i):
         wsend[ds(i, 32)] = blend(ds(i + 8, 32)).astype(BF)
 
-    rep(8, gather_mate)
+    rep(8, gather_mate, 2)
     cp_w = net.go(wsend, wrec, w.mate())
 
     def gather_own(i):
         wown[ds(i, 32)] = blend(ds(i, 32))
 
-    rep(8, gather_own)
+    rep(8, gather_own, 2)
     cp_w.wait_recv()
 
     def upstream(i):
@@ -506,7 +507,7 @@
         upT[i] = block.astype(BF).reshape(2, 64, T)
 
     cp_pre = net.go(gpre.at[:, pl.ds(0, HID)], gprem.at[:, pl.ds(0, HID)], w.mate())
-    rep(8, flip_up)
+    rep(8, flip_up, 2)
     cp_up = net.go(upT.at[:, 1 - c], upTm, w.mate())
 
     def back_attend(h):
@@ -520,7 +521,7 @@
         gpre[:, col(2)] = (gq * slope[:, col(2)]).astype(BF)
         gpre[:, col(3)] = (gk * slope[:, col(3)]).astype(BF)
 
-    rep(4, back_attend)
+    rep(4, back_attend, 2)
     rest = pl.ds(HID, 3 * HID)
     cp_rest = net.go(gpre.at[:, rest], gprem.at[:, rest], w.mate())
 
@@ -627,11 +628,13 @@
         res[:, ds(i, 256)] += part[T:]
 
     rep(4, h_first)
+    for ring in (ga, gb):
+        ring.relay()
     hop.wait_recv()
     a, b = pl.ds(0, 512), pl.ds(512, 512)
     hop = net.bundle(yall.at[0], (yall.at[5, :, a], yall.at[4, :, a], w.zoff(1)),
                      (yall.at[3, :, b], yall.at[4, :, b], w.zoff(-1)))
-    for ring in (ga, gb, gc, gd):
+    for ring in (gc, gd):
         ring.relay()
     for ring in (ga, gb, gc, gd):
         ring.finish()
@@ -651,20 +654,18 @@
     ga2.finish()
     gb2.finish()
     cp_z = net.bundle(zbuf.at[pl.ds(0, 7)], *[(piece.at[(z + k) % 8], zbuf.at[k], w.zoff(k)) for k in range(1, 8)])
+    cp_slot.append(slots(7, 9, 6, 10, 5, 11, 4, 12, 3, 13))
     ha.relay()
     hb.relay()
-    total = piece[z].astype(F32)
-    cp_z.wait_recv()
-    cp_slot.append(slots(7, 9, 6, 10, 5, 11, 4, 12, 3, 13))
-    for k in range(1, 8):
-        total = total + zbuf[k].astype(F32)
-    wpiece[...] = total.astype(BF)
     ha.finish()
     ha2.start()
     hb.finish()
     hb2.start()
-    cp_sum = net.bundle(wall.at[pl.ds(0, 15)], *[(wpiece, wall.at[g], peer(i, j)) for i, j in plane])
-    wall[g] = wpiece[...]
+    total = piece[z].astype(F32)
+    cp_z.wait_recv()
+    for k in range(1, 8):
+        total = total + zbuf[k].astype(F32)
+    wpiece[...] = total.astype(BF)
     ha2.finish()
     hb2.finish()
     rows = traw[ds(g, 32)].astype(F32)
@@ -678,6 +679,8 @@
         part, whole = mine.at[:, cols], hall.at[0, pl.ds(0, 3), :, cols]
         spread[name] = net.bundle(whole, *[(part, part, along(k)) for k in hops])
         cross[name] = net.bundle(whole, *[(part, part, over(k)) for k in hops])
+    cp_sum = net.bundle(wall.at[pl.ds(0, 15)], *[(wpiece, wall.at[g], peer(i, j)) for i, j in plane])
+    wall[g] = wpiece[...]
     cover = []
     for name, cols, along, over in plans:
         parts = [hall.at[(px + k) % 4, py, :, cols] if name == "x" else hall.at[px, (py + k) % 4, :, cols] for k in hops]

time: 121 us -> 121 us (level)
  no operation moved by 1% of the time
where the time goes in v7:
time: 121 us; the launch traced here: 119 us
  Pallas kernels  119 us (98%)
    pallas_call x1, Pallas kernels, train_call(): pl.pallas_call(train_kernel, out_shape=(jax.ShapeDtypeStruct((T, D), BF),...  115 us
    pallas_call x1, Pallas kernels, last_call(): pl.pallas_call(last_kernel, grid=(4,), out_shape=(jax.ShapeDtypeStruct((T...  4.02 us

profile of v7, /device:TPU:32, one launch (start us, length us, event | category | flops | bytes accessed | tf_op | source)
XLA Modules:
  0.0 119.4 jit_solution(5648470076229136649)
XLA Ops:
  0.6 114.8 %train.1 = (bf16[256,1024]{1,0:T(8,128)(2,1)}, bf16[16,16,640]{2,1,0:T(8,128)(2,1)}, bf16[4,4,32,1024]{3,2,1,0:T(8,128)(2,1)}) custom-call(s32[1,16]{1,0:T(1,128)} %len_s.1, s32[1,16]{1,0:T(1,128)} %dst_s.1, s32[1,256]{1,0:T(1,128)} %bitcast.5, s32[3,256]{1,0:T(4,128)} %bitcast.4, bf16[256,1024]{1,0:T(8,128)(2,1)} %ev_h.1, bf16[1024,2048]{1,0:T(8,128)(2,1)} %win_h.1, ...), custom_call_target="tpu_custom_call" | custom-call | tf_op jit(solution)/shard_map/train/pallas_call | solution.py:741
  115.4 4.0 %last.1 = (bf16[256,1024]{1,0:T(8,128)(2,1)}, f32[64,2048]{1,0:T(8,128)}, f32[64,512]{1,0:T(8,128)}, f32[512,1024]{1,0:T(8,128)}) custom-call(bf16[256,1024]{1,0:T(8,128)(2,1)} %get-tuple-element.7.lay, bf16[4,4,16,640]{3,2,1,0:T(8,128)(2,1)} %bitcast.3, bf16[4,4,32,1024]{3,2,1,0:T(8,128)(2,1)} %get-tuple-element.9.h), custom_call_target="tpu_custom_call" | custom-call | tf_op jit(solution)/shard_map/last/pallas_call | solution.py:763
